TPU v7x, 32 devices: a whole 2x2x4 slice. The times are simulated.
32 devices in a mesh: groups: 2 (over y), ctx: 4 (over z), tp: 2 (over x), sub: 2 (over core).
Axes of the slice: x: 2, y: 2, z: 4, core: 2. Of those that a mesh axis runs over, the one named last changes fastest.
Arguments:
- x_input: bfloat16 [4096, 8192], P(('groups', 'ctx', 'sub'), 'tp'), parts along dimension 0, may hold values from -48 to 48
- gate_input: bfloat16 [4096, 8192], P(('groups', 'ctx', 'sub'), 'tp'), parts along dimension 0, may hold values from -6 to 6
- state_proj: bfloat16 [4096, 8, 2, 128], P(('groups', 'ctx', 'sub'), 'tp'), parts along dimension 0, may hold values from -2.5 to 2.5
- mix_weight: bfloat16 [4, 8192], P(None, 'tp'), may hold values from -3 to 3
- mix_bias: float32 [8192], P('tp'), may hold values from -3 to 3
- state_weight: bfloat16 [4, 8, 2, 128], P(None, 'tp'), may hold values from -3 to 3
- state_bias: float32 [8, 2, 128], P('tp'), may hold values from -2.5 to 2.5
- step_raw: float32 [4096, 128], P(('groups', 'ctx', 'sub'), 'tp'), parts along dimension 0, may hold values from -4.5 to 50
- decay_log: float32 [128], P('tp'), may hold values from -5.3 to 0.41
- skip_gain: float32 [128], P('tp'), may hold values from 0.5 to 1.5
- norm_gain: float32 [8192], P('tp'), may hold values from 0.5 to 1.5
- out_weight: bfloat16 [8192, 4096], P(('tp', 'sub')), may hold values from -0.0625 to 0.0625
- doc_lengths: int32 [16], P('groups'), parts along dimension 0, may hold values from 1 to 1024, 2048 in all
Outputs:
- output: bfloat16 [4096, 4096], P(('groups', 'ctx', 'sub'), 'tp'), parts along dimension 0
There are 2 independent parts, one for each index of `groups`. A program takes and returns all parts, laid end to end along the dimension named above; an argument that names none is the same for every part. Nothing has to cross between parts.
Inputs may be any that keep to these rules, and one draw needn't show every extreme that they name: `doc_lengths`: documents lie end to end from position 0 in the given order; the largest has exactly 1024 positions.
All inputs are finite; a program needn't handle non-finite values.
Results may differ from a plain program's by a relative error of at most 0.0095.
Values may be sent and summed in bfloat16 or wider, within the bound.
No kernel may reach another device: no remote copies, remote signals or barrier semaphores. Data moves between devices by JAX's collectives and lax.ppermute only.
A program may use at most 192 MiB of HBM per device.

v0:
```python
import functools

import jax
import jax.numpy as jnp
from jax import lax
from jax.experimental import pallas as pl
from jax.experimental.pallas import tpu as pltpu
from jax.sharding import PartitionSpec as P

HEADS = 128
GROUPS = 8
CHUNK = 128
EPSILON = 1e-05
LOG2E = 1.4426950408889634
CEILING = 126.0
VMEM = 60 << 20
F32 = jnp.float32
BF16 = jnp.bfloat16


def shifted(shard, axis, by):
    peers = lax.axis_size(axis)
    pairs = [(i, i + by) for i in range(peers) if 0 <= i + by < peers]
    return lax.ppermute(shard, axis, pairs)


def swapped(shard, axis):
    return lax.ppermute(shard, axis, [(i, i ^ 1) for i in range(lax.axis_size(axis))])


def doc_start(positions, docs_ref):
    start = jnp.zeros_like(positions)
    total = jnp.int32(0)
    for doc in range(docs_ref.shape[0]):
        start = jnp.where(positions >= total, total, start)
        total = total + docs_ref[doc]
    return start


def rows_of(count, first):
    return first + lax.broadcasted_iota(jnp.int32, (count, 1), 0)


def split2(value):
    high = value.astype(BF16)
    return high, (value - high.astype(F32)).astype(BF16)


def split3(value):
    high = value.astype(BF16)
    rest = value - high.astype(F32)
    mid = rest.astype(BF16)
    return high, mid, (rest - mid.astype(F32)).astype(BF16)


def mm(a, b):
    return jnp.dot(a, b, preferred_element_type=F32)


def contract_lanes(a, b):
    return lax.dot_general(a, b, (((1,), (1,)), ((), ())), preferred_element_type=F32)


def silu(value):
    half = 0.5 * value
    return half + half * jnp.tanh(half)


def head_lanes(copies, heads, head_width, lanes, first_lane):
    shape = (copies * heads, lanes)
    head = lax.rem(lax.broadcasted_iota(jnp.int32, shape, 0), heads)
    lane = first_lane + lax.broadcasted_iota(jnp.int32, shape, 1)
    low = head * head_width
    return jnp.where((lane >= low) & (lane < low + head_width), 1.0, 0.0).astype(BF16)


def convolved(first, docs, pieces, store, taps):
    count = pieces[0][0].shape[0]
    rims = pieces[0][1].shape[0]
    start = doc_start(rows_of(count, first), docs) - first
    row = lax.broadcasted_iota(jnp.int32, (count, count), 0)
    col = lax.broadcasted_iota(jnp.int32, (count, count), 1)
    rim_row = lax.broadcasted_iota(jnp.int32, (rims, rims), 0)
    rim_col = lax.broadcasted_iota(jnp.int32, (rims, rims), 1) - rims
    shifts = []
    for back in range(1, taps):
        hit = (col == row - back) & (col >= start)
        rim_hit = (rim_col == rim_row - back) & (rim_col >= start[:rims])
        shifts.append((jnp.where(hit, 1.0, 0.0).astype(BF16), jnp.where(rim_hit, 1.0, 0.0).astype(BF16)))
    for index, (x, rim, w, bias) in enumerate(pieces):
        span = min(256, x.shape[1])
        for low in range(0, x.shape[1], span):
            at = slice(low, low + span)
            value = x[:, at]
            weight = w[:, at].astype(F32)
            summed = bias[:, at] + value.astype(F32) * weight[taps - 1 : taps]
            top = jnp.zeros((rims, span), F32)
            for back in range(1, taps):
                line = weight[taps - 1 - back : taps - back]
                shift, rim_shift = shifts[back - 1]
                summed = summed + mm(shift, value) * line
                top = top + mm(rim_shift, rim[:, at]) * line
            store(index, at, slice(0, rims), silu(summed[:rims] + top).astype(BF16))
            store(index, at, slice(rims, count), silu(summed[rims:]).astype(BF16))


def conv_kernel(meta, docs, x, x_rim, w, bias, s, s_rim, sw, sbias, out, *, taps):
    width = x.shape[1]

    def store(index, at, rows, value):
        out[rows, slice(at.start + index * width, at.stop + index * width)] = value

    first = meta[1] + meta[0] * x.shape[0]
    convolved(first, docs, [(x, x_rim, w, bias), (s, s_rim, sw, sbias)], store, taps)


def decay_kernel(
    meta, docs, own_raw, got_raw, rate, cum_out, dlt_out, tail_out, kept_out, raw,
):
    half = own_raw.shape[1]
    heads, count = raw.shape
    mine = meta[0] == 0
    first = meta[1]
    own_at = pl.ds(pl.multiple_of(meta[0] * half, half), half)
    got_at = pl.ds(pl.multiple_of((1 - meta[0]) * half, half), half)
    last_start = doc_start(first + count - 1, docs)
    raw[:, own_at] = jnp.where(mine, own_raw[:heads], own_raw[heads:])
    raw[:, got_at] = jnp.where(mine, got_raw[:heads], got_raw[heads:])
    value = raw[...]
    size = jnp.maximum(value, 0.0) + jnp.log(1.0 + jnp.exp(-jnp.abs(value)))
    decay = (-LOG2E * jnp.exp(jnp.where(mine, rate[:heads], rate[heads:]))) * size
    row = lax.broadcasted_iota(jnp.int32, (count, count), 0)
    col = lax.broadcasted_iota(jnp.int32, (count, count), 1)
    above = jnp.where(row <= col, 1.0, 0.0).astype(BF16)
    high, mid, low = split3(decay)
    cum = mm(high, above) + (mm(mid, above) + mm(low, above))
    dlt_out[...] = cum - jnp.log2(size)
    end = cum[:, count - 1 :]
    places = first + lax.broadcasted_iota(jnp.int32, (1, count), 1)
    tail = jnp.where(places >= last_start, size * jnp.exp2(end - cum), 0.0)
    high, low = split2(tail.T)
    tail_out[:, :heads] = high
    tail_out[:, heads:] = low
    cum = cum.T
    cum_out[...] = cum
    kept = jnp.exp2(jnp.broadcast_to(cum[count - 1 :], (8, heads)))
    high, mid, low = split3(jnp.where(last_start < first, kept, 0.0))
    kept_out[:, :heads] = high
    kept_out[:, heads : 2 * heads] = mid
    kept_out[:, 2 * heads :] = low


def state_kernel(
    meta, docs, x, x_rim, w, bias, s, s_rim, sw, sbias, got, tail, kept,
    x_out, bc_out, s_out, d_out, *, taps, heads, head_width, first_lane,
):
    half, width = x.shape
    state_width = bc_out.shape[1] // 2
    own_row = pl.multiple_of(meta[0] * half, half)
    got_at = pl.ds(pl.multiple_of((1 - meta[0]) * half, half), half)

    def store(index, at, rows, value):
        place = pl.ds(pl.multiple_of(own_row + rows.start, 16), rows.stop - rows.start)
        if index:
            bc_out[place, at] = value
        else:
            x_out[place, at] = value

    convolved(meta[1] + meta[0] * half, docs, [(x, x_rim, w, bias), (s, s_rim, sw, sbias)], store, taps)
    x_out[got_at, :] = got[:, :width]
    bc_out[got_at, :] = got[:, width:]
    b = bc_out[:, :state_width].T
    span = min(256, width)
    for low in range(0, width, span):
        at = slice(low, low + span)
        tails = mm(tail[...], head_lanes(2, heads, head_width, span, first_lane + low))
        weighted = (x_out[:, at].astype(F32) * tails).astype(BF16)
        s_out[:, at] = mm(b, weighted).astype(BF16)
        d_out[:, at] = mm(kept[...], head_lanes(3, heads, head_width, span, first_lane + low))


def intra_kernel(
    meta, docs, x, bc, cum, dlt, gate_own, gate_got, gain,
    a_out, f_out, state, base, spread, skip, reach, into, tail,
    *, head_width, first_head, group_heads,
):
    step = pl.program_id(0)
    count, width = x.shape
    heads = cum.shape[1]
    state_width = bc.shape[1] // 2
    first = meta[1] + step * count

    @pl.when(step == 0)
    def _():
        state[...] = jnp.zeros_like(state)
        base[...] = jnp.zeros_like(base)
        spread[...] = head_lanes(3, heads, head_width, width, first_head * head_width)
        mine = jnp.where(meta[0] == 0, gain[:, :heads], gain[:, heads:])
        skip[...] = mm(jnp.concatenate(split3(jnp.broadcast_to(mine, (8, heads))), axis=1), spread[...])

    starts = doc_start(rows_of(count, first), docs)
    last_start = doc_start(first + count - 1, docs)
    here = cum[...]
    before = base[:1, :]
    end = here[count - 1 :]

    def spread_over(value):
        return mm(jnp.concatenate(split2(value), axis=1), spread[: 2 * heads])

    reach[...] = spread_over(jnp.where(starts < first, jnp.exp2(here - before), 0.0))
    into[...] = spread_over(jnp.where(starts < meta[1], jnp.exp2(here), 0.0))
    to_end = jnp.exp2(end - dlt[...].T)
    tail[...] = spread_over(jnp.where(rows_of(count, first) >= last_start, to_end, 0.0))
    kept = jnp.broadcast_to(jnp.where(last_start < first, jnp.exp2(end - before), 0.0), (8, heads))
    kept = mm(jnp.concatenate(split3(kept), axis=1), spread[...])[:1]
    row = lax.broadcasted_iota(jnp.int32, (count, count), 0)
    col = lax.broadcasted_iota(jnp.int32, (count, count), 1)
    is_own = (step * count) // (count * (pl.num_programs(0) // 2)) == meta[0]
    low_lanes = lax.broadcasted_iota(jnp.int32, (count, 2 * head_width), 1) < head_width
    zero = jnp.zeros((count, 2 * head_width), BF16)
    b = bc[:, :state_width]
    c = bc[:, state_width:]
    b_turned = b.T
    scores = jnp.where((col <= row) & (col >= starts - first), contract_lanes(c, b), 0.0)
    for head in range(0, group_heads, 2):
        at = slice(head * head_width, (head + 2) * head_width)
        pair = []
        for k in (first_head + head, first_head + head + 1):
            exponent = jnp.minimum(here[:, k : k + 1] - dlt[k : k + 1, :], CEILING)
            pair.append((jnp.exp2(exponent) * scores).astype(BF16))
        value = x[:, at]
        stacked = jnp.concatenate([jnp.where(low_lanes, value, zero), jnp.where(low_lanes, zero, value)], axis=0)
        within = mm(jnp.concatenate(pair, axis=1), stacked)
        old = state[:, at]
        carried = mm(c, old.astype(BF16)) * reach[:, at]
        x_part = value.astype(F32)
        y = within + carried + x_part * skip[:1, at]
        gate = silu(jnp.where(is_own, gate_own[:, at], gate_got[:, at]).astype(F32))
        a_out[:, at] = y * gate
        f_out[:, at] = gate * into[:, at]
        fresh = mm(b_turned, (x_part * tail[:, at]).astype(BF16))
        state[:, at] = old * kept[:, at] + fresh
    base[...] = jnp.broadcast_to(end, base.shape)


def normed(a, f, bc, incoming, gain, squares, divisor):
    state_width = bc.shape[1] // 2
    gated = a[...] + mm(bc[:, state_width:], incoming[...]) * f[...]
    total = jnp.sum(gated * gated, axis=1, keepdims=True) if squares is None else squares[...]
    return (gated * lax.rsqrt(total / divisor + EPSILON) * gain[...]).astype(BF16)


def norm_kernel(meta, a, f, bc, incoming, gain, hidden, *, divisor):
    hidden[...] = normed(a, f, bc, incoming, gain, None, divisor)


def project_kernel(meta, *refs, ready, squared, divisor):
    refs = list(refs)
    rows = []
    for _ in range(2):
        rows.append((refs[:ready], refs[ready : ready + 3], refs[ready + 3] if squared else None))
        refs = refs[ready + 3 + squared :]
    incoming, gain, w, hidden, send, keep = refs
    count = send.shape[0]

    @pl.when(pl.program_id(0) == 0)
    def _():
        for index, (done, (a, f, bc), squares) in enumerate(rows):
            at = slice(index * count, (index + 1) * count)
            width = a.shape[1]
            for group, part in enumerate(done):
                hidden[at, group * width : (group + 1) * width] = part[...]
            hidden[at, ready * width :] = normed(a, f, bc, incoming, gain, squares, divisor)

    product = mm(hidden[...], w[...])
    send[...] = product[:count].astype(BF16)
    keep[...] = product[count:]


def product_kernel(meta, *refs):
    hiddens, (w, send, keep) = refs[:-3], refs[-3:]
    count = hiddens[0].shape[0] // 2
    for index, hidden in enumerate(hiddens):
        at = slice(index * count, (index + 1) * count)
        product = mm(hidden[...], w[...])
        send[at, :] = product[:count].astype(BF16)
        keep[at, :] = product[count:]


def local(
    x_input, gate_input, state_proj, mix_weight, mix_bias, state_weight, state_bias,
    step_raw, decay_log, skip_gain, norm_gain, out_weight, doc_lengths,
):
    half, channels = x_input.shape
    all_heads = step_raw.shape[1]
    groups, _, state_width = state_proj.shape[1:]
    taps = mix_weight.shape[0]
    features = out_weight.shape[1]
    head_width = channels // all_heads
    heads = all_heads // 2
    width = channels // 2
    count = 2 * half
    whole_groups = groups % 2 == 0
    parts = groups // 2 if whole_groups else groups
    part_heads = heads // parts
    part_width = part_heads * head_width
    block = 2 * state_width
    chunks = count // CHUNK
    splits = half // CHUNK
    sub = lax.axis_index("sub").astype(jnp.int32)
    ctx = lax.axis_index("ctx").astype(jnp.int32)
    tp = lax.axis_index("tp").astype(jnp.int32)
    tp_size = lax.axis_size("tp")
    ctx_size = lax.axis_size("ctx")
    docs = doc_lengths.astype(jnp.int32)
    meta = jnp.stack([sub, ctx * count, tp])
    params = pltpu.CompilerParams(vmem_limit_bytes=VMEM)
    fixed = lambda *shape: pl.BlockSpec(shape, lambda i, *m: (0,) * len(shape))
    shape_of = jax.ShapeDtypeStruct

    def call(body, name, grid, in_specs, out_specs, out_shape, scratch=(), flops=0, moved=0, prefetch=2):
        return pl.pallas_call(
            body,
            grid_spec=pltpu.PrefetchScalarGridSpec(
                num_scalar_prefetch=prefetch, grid=grid, in_specs=in_specs, out_specs=out_specs,
                scratch_shapes=list(scratch),
            ),
            out_shape=out_shape,
            compiler_params=params,
            cost_estimate=pl.CostEstimate(flops=flops, bytes_accessed=moved, transcendentals=0),
            name=name,
        )

    s_input = state_proj.reshape(half, groups * block)
    s_weight = state_weight.reshape(taps, groups * block)
    s_bias = state_bias.reshape(1, groups * block)
    bias = mix_bias.reshape(1, channels)
    rims = 16
    s_rim = state_proj[half - rims :].reshape(rims, groups * block)
    rim = shifted(jnp.concatenate([x_input[half - rims :], s_rim], axis=1), ("ctx", "sub"), 1)
    raw = step_raw.T
    got_raw = swapped(raw, "sub")
    mixed = (x_input, rim, mix_weight, bias, s_input, rim, s_weight, s_bias)

    def mix_specs(part, other):
        at = lambda m: (1 - m[0] if other else m[0]) * parts + part
        s_at = at if whole_groups else (lambda m: 0)
        rim_at = lambda m: channels // block + s_at(m)
        specs = []
        for size, places in ((part_width, (at, at, at, at)), (block, (s_at, rim_at, s_at, s_at))):
            for rows, place in zip((half, rims, taps, 1), places):
                specs.append(pl.BlockSpec((rows, size), lambda i, m, d, place=place: (0, place(m))))
        return specs

    got = []
    for part in range(parts):
        other = call(
            functools.partial(conv_kernel, taps=taps), "conv", (1,), mix_specs(part, True),
            fixed(half, part_width + block), shape_of((half, part_width + block), BF16),
            flops=2 * taps * half * half * part_width, moved=4 * half * part_width,
        )(meta, docs, *mixed)
        got.append(swapped(other, "sub"))

    cum, dlt, tail, kept = call(
        decay_kernel, "decay", (1,),
        [fixed(all_heads, half), fixed(all_heads, half), fixed(all_heads, 1)],
        [fixed(count, heads), fixed(heads, count), fixed(count, 2 * heads), fixed(8, 3 * heads)],
        [
            shape_of((count, heads), F32), shape_of((heads, count), F32),
            shape_of((count, 2 * heads), BF16), shape_of((8, 3 * heads), BF16),
        ],
        [pltpu.VMEM((heads, count), F32)], flops=2 * count * count * 128, moved=16 * count * heads,
    )(meta, docs, raw, got_raw, decay_log.reshape(all_heads, 1))

    def onward(shard):
        return lax.ppermute(shard, "ctx", [(i, (i + 1) % ctx_size) for i in range(ctx_size)])

    made = []
    for part in range(parts):
        x_cat, bc, state, decay = call(
            functools.partial(
                state_kernel, taps=taps, heads=heads, head_width=head_width, first_lane=part * part_width
            ),
            "state", (1,),
            mix_specs(part, False)
            + [fixed(half, part_width + block), fixed(count, 2 * heads), fixed(8, 3 * heads)],
            [
                fixed(count, part_width), fixed(count, block), fixed(state_width, part_width), fixed(8, part_width),
            ],
            [
                shape_of((count, part_width), BF16), shape_of((count, block), BF16),
                shape_of((state_width, part_width), BF16), shape_of((8, part_width), F32),
            ],
            flops=4 * half * count * part_width, moved=6 * count * part_width,
        )(meta, docs, *mixed, got[part], tail, kept)
        made.append((x_cat, bc, state, decay, onward(state)))

    got_gate = swapped(lax.dynamic_slice_in_dim(gate_input, (1 - sub) * width, width, 1), "sub")
    by_row = lambda n: pl.BlockSpec((CHUNK, n), lambda i, *m: (i, 0))
    skip = skip_gain.reshape(1, all_heads)
    ready = []
    for part in range(parts):
        x_cat, bc, state, decay, arriving = made[part]
        for _ in range(ctx_size // 2 - 1):
            arriving = onward((state.astype(F32) + decay[:1] * arriving.astype(F32)).astype(BF16))
        gate_at = lambda i, m, d, part=part: (lax.rem(i, splits), m[0] * parts + part)
        got_at = lambda i, m, d, part=part: (lax.rem(i, splits), part)
        gated, carry_gate = call(
            functools.partial(
                intra_kernel, head_width=head_width, first_head=part * part_heads, group_heads=part_heads
            ),
            "intra", (chunks,),
            [
                by_row(part_width), by_row(block), by_row(heads),
                pl.BlockSpec((heads, CHUNK), lambda i, *m: (0, i)),
                pl.BlockSpec((CHUNK, part_width), gate_at), pl.BlockSpec((CHUNK, part_width), got_at),
                fixed(1, all_heads),
            ],
            [by_row(part_width), by_row(part_width)],
            [shape_of((count, part_width), F32), shape_of((count, part_width), F32)],
            [
                pltpu.VMEM((state_width, part_width), F32), pltpu.VMEM((8, heads), F32),
                pltpu.VMEM((3 * heads, part_width), BF16), pltpu.VMEM((8, part_width), F32),
                pltpu.VMEM((CHUNK, part_width), F32), pltpu.VMEM((CHUNK, part_width), F32),
                pltpu.VMEM((CHUNK, part_width), F32),
            ],
            flops=10 * count * part_width * CHUNK, moved=14 * count * part_width,
        )(meta, docs, x_cat, bc, cum, dlt, gate_input, got_gate, skip)
        ready.append((gated, carry_gate, bc, arriving))

    divisor = HEADS // GROUPS * head_width
    gain = norm_gain.reshape(1, channels)
    gain_at = lambda part: pl.BlockSpec((1, part_width), lambda i, m: (0, m[0] * parts + part))
    hiddens = []
    for part, (gated, carry_gate, bc, arriving) in enumerate(ready[:-1]):
        hiddens.append(
            call(
                functools.partial(norm_kernel, divisor=divisor), "norm", (chunks,),
                [by_row(part_width), by_row(part_width), by_row(block), fixed(state_width, part_width), gain_at(part)],
                by_row(part_width), shape_of((count, part_width), BF16),
                flops=2 * count * part_width * state_width, moved=10 * count * part_width, prefetch=1,
            )(meta, gated, carry_gate, bc, arriving, gain)
        )

    gated, carry_gate, bc, arriving = ready[-1]
    squares = []
    if not whole_groups:
        total = gated + jnp.dot(bc[:, state_width:], arriving, preferred_element_type=F32) * carry_gate
        mine = jnp.sum(total * total, axis=1, keepdims=True)
        squares = [mine + swapped(mine, "sub")]
    operands = [*hiddens, gated, carry_gate, bc, *squares]
    out_cols = features // tp_size
    mm_cols = min(512, out_cols)
    pair = tp_size == 2
    near_blocks = out_cols // mm_cols
    far_blocks = near_blocks if pair else features // mm_cols
    far_at = (lambda i, m: (1 - m[2]) * near_blocks + i) if pair else (lambda i, m: i)
    far_cols = far_blocks * mm_cols
    far, kept_rows = [], []
    for split in range(splits):
        there = lambda i, m, split=split: ((1 - m[0]) * splits + split, 0)
        here = lambda i, m, split=split: (m[0] * splits + split, 0)
        specs = [pl.BlockSpec((CHUNK, v.shape[1]), at) for at in (there, here) for v in operands]
        specs += [
            fixed(state_width, part_width), gain_at(parts - 1),
            pl.BlockSpec((width, mm_cols), lambda i, m: (0, far_at(i, m))),
        ]
        hidden, send, keep = call(
            functools.partial(project_kernel, ready=len(hiddens), squared=len(squares), divisor=divisor),
            "project", (far_blocks,), specs,
            [
                fixed(2 * CHUNK, width),
                pl.BlockSpec((CHUNK, mm_cols), lambda i, m: (0, i)),
                pl.BlockSpec((CHUNK, mm_cols), lambda i, m: (0, i)),
            ],
            [
                shape_of((2 * CHUNK, width), BF16), shape_of((CHUNK, far_cols), BF16),
                shape_of((CHUNK, far_cols), F32),
            ],
            flops=4 * CHUNK * width * far_cols, moved=2 * width * far_cols, prefetch=1,
        )(meta, *operands, *operands, arriving, gain, out_weight)
        summed = (keep + swapped(send, "sub").astype(F32)).astype(BF16)
        far.append(swapped(summed, "tp") if pair else summed)
        kept_rows.append(hidden)
    if not pair:
        return lax.psum_scatter(jnp.concatenate(far), "tp", scatter_dimension=1, tiled=True)
    send, keep = call(
        product_kernel, "product", (near_blocks,),
        [fixed(2 * CHUNK, width)] * splits
        + [pl.BlockSpec((width, mm_cols), lambda i, m: (0, m[2] * near_blocks + i))],
        [pl.BlockSpec((half, mm_cols), lambda i, m: (0, i)), pl.BlockSpec((half, mm_cols), lambda i, m: (0, i))],
        [shape_of((half, out_cols), BF16), shape_of((half, out_cols), F32)],
        flops=2 * count * width * out_cols, moved=2 * width * out_cols, prefetch=1,
    )(meta, *kept_rows, out_weight)
    near = keep + swapped(send, "sub").astype(F32)
    return (near + jnp.concatenate(far).astype(F32)).astype(BF16)


def solution(mesh):
    in_specs = (
        P(("groups", "ctx", "sub"), "tp"),
        P(("groups", "ctx", "sub"), "tp"),
        P(("groups", "ctx", "sub"), "tp", None, None),
        P(None, "tp"),
        P("tp"),
        P(None, "tp", None, None),
        P("tp", None, None),
        P(("groups", "ctx", "sub"), "tp"),
        P("tp"),
        P("tp"),
        P("tp"),
        P(("tp", "sub"), None),
        P("groups"),
    )
    out_specs = P(("groups", "ctx", "sub"), "tp")
    return jax.shard_map(local, mesh=mesh, in_specs=in_specs, out_specs=out_specs, check_vma=False)
```

profile of v0, /device:TPU:0, one launch (start us, length us, event | category | flops | bytes accessed | tf_op | source)
XLA Modules:
  0.0 127.6 jit_solution(12937807687372193429)
XLA Ops:
  0.0 0.8 slice.13
  0.8 0.9 slice.12
  1.8 2.4 %collective-permute-start = (bf16[16,5120]{1,0:T(8,128)(2,1)S(1)}, bf16[16,5120]{1,0:T(8,128)(2,1)S(1)}, u32[]{:S(2)}, u32[]{:S(2)}) collective-permute-start(bf16[16,5120]{1,0:T(8,128)(2,1)S(1)} %pad_maximum_fusion), channel_id=1, source_target_pairs={{0,1},{1,4},{4,5},{5,8},{8,9},{9,12},{12,13},{2,3},{3,6},{6,7},{7,... | collective-permute-start | bytes 491528 | tf_op jit(solution)/shard_map/ppermute | solution.py:24
  4.1 2.2 %reshape.26.s = bf16[256,1024]{1,0:T(8,128)(2,1)} reshape(bf16[256,4,2,128]{3,2,1,0:T(2,128)(2,1)} %param.15) | data formatting | bytes 1048576 | tf_op jit(solution)/shard_map/reshape | solution.py:334
  6.3 1.3 %reshape.27.sw = bf16[4,1024]{1,0:T(4,128)(2,1)} reshape(bf16[4,4,2,128]{3,2,1,0:T(2,128)(2,1)} %param.18) | data formatting | bytes 16384 | tf_op jit(solution)/shard_map/reshape | solution.py:335
  8.9 3.6 %conv.2 = bf16[256,1280]{1,0:T(8,128)(2,1)} custom-call(s32[3]{0:T(128)} %pad_add_fusion.meta, s32[8]{0:T(128)} %docs.13, bf16[256,4096]{1,0:T(8,128)(2,1)} %x.7, bf16[16,5120]{1,0:T(8,128)(2,1)} %copy-done.1, bf16[4,4096]{1,0:T(4,128)(2,1)} %w.7, f32[1,4096]{1,0:T(1,128)} %bitcast.11, bf16[256,1024]{1,0:T(8,128)(2,1)} %reshape.26.s, ...), custom_call_target="tpu_custom_call" | custom-call | flops 536870912 | bytes 1048576 | tf_op jit(solution)/shard_map/conv/pallas_call | solution.py:357
  12.6 2.7 %collective-permute-start.1 = (bf16[256,1280]{1,0:T(8,128)(2,1)}, bf16[256,1280]{1,0:T(8,128)(2,1)}, u32[]{:S(2)}, u32[]{:S(2)}) collective-permute-start(bf16[256,1280]{1,0:T(8,128)(2,1)} %conv.2), channel_id=1, source_target_pairs={{0,1},{1,0},{2,3},{3,2},{4,5},{5,4},{6,7},{7,6},{8,9},{9,8},{10,11... | collective-permute-start | bytes 1966088 | tf_op jit(solution)/shard_map/ppermute | solution.py:28
  15.3 3.6 %conv.3 = bf16[256,1280]{1,0:T(8,128)(2,1)} custom-call(s32[3]{0:T(128)} %pad_add_fusion.meta, s32[8]{0:T(128)} %docs.13, bf16[256,4096]{1,0:T(8,128)(2,1)} %x.7, bf16[16,5120]{1,0:T(8,128)(2,1)} %copy-done.1, bf16[4,4096]{1,0:T(4,128)(2,1)} %w.7, f32[1,4096]{1,0:T(1,128)} %bitcast.12, bf16[256,1024]{1,0:T(8,128)(2,1)} %reshape.26.s, ...), custom_call_target="tpu_custom_call" | custom-call | flops 536870912 | bytes 1048576 | tf_op jit(solution)/shard_map/conv/pallas_call | solution.py:357
  19.8 0.7 copy.14.rate
  20.5 2.2 %collective-permute-done.2.got_raw = f32[64,256]{1,0:T(8,128)S(1)} collective-permute-done((f32[64,256]{1,0:T(8,128)S(1)}, f32[64,256]{1,0:T(8,128)S(1)}, u32[]{:S(2)}, u32[]{:S(2)}) %collective-permute-start.2) | collective-permute-done | bytes 65568 | tf_op jit(solution)/shard_map/ppermute | solution.py:28
  23.2 2.9 %decay.1 = (f32[512,32]{1,0:T(8,128)}, f32[32,512]{1,0:T(8,128)}, bf16[512,64]{1,0:T(8,128)(2,1)}, bf16[8,96]{1,0:T(8,128)(2,1)}) custom-call(s32[3]{0:T(128)} %pad_add_fusion.meta, s32[8]{0:T(128)} %docs.13, f32[64,256]{1,0:T(8,128)} %bitcast.27, f32[64,256]{1,0:T(8,128)} %copy-done.11, f32[64,1]{1,0:T(8,128)} %copy.14.rate), custom_call_target="tpu_custom_call" | custom-call | flops 67108864 | bytes 262144 | tf_op jit(solution)/shard_map/decay/pallas_call | solution.py:364
  26.2 5.2 %state.2 = (bf16[512,1024]{1,0:T(8,128)(2,1)}, bf16[512,256]{1,0:T(8,128)(2,1)}, bf16[128,1024]{1,0:T(8,128)(2,1)}, f32[8,1024]{1,0:T(8,128)}) custom-call(s32[3]{0:T(128)} %pad_add_fusion.meta, s32[8]{0:T(128)} %docs.13, bf16[256,4096]{1,0:T(8,128)(2,1)} %x.7, bf16[16,5120]{1,0:T(8,128)(2,1)} %copy-done.1, bf16[4,4096]{1,0:T(4,128)(2,1)} %w.7, ...), custom_call_target="tpu_custom_call" | custom-call | flops 536870912 | bytes 3145728 | tf_op jit(solution)/shard_map/state/pallas_call | solution.py:380
  31.3 1.6 %collective-permute-start.4 = (bf16[128,1024]{1,0:T(8,128)(2,1)}, bf16[128,1024]{1,0:T(8,128)(2,1)S(1)}, u32[]{:S(2)}, u32[]{:S(2)}) collective-permute-start(bf16[128,1024]{1,0:T(8,128)(2,1)} %get-tuple-element.37), channel_id=1, source_target_pairs={{0,4},{4,8},{8,12},{12,0},{1,5},{5,9},{9,13},{13,1},{2,6},{6,10},{... | collective-permute-start | bytes 786440 | tf_op jit(solution)/shard_map/ppermute | solution.py:376
  32.9 5.1 %state.3 = (bf16[512,1024]{1,0:T(8,128)(2,1)}, bf16[512,256]{1,0:T(8,128)(2,1)}, bf16[128,1024]{1,0:T(8,128)(2,1)}, f32[8,1024]{1,0:T(8,128)}) custom-call(s32[3]{0:T(128)} %pad_add_fusion.meta, s32[8]{0:T(128)} %docs.13, bf16[256,4096]{1,0:T(8,128)(2,1)} %x.7, bf16[16,5120]{1,0:T(8,128)(2,1)} %copy-done.1, bf16[4,4096]{1,0:T(4,128)(2,1)} %w.7, ...), custom_call_target="tpu_custom_call" | custom-call | flops 536870912 | bytes 3145728 | tf_op jit(solution)/shard_map/state/pallas_call | solution.py:380
  38.0 1.6 %collective-permute-start.7 = (bf16[128,1024]{1,0:T(8,128)(2,1)}, bf16[128,1024]{1,0:T(8,128)(2,1)S(1)}, u32[]{:S(2)}, u32[]{:S(2)}) collective-permute-start(bf16[128,1024]{1,0:T(8,128)(2,1)} %get-tuple-element.43), channel_id=1, source_target_pairs={{0,4},{4,8},{8,12},{12,0},{1,5},{5,9},{9,13},{13,1},{2,6},{6,10},{... | collective-permute-start | bytes 786440 | tf_op jit(solution)/shard_map/ppermute | solution.py:376
  39.6 0.8 slice.14
  40.4 0.8 slice.15
  41.9 7.3 %collective-permute-done.7 = bf16[128,1024]{1,0:T(8,128)(2,1)S(1)} collective-permute-done((bf16[128,1024]{1,0:T(8,128)(2,1)}, bf16[128,1024]{1,0:T(8,128)(2,1)S(1)}, u32[]{:S(2)}, u32[]{:S(2)}) %collective-permute-start.7) | collective-permute-done | bytes 262176 | tf_op jit(solution)/shard_map/ppermute | solution.py:376
  49.2 1.0 add_convert_fusion.3
  50.5 1.0 copy-done.2
  51.5 7.5 %intra.2 = (f32[512,1024]{1,0:T(8,128)}, f32[512,1024]{1,0:T(8,128)}) custom-call(s32[3]{0:T(128)} %pad_add_fusion.meta, s32[8]{0:T(128)} %docs.13, bf16[512,1024]{1,0:T(8,128)(2,1)} %get-tuple-element.31.x, bf16[512,256]{1,0:T(8,128)(2,1)} %get-tuple-element.32.bc, f32[512,32]{1,0:T(8,128)} %get-tuple-element.33.cum, f32[32,512]{1,0:T(8,128)} %get-tuple-element.34.dlt, ...), custom_call_target="tpu_custom_call" | custom-call | flops 671088640 | bytes 7340032 | tf_op jit(solution)/shard_map/intra/pallas_call | solution.py:408
  59.0 7.5 %intra.3 = (f32[512,1024]{1,0:T(8,128)}, f32[512,1024]{1,0:T(8,128)}) custom-call(s32[3]{0:T(128)} %pad_add_fusion.meta, s32[8]{0:T(128)} %docs.13, bf16[512,1024]{1,0:T(8,128)(2,1)} %get-tuple-element.39.x, bf16[512,256]{1,0:T(8,128)(2,1)} %get-tuple-element.40.bc.refs_3_.refs_7_, f32[512,32]{1,0:T(8,128)} %get-tuple-element.33.cum, ...), custom_call_target="tpu_custom_call" | custom-call | flops 671088640 | bytes 7340032 | tf_op jit(solution)/shard_map/intra/pallas_call | solution.py:408
  67.2 5.5 %norm.1.refs_0_.refs_4_ = bf16[512,1024]{1,0:T(8,128)(2,1)} custom-call(s32[3]{0:T(128)} %pad_add_fusion.meta, f32[512,1024]{1,0:T(8,128)} %get-tuple-element.35.a, f32[512,1024]{1,0:T(8,128)} %get-tuple-element.36.f, bf16[512,256]{1,0:T(8,128)(2,1)} %get-tuple-element.32.bc, bf16[128,1024]{1,0:T(8,128)(2,1)} %copy-done.7, f32[1,4096]{1,0:T(1,128)} %bitcast.15), custom_call_target="tpu_custom_call" | custom-call | flops 134217728 | bytes 5242880 | tf_op jit(solution)/shard_map/norm/pallas_call | solution.py:437
  72.7 0.7 copy-done.4
  73.4 8.4 %project.3 = (bf16[256,2048]{1,0:T(8,128)(2,1)}, bf16[128,2048]{1,0:T(8,128)(2,1)}, f32[128,2048]{1,0:T(8,128)}) custom-call(s32[3]{0:T(128)} %pad_add_fusion.meta, bf16[512,1024]{1,0:T(8,128)(2,1)} %norm.1.refs_0_.refs_4_, f32[512,1024]{1,0:T(8,128)} %get-tuple-element.41.refs_1_.refs_5_, f32[512,1024]{1,0:T(8,128)} %get-tuple-element.42.refs_2_.refs_6_, ...), custom_call_target="tpu_custom_call" | custom-call | flops 2147483648 | bytes 8388608 | tf_op jit(solution)/shard_map/project/pallas_call | solution.py:468
  81.8 8.4 %project.2 = (bf16[256,2048]{1,0:T(8,128)(2,1)}, bf16[128,2048]{1,0:T(8,128)(2,1)}, f32[128,2048]{1,0:T(8,128)}) custom-call(s32[3]{0:T(128)} %pad_add_fusion.meta, bf16[512,1024]{1,0:T(8,128)(2,1)} %norm.1.refs_0_.refs_4_, f32[512,1024]{1,0:T(8,128)} %get-tuple-element.41.refs_1_.refs_5_, f32[512,1024]{1,0:T(8,128)} %get-tuple-element.42.refs_2_.refs_6_, ...), custom_call_target="tpu_custom_call" | custom-call | flops 2147483648 | bytes 8388608 | tf_op jit(solution)/shard_map/project/pallas_call | solution.py:468
  90.8 9.6 %product.1 = (bf16[256,2048]{1,0:T(8,128)(2,1)}, f32[256,2048]{1,0:T(8,128)}) custom-call(s32[3]{0:T(128)} %pad_add_fusion.meta, bf16[256,2048]{1,0:T(8,128)(2,1)} %get-tuple-element.45.refs_0_, bf16[256,2048]{1,0:T(8,128)(2,1)} %get-tuple-element.46.refs_1_, bf16[2048,4096]{1,0:T(8,128)(2,1)} %refs_2_.1), custom_call_target="tpu_custom_call" | custom-call | flops 4294967296 | bytes 8388608 | tf_op jit(solution)/shard_map/product/pallas_call | solution.py:487
  100.6 1.6 %collective-permute-start.13 = (bf16[128,2048]{1,0:T(8,128)(2,1)S(1)}, bf16[128,2048]{1,0:T(8,128)(2,1)S(1)}, u32[]{:S(2)}, u32[]{:S(2)}) collective-permute-start(bf16[128,2048]{1,0:T(8,128)(2,1)S(1)} %add_convert_fusion.1), channel_id=1, source_target_pairs={{0,2},{2,0},{1,3},{3,1},{4,6},{6,4},{5,7},{7,5},{8,10},{10,8},{9,1... | collective-permute-start | bytes 1572872 | tf_op jit(solution)/shard_map/ppermute | solution.py:28
  102.3 1.1 collective-permute-start.11
  103.3 12.0 %collective-permute-done.13 = bf16[128,2048]{1,0:T(8,128)(2,1)S(1)} collective-permute-done((bf16[128,2048]{1,0:T(8,128)(2,1)S(1)}, bf16[128,2048]{1,0:T(8,128)(2,1)S(1)}, u32[]{:S(2)}, u32[]{:S(2)}) %collective-permute-start.13) | collective-permute-done | bytes 524320 | tf_op jit(solution)/shard_map/ppermute | solution.py:28
  115.4 10.8 %collective-permute-done.11 = bf16[128,2048]{1,0:T(8,128)(2,1)S(1)} collective-permute-done((bf16[128,2048]{1,0:T(8,128)(2,1)S(1)}, bf16[128,2048]{1,0:T(8,128)(2,1)S(1)}, u32[]{:S(2)}, u32[]{:S(2)}) %collective-permute-start.11) | collective-permute-done | bytes 524320 | tf_op jit(solution)/shard_map/ppermute | solution.py:28
  126.2 1.4 %add_convert_fusion = bf16[256,2048]{1,0:T(8,128)(2,1)} fusion(f32[256,2048]{1,0:T(8,128)S(1)} %copy-done.3, bf16[256,2048]{1,0:T(8,128)(2,1)S(1)} %collective-permute-done.9, bf16[128,2048]{1,0:T(8,128)(2,1)S(1)} %collective-permute-done.13, bf16[128,2048]{1,0:T(8,128)(2,1)S(1)} %collective-permute-done.11), kind=kLoop, calls=%fused_computation | loop fusion | flops 4194304 | bytes 5242880 | tf_op jit(solution)/shard_map/convert_element_type | solution.py:496
  (47 shorter events, 5.2 us)
Async XLA Ops:
  1.8 6.5 %collective-permute-start = (bf16[16,5120]{1,0:T(8,128)(2,1)S(1)}, bf16[16,5120]{1,0:T(8,128)(2,1)S(1)}, u32[]{:S(2)}, u32[]{:S(2)}) collective-permute-start(bf16[16,5120]{1,0:T(8,128)(2,1)S(1)} %pad_maximum_fusion), channel_id=1, source_target_pairs={{0,1},{1,4},{4,5},{5,8},{8,9},{9,12},{12,13},{2,3},{3,6},{6,7},{7,... | collective-permute-start | bytes 491528 | tf_op jit(solution)/shard_map/ppermute | solution.py:24
  8.2 0.7 copy-start.1
  12.5 6.5 %copy-start = (bf16[256,4096]{1,0:T(8,128)(2,1)S(1)}, bf16[256,4096]{1,0:T(8,128)(2,1)}, u32[]{:S(2)}) copy-start(bf16[256,4096]{1,0:T(8,128)(2,1)} %gate_own.3) | copy-start | bytes 6291460
  12.5 7.1 %copy-start.10 = (f32[256,64]{0,1:T(8,128)S(1)}, f32[256,64]{0,1:T(8,128)}, u32[]{:S(2)}) copy-start(f32[256,64]{0,1:T(8,128)} %param.20) | copy-start | bytes 196612
  12.5 7.2 %copy-start.9 = (f32[64]{0:T(128)S(1)}, f32[64]{0:T(128)}, u32[]{:S(2)}) copy-start(f32[64]{0:T(128)} %param.21) | copy-start | bytes 772
  12.6 13.6 %collective-permute-start.1 = (bf16[256,1280]{1,0:T(8,128)(2,1)}, bf16[256,1280]{1,0:T(8,128)(2,1)}, u32[]{:S(2)}, u32[]{:S(2)}) collective-permute-start(bf16[256,1280]{1,0:T(8,128)(2,1)} %conv.2), channel_id=1, source_target_pairs={{0,1},{1,0},{2,3},{3,2},{4,5},{5,4},{6,7},{7,6},{8,9},{9,8},{10,11... | collective-permute-start | bytes 1966088 | tf_op jit(solution)/shard_map/ppermute | solution.py:28
  18.9 14.0 %collective-permute-start.6 = (bf16[256,1280]{1,0:T(8,128)(2,1)}, bf16[256,1280]{1,0:T(8,128)(2,1)}, u32[]{:S(2)}, u32[]{:S(2)}) collective-permute-start(bf16[256,1280]{1,0:T(8,128)(2,1)} %conv.3), channel_id=1, source_target_pairs={{0,1},{1,0},{2,3},{3,2},{4,5},{5,4},{6,7},{7,6},{8,9},{9,8},{10,11... | collective-permute-start | bytes 1966088 | tf_op jit(solution)/shard_map/ppermute | solution.py:28
  19.2 31.3 %collective-permute-start.3 = (bf16[256,2048]{1,0:T(8,128)(2,1)S(1)}, bf16[256,2048]{1,0:T(8,128)(2,1)S(1)}, u32[]{:S(2)}, u32[]{:S(2)}) collective-permute-start(bf16[256,2048]{1,0:T(8,128)(2,1)S(1)} %constant_dynamic-slice_fusion), channel_id=1, source_target_pairs={{0,1},{1,0},{2,3},{3,2},{4,5},{5,4},{6,7},{7,6},{8,9},{9,8},{10,11... | collective-permute-start | bytes 3145736 | tf_op jit(solution)/shard_map/ppermute | solution.py:28
  19.6 3.0 %collective-permute-start.2 = (f32[64,256]{1,0:T(8,128)S(1)}, f32[64,256]{1,0:T(8,128)S(1)}, u32[]{:S(2)}, u32[]{:S(2)}) collective-permute-start(f32[64,256]{1,0:T(8,128)S(1)} %bitcast.28), channel_id=1, source_target_pairs={{0,1},{1,0},{2,3},{3,2},{4,5},{5,4},{6,7},{7,6},{8,9},{9,8},{10,11... | collective-permute-start | bytes 196616 | tf_op jit(solution)/shard_map/ppermute | solution.py:28
  22.6 0.6 copy-start.11
  31.3 10.4 %copy-start.8 = (bf16[128,1024]{1,0:T(8,128)(2,1)S(1)}, bf16[128,1024]{1,0:T(8,128)(2,1)}, u32[]{:S(2)}) copy-start(bf16[128,1024]{1,0:T(8,128)(2,1)} %get-tuple-element.37) | copy-start | bytes 786436
  31.3 10.4 %collective-permute-start.4 = (bf16[128,1024]{1,0:T(8,128)(2,1)}, bf16[128,1024]{1,0:T(8,128)(2,1)S(1)}, u32[]{:S(2)}, u32[]{:S(2)}) collective-permute-start(bf16[128,1024]{1,0:T(8,128)(2,1)} %get-tuple-element.37), channel_id=1, source_target_pairs={{0,4},{4,8},{8,12},{12,0},{1,5},{5,9},{9,13},{13,1},{2,6},{6,10},{... | collective-permute-start | bytes 786440 | tf_op jit(solution)/shard_map/ppermute | solution.py:376
  38.0 11.2 %collective-permute-start.7 = (bf16[128,1024]{1,0:T(8,128)(2,1)}, bf16[128,1024]{1,0:T(8,128)(2,1)S(1)}, u32[]{:S(2)}, u32[]{:S(2)}) collective-permute-start(bf16[128,1024]{1,0:T(8,128)(2,1)} %get-tuple-element.43), channel_id=1, source_target_pairs={{0,4},{4,8},{8,12},{12,0},{1,5},{5,9},{9,13},{13,1},{2,6},{6,10},{... | collective-permute-start | bytes 786440 | tf_op jit(solution)/shard_map/ppermute | solution.py:376
  41.8 24.7 %collective-permute-start.5 = (bf16[128,1024]{1,0:T(8,128)(2,1)S(1)}, bf16[128,1024]{1,0:T(8,128)(2,1)S(1)}, u32[]{:S(2)}, u32[]{:S(2)}) collective-permute-start(bf16[128,1024]{1,0:T(8,128)(2,1)S(1)} %add_convert_fusion.4), channel_id=1, source_target_pairs={{0,4},{4,8},{8,12},{12,0},{1,5},{5,9},{9,13},{13,1},{2,6},{6,10},{... | collective-permute-start | bytes 786440 | tf_op jit(solution)/shard_map/ppermute | solution.py:376
  50.3 22.4 %collective-permute-start.8 = (bf16[128,1024]{1,0:T(8,128)(2,1)S(1)}, bf16[128,1024]{1,0:T(8,128)(2,1)S(1)}, u32[]{:S(2)}, u32[]{:S(2)}) collective-permute-start(bf16[128,1024]{1,0:T(8,128)(2,1)S(1)} %add_convert_fusion.3), channel_id=1, source_target_pairs={{0,4},{4,8},{8,12},{12,0},{1,5},{5,9},{9,13},{13,1},{2,6},{6,10},{... | collective-permute-start | bytes 786440 | tf_op jit(solution)/shard_map/ppermute | solution.py:376
  50.5 1.0 copy-start.2
  66.5 0.7 copy-start.7
  72.7 0.7 copy-start.4
  81.8 18.6 %collective-permute-start.12 = (bf16[128,2048]{1,0:T(8,128)(2,1)}, bf16[128,2048]{1,0:T(8,128)(2,1)S(1)}, u32[]{:S(2)}, u32[]{:S(2)}) collective-permute-start(bf16[128,2048]{1,0:T(8,128)(2,1)} %get-tuple-element.52), channel_id=1, source_target_pairs={{0,1},{1,0},{2,3},{3,2},{4,5},{5,4},{6,7},{7,6},{8,9},{9,8},{10,11... | collective-permute-start | bytes 1572872 | tf_op jit(solution)/shard_map/ppermute | solution.py:28
  90.3 11.8 %collective-permute-start.10 = (bf16[128,2048]{1,0:T(8,128)(2,1)}, bf16[128,2048]{1,0:T(8,128)(2,1)S(1)}, u32[]{:S(2)}, u32[]{:S(2)}) collective-permute-start(bf16[128,2048]{1,0:T(8,128)(2,1)} %get-tuple-element.50), channel_id=1, source_target_pairs={{0,1},{1,0},{2,3},{3,2},{4,5},{5,4},{6,7},{7,6},{8,9},{9,8},{10,11... | collective-permute-start | bytes 1572872 | tf_op jit(solution)/shard_map/ppermute | solution.py:28
  90.8 9.7 %copy-start.6 = (f32[128,2048]{1,0:T(8,128)S(1)}, f32[128,2048]{1,0:T(8,128)}, u32[]{:S(2)}) copy-start(f32[128,2048]{1,0:T(8,128)} %get-tuple-element.51) | copy-start | bytes 3145732
  100.4 1.7 %copy-start.5 = (f32[128,2048]{1,0:T(8,128)S(1)}, f32[128,2048]{1,0:T(8,128)}, u32[]{:S(2)}) copy-start(f32[128,2048]{1,0:T(8,128)} %get-tuple-element.49) | copy-start | bytes 3145732
  100.4 2.9 %collective-permute-start.9 = (bf16[256,2048]{1,0:T(8,128)(2,1)}, bf16[256,2048]{1,0:T(8,128)(2,1)S(1)}, u32[]{:S(2)}, u32[]{:S(2)}) collective-permute-start(bf16[256,2048]{1,0:T(8,128)(2,1)} %get-tuple-element.48), channel_id=1, source_target_pairs={{0,1},{1,0},{2,3},{3,2},{4,5},{5,4},{6,7},{7,6},{8,9},{9,8},{10,11... | collective-permute-start | bytes 3145736 | tf_op jit(solution)/shard_map/ppermute | solution.py:28
  100.5 25.7 %copy-start.3 = (f32[256,2048]{1,0:T(8,128)S(1)}, f32[256,2048]{1,0:T(8,128)}, u32[]{:S(2)}) copy-start(f32[256,2048]{1,0:T(8,128)} %get-tuple-element.47) | copy-start | bytes 6291460
  100.6 14.8 %collective-permute-start.13 = (bf16[128,2048]{1,0:T(8,128)(2,1)S(1)}, bf16[128,2048]{1,0:T(8,128)(2,1)S(1)}, u32[]{:S(2)}, u32[]{:S(2)}) collective-permute-start(bf16[128,2048]{1,0:T(8,128)(2,1)S(1)} %add_convert_fusion.1), channel_id=1, source_target_pairs={{0,2},{2,0},{1,3},{3,1},{4,6},{6,4},{5,7},{7,5},{8,10},{10,8},{9,1... | collective-permute-start | bytes 1572872 | tf_op jit(solution)/shard_map/ppermute | solution.py:28
  102.3 23.9 %collective-permute-start.11 = (bf16[128,2048]{1,0:T(8,128)(2,1)S(1)}, bf16[128,2048]{1,0:T(8,128)(2,1)S(1)}, u32[]{:S(2)}, u32[]{:S(2)}) collective-permute-start(bf16[128,2048]{1,0:T(8,128)(2,1)S(1)} %add_convert_fusion.2), channel_id=1, source_target_pairs={{0,2},{2,0},{1,3},{3,1},{4,6},{6,4},{5,7},{7,5},{8,10},{10,8},{9,1... | collective-permute-start | bytes 1572872 | tf_op jit(solution)/shard_map/ppermute | solution.py:28
where the time goes:
time: 129 us; the launch traced here: 128 us
  Pallas kernels  67.4 us (52%)
  waiting for transfers between devices  32.9 us (26%)
  starting transfers between devices  12.5 us (10%)
  local copies, waits for them, and re-layouts  11.3 us (9%)
  other arithmetic  3.4 us (3%)
    ppermute x9, waiting for transfers between devices, swapped(): lax.ppermute(shard, axis, [(i, i ^ 1) for i in range(lax.axis_size(axis))])  25 us
    pallas_call x2, Pallas kernels, local(): call(functools.partial(project_kernel, ready=len(hiddens), squared=len(sq...  16.9 us
    pallas_call x2, Pallas kernels, local(): call(functools.partial(intra_kernel, head_width=head_width, first_head=pa...  15 us
    pallas_call x2, Pallas kernels, local(): call(functools.partial(state_kernel, taps=taps, heads=heads, head_width=h...  10.3 us
    pallas_call x1, Pallas kernels, local(): call(product_kernel, 'product', (near_blocks,), [fixed(2 * CHUNK, width)]...  9.64 us
    ppermute x4, waiting for transfers between devices, onward(): lax.ppermute(shard, 'ctx', [(i, (i + 1) % ctx_size) for i in range(ctx_si...  7.86 us
    pallas_call x2, Pallas kernels, local(): call(functools.partial(conv_kernel, taps=taps), 'conv', (1,), mix_specs(p...  7.27 us
    ppermute x9, starting transfers between devices, swapped(): lax.ppermute(shard, axis, [(i, i ^ 1) for i in range(lax.axis_size(axis))])  6.61 us
  transfers between devices with their start and end apart: 14, of which 5 were waited for; matrix products, arithmetic and copies ran while one was open for 6% of the time, Pallas kernels for 43%

commit v1 on v0

--- a/solution.py
+++ b/solution.py
@@ -26,6 +26,10 @@
 
 def swapped(shard, axis):
     return lax.ppermute(shard, axis, [(i, i ^ 1) for i in range(lax.axis_size(axis))])
+
+
+def after(*values):
+    return lax.optimization_barrier(values)
 
 
 def doc_start(positions, docs_ref):
@@ -255,36 +259,30 @@
 
 
 def project_kernel(meta, *refs, ready, squared, divisor):
-    refs = list(refs)
-    rows = []
-    for _ in range(2):
-        rows.append((refs[:ready], refs[ready : ready + 3], refs[ready + 3] if squared else None))
-        refs = refs[ready + 3 + squared :]
-    incoming, gain, w, hidden, send, keep = refs
-    count = send.shape[0]
+    a, f, bc, incoming, gain = refs[ready : ready + 5]
+    w, hidden, send, keep = refs[-4:]
+    width = a.shape[1]
 
     @pl.when(pl.program_id(0) == 0)
     def _():
-        for index, (done, (a, f, bc), squares) in enumerate(rows):
-            at = slice(index * count, (index + 1) * count)
-            width = a.shape[1]
-            for group, part in enumerate(done):
-                hidden[at, group * width : (group + 1) * width] = part[...]
-            hidden[at, ready * width :] = normed(a, f, bc, incoming, gain, squares, divisor)
-
-    product = mm(hidden[...], w[...])
-    send[...] = product[:count].astype(BF16)
-    keep[...] = product[count:]
-
-
-def product_kernel(meta, *refs):
-    hiddens, (w, send, keep) = refs[:-3], refs[-3:]
-    count = hiddens[0].shape[0] // 2
-    for index, hidden in enumerate(hiddens):
-        at = slice(index * count, (index + 1) * count)
-        product = mm(hidden[...], w[...])
-        send[at, :] = product[:count].astype(BF16)
-        keep[at, :] = product[count:]
+        for group, part in enumerate(refs[:ready]):
+            hidden[:, group * width : (group + 1) * width] = part[...]
+        squares = refs[ready + 5] if squared else None
+        hidden[:, ready * width :] = normed(a, f, bc, incoming, gain, squares, divisor)
+
+    multiply(meta, hidden, w, send, keep)
+
+
+def multiply(meta, hidden, w, send, keep):
+    half = send.shape[0]
+    there = pl.ds(pl.multiple_of((1 - meta[0]) * half, half), half)
+    here = pl.ds(pl.multiple_of(meta[0] * half, half), half)
+    send[...] = mm(hidden[there, :], w[...]).astype(BF16)
+    keep[...] = mm(hidden[here, :], w[...])
+
+
+def add_kernel(a, b, out):
+    out[...] = a[...] + b[...].astype(F32)
 
 
 def local(
@@ -340,6 +338,7 @@
     rim = shifted(jnp.concatenate([x_input[half - rims :], s_rim], axis=1), ("ctx", "sub"), 1)
     raw = step_raw.T
     got_raw = swapped(raw, "sub")
+    rim, got_raw = after(rim, got_raw)
     mixed = (x_input, rim, mix_weight, bias, s_input, rim, s_weight, s_bias)
 
     def mix_specs(part, other):
@@ -401,8 +400,13 @@
     ready = []
     for part in range(parts):
         x_cat, bc, state, decay, arriving = made[part]
+        if ready:
+            arriving, gate = after(arriving, ready[-1][0])
+            ready[-1] = (gate, *ready[-1][1:])
         for _ in range(ctx_size // 2 - 1):
-            arriving = onward((state.astype(F32) + decay[:1] * arriving.astype(F32)).astype(BF16))
+            leaving = (state.astype(F32) + decay[:1] * arriving.astype(F32)).astype(BF16)
+            leaving, x_cat = after(leaving, x_cat)
+            arriving = onward(leaving)
         gate_at = lambda i, m, d, part=part: (lax.rem(i, splits), m[0] * parts + part)
         got_at = lambda i, m, d, part=part: (lax.rem(i, splits), part)
         gated, carry_gate = call(
@@ -443,57 +447,58 @@
         )
 
     gated, carry_gate, bc, arriving = ready[-1]
+    if hiddens:
+        arriving, hiddens[-1] = after(arriving, hiddens[-1])
     squares = []
     if not whole_groups:
         total = gated + jnp.dot(bc[:, state_width:], arriving, preferred_element_type=F32) * carry_gate
         mine = jnp.sum(total * total, axis=1, keepdims=True)
         squares = [mine + swapped(mine, "sub")]
-    operands = [*hiddens, gated, carry_gate, bc, *squares]
     out_cols = features // tp_size
     mm_cols = min(512, out_cols)
     pair = tp_size == 2
     near_blocks = out_cols // mm_cols
+    row_specs = [pl.BlockSpec((half, mm_cols), lambda i, m: (0, i))] * 2
+
+    def product(first, blocks, body, name, operands, specs, outs, out_shapes):
+        cols = blocks * mm_cols
+        return call(
+            body, name, (blocks,),
+            specs + [pl.BlockSpec((width, mm_cols), lambda i, m: (0, first(m) + i))],
+            outs + row_specs,
+            out_shapes + [shape_of((half, cols), BF16), shape_of((half, cols), F32)],
+            flops=2 * count * width * cols, moved=2 * width * cols, prefetch=1,
+        )(meta, *operands, out_weight)
+
+    far_first = (lambda m: (1 - m[2]) * near_blocks) if pair else (lambda m: 0)
     far_blocks = near_blocks if pair else features // mm_cols
-    far_at = (lambda i, m: (1 - m[2]) * near_blocks + i) if pair else (lambda i, m: i)
-    far_cols = far_blocks * mm_cols
-    far, kept_rows = [], []
-    for split in range(splits):
-        there = lambda i, m, split=split: ((1 - m[0]) * splits + split, 0)
-        here = lambda i, m, split=split: (m[0] * splits + split, 0)
-        specs = [pl.BlockSpec((CHUNK, v.shape[1]), at) for at in (there, here) for v in operands]
-        specs += [
-            fixed(state_width, part_width), gain_at(parts - 1),
-            pl.BlockSpec((width, mm_cols), lambda i, m: (0, far_at(i, m))),
-        ]
-        hidden, send, keep = call(
-            functools.partial(project_kernel, ready=len(hiddens), squared=len(squares), divisor=divisor),
-            "project", (far_blocks,), specs,
-            [
-                fixed(2 * CHUNK, width),
-                pl.BlockSpec((CHUNK, mm_cols), lambda i, m: (0, i)),
-                pl.BlockSpec((CHUNK, mm_cols), lambda i, m: (0, i)),
-            ],
-            [
-                shape_of((2 * CHUNK, width), BF16), shape_of((CHUNK, far_cols), BF16),
-                shape_of((CHUNK, far_cols), F32),
-            ],
-            flops=4 * CHUNK * width * far_cols, moved=2 * width * far_cols, prefetch=1,
-        )(meta, *operands, *operands, arriving, gain, out_weight)
+    lead = max(far_blocks // 2, 1)
+    operands = [*hiddens, gated, carry_gate, bc, arriving, gain, *squares]
+    specs = [fixed(*v.shape) for v in operands]
+    specs[len(hiddens) + 4] = gain_at(parts - 1)
+    hidden, send, keep = product(
+        far_first, lead, functools.partial(project_kernel, ready=len(hiddens), squared=len(squares), divisor=divisor),
+        "project", operands, specs, [fixed(count, width)], [shape_of((count, width), BF16)],
+    )
+    far = []
+    rest = [(lambda m: far_first(m) + lead, far_blocks - lead)] if far_blocks > lead else []
+    if pair:
+        rest.append((lambda m: m[2] * near_blocks, near_blocks))
+    for first, blocks in rest:
         summed = (keep + swapped(send, "sub").astype(F32)).astype(BF16)
+        hidden, summed = after(hidden, summed)
         far.append(swapped(summed, "tp") if pair else summed)
-        kept_rows.append(hidden)
+        send, keep = product(first, blocks, multiply, "product", [hidden], [fixed(count, width)], [], [])
     if not pair:
-        return lax.psum_scatter(jnp.concatenate(far), "tp", scatter_dimension=1, tiled=True)
-    send, keep = call(
-        product_kernel, "product", (near_blocks,),
-        [fixed(2 * CHUNK, width)] * splits
-        + [pl.BlockSpec((width, mm_cols), lambda i, m: (0, m[2] * near_blocks + i))],
-        [pl.BlockSpec((half, mm_cols), lambda i, m: (0, i)), pl.BlockSpec((half, mm_cols), lambda i, m: (0, i))],
-        [shape_of((half, out_cols), BF16), shape_of((half, out_cols), F32)],
-        flops=2 * count * width * out_cols, moved=2 * width * out_cols, prefetch=1,
-    )(meta, *kept_rows, out_weight)
-    near = keep + swapped(send, "sub").astype(F32)
-    return (near + jnp.concatenate(far).astype(F32)).astype(BF16)
+        far.append((keep + swapped(send, "sub").astype(F32)).astype(BF16))
+        return lax.psum_scatter(jnp.concatenate(far, axis=1), "tp", scatter_dimension=1, tiled=True)
+    lead_cols = far[0].shape[1]
+    early = call(
+        add_kernel, "add", (1,), [fixed(half, lead_cols)] * 2, fixed(half, lead_cols),
+        shape_of((half, lead_cols), F32), flops=1 << 38, moved=10 * half * lead_cols, prefetch=0,
+    )(keep, far[0])
+    late = [keep[:, lead_cols:] + v.astype(F32) for v in far[1:]]
+    return (jnp.concatenate([early, *late], axis=1) + swapped(send, "sub").astype(F32)).astype(BF16)
 
 
 def solution(mesh):

time: 129 us -> 114 us (0.88)
  waiting for transfers between devices: 32.9 us -> 10.1 us
  other arithmetic: 3.4 us -> 7.98 us
    ppermute x9, waiting for transfers between devices: 25 us -> 9.67 us  [swapped(): lax.ppermute(shard, axis, [(i, i ^ 1) for i in range(lax.axis_size(axis))])]
    ppermute x4, waiting for transfers between devices: 7.86 us -> 0.44 us  [onward(): lax.ppermute(shard, 'ctx', [(i, (i + 1) % ctx_size) for i in range(ctx_si...]
    convert_element_type x2, other arithmetic: 0.21 us -> 3.52 us  [local(): summed = (keep + swapped(send, 'sub').astype(F32)).astype(BF16)]
    unnamed x24 -> x26, local copies, waits for them, and re-layouts: 3.73 us -> 4.77 us
    pallas_call x3 -> x4, Pallas kernels: 26.5 us -> 26.9 us  [the longest x3 24.3 us: product(): call(body, name, (blocks,), specs + [pl.BlockSpec((width, mm_cols), lambd...]
  transfers between devices with their start and end apart: 14 -> 14, of which waited for: 5 -> 5; matrix products, arithmetic and copies ran while one was open for 6% -> 9% of each run, Pallas kernels for 43% -> 44%
where the time goes in v1:
time: 114 us; the launch traced here: 112 us
  Pallas kernels  68 us (60%)
  starting transfers between devices  13.7 us (12%)
  local copies, waits for them, and re-layouts  12.5 us (11%)
  waiting for transfers between devices  10.1 us (9%)
  other arithmetic  7.98 us (7%)
    pallas_call x3, Pallas kernels, product(): call(body, name, (blocks,), specs + [pl.BlockSpec((width, mm_cols), lambd...  24.3 us
    pallas_call x2, Pallas kernels, local(): call(functools.partial(intra_kernel, head_width=head_width, first_head=pa...  15.1 us
    pallas_call x2, Pallas kernels, local(): call(functools.partial(state_kernel, taps=taps, heads=heads, head_width=h...  10.3 us
    ppermute x9, waiting for transfers between devices, swapped(): lax.ppermute(shard, axis, [(i, i ^ 1) for i in range(lax.axis_size(axis))])  9.67 us
    pallas_call x2, Pallas kernels, local(): call(functools.partial(conv_kernel, taps=taps), 'conv', (1,), mix_specs(p...  7.26 us
    ppermute x9, starting transfers between devices, swapped(): lax.ppermute(shard, axis, [(i, i ^ 1) for i in range(lax.axis_size(axis))])  6.48 us
    pallas_call x1, Pallas kernels, local(): call(functools.partial(norm_kernel, divisor=divisor), 'norm', (chunks,),...  5.48 us
    ppermute x4, starting transfers between devices, onward(): lax.ppermute(shard, 'ctx', [(i, (i + 1) % ctx_size) for i in range(ctx_si...  4.82 us
  transfers between devices with their start and end apart: 14, of which 5 were waited for; matrix products, arithmetic and copies ran while one was open for 9% of the time, Pallas kernels for 44%

profile of v1, /device:TPU:0, one launch (start us, length us, event | category | flops | bytes accessed | tf_op | source)
XLA Modules:
  0.0 112.4 jit_solution(10355615287205330803)
XLA Ops:
  0.0 0.8 slice.16
  0.8 0.9 slice.15
  1.8 2.4 %collective-permute-start = (bf16[16,5120]{1,0:T(8,128)(2,1)S(1)}, bf16[16,5120]{1,0:T(8,128)(2,1)S(1)}, u32[]{:S(2)}, u32[]{:S(2)}) collective-permute-start(bf16[16,5120]{1,0:T(8,128)(2,1)S(1)} %pad_maximum_fusion), channel_id=1, source_target_pairs={{0,1},{1,4},{4,5},{5,8},{8,9},{9,12},{12,13},{2,3},{3,6},{6,7},{7,... | collective-permute-start | bytes 491528 | tf_op jit(solution)/shard_map/ppermute | solution.py:24
  4.1 2.7 %collective-permute-start.1 = (f32[64,256]{1,0:T(8,128)}, f32[64,256]{1,0:T(8,128)S(1)}, u32[]{:S(2)}, u32[]{:S(2)}) collective-permute-start(f32[64,256]{1,0:T(8,128)} %bitcast.26), channel_id=1, source_target_pairs={{0,1},{1,0},{2,3},{3,2},{4,5},{5,4},{6,7},{7,6},{8,9},{9,8},{10,11... | collective-permute-start | bytes 196616 | tf_op jit(solution)/shard_map/ppermute | solution.py:28
  6.9 2.2 %reshape.26.s = bf16[256,1024]{1,0:T(8,128)(2,1)} reshape(bf16[256,4,2,128]{3,2,1,0:T(2,128)(2,1)} %param.15) | data formatting | bytes 1048576 | tf_op jit(solution)/shard_map/reshape | solution.py:332
  9.1 1.5 %reshape.27.sw = bf16[4,1024]{1,0:T(4,128)(2,1)} reshape(bf16[4,4,2,128]{3,2,1,0:T(2,128)(2,1)} %param.18) | data formatting | bytes 16384 | tf_op jit(solution)/shard_map/reshape | solution.py:333
  11.8 3.6 %conv.3 = bf16[256,1280]{1,0:T(8,128)(2,1)} custom-call(s32[3]{0:T(128)} %pad_add_fusion.meta, s32[8]{0:T(128)} %docs.13, bf16[256,4096]{1,0:T(8,128)(2,1)} %x.7, bf16[16,5120]{1,0:T(8,128)(2,1)} %copy-done.1, bf16[4,4096]{1,0:T(4,128)(2,1)} %w.9, f32[1,4096]{1,0:T(1,128)} %bitcast.11, bf16[256,1024]{1,0:T(8,128)(2,1)} %reshape.26.s, ...), custom_call_target="tpu_custom_call" | custom-call | flops 536870912 | bytes 1048576 | tf_op jit(solution)/shard_map/conv/pallas_call | solution.py:356
  16.1 3.6 %conv.2 = bf16[256,1280]{1,0:T(8,128)(2,1)} custom-call(s32[3]{0:T(128)} %pad_add_fusion.meta, s32[8]{0:T(128)} %docs.13, bf16[256,4096]{1,0:T(8,128)(2,1)} %x.7, bf16[16,5120]{1,0:T(8,128)(2,1)} %copy-done.1, bf16[4,4096]{1,0:T(4,128)(2,1)} %w.9, f32[1,4096]{1,0:T(1,128)} %bitcast.12, bf16[256,1024]{1,0:T(8,128)(2,1)} %reshape.26.s, ...), custom_call_target="tpu_custom_call" | custom-call | flops 536870912 | bytes 1048576 | tf_op jit(solution)/shard_map/conv/pallas_call | solution.py:356
  20.5 2.9 %decay.1 = (f32[512,32]{1,0:T(8,128)}, f32[32,512]{1,0:T(8,128)}, bf16[512,64]{1,0:T(8,128)(2,1)}, bf16[8,96]{1,0:T(8,128)(2,1)}) custom-call(s32[3]{0:T(128)} %pad_add_fusion.meta, s32[8]{0:T(128)} %docs.13, f32[64,256]{1,0:T(8,128)} %bitcast.27, f32[64,256]{1,0:T(8,128)} %copy-done.12, f32[64,1]{1,0:T(8,128)} %copy.14.rate), custom_call_target="tpu_custom_call" | custom-call | flops 67108864 | bytes 262144 | tf_op jit(solution)/shard_map/decay/pallas_call | solution.py:363
  23.4 5.1 %state.3 = (bf16[512,1024]{1,0:T(8,128)(2,1)}, bf16[512,256]{1,0:T(8,128)(2,1)}, bf16[128,1024]{1,0:T(8,128)(2,1)}, f32[8,1024]{1,0:T(8,128)}) custom-call(s32[3]{0:T(128)} %pad_add_fusion.meta, s32[8]{0:T(128)} %docs.13, bf16[256,4096]{1,0:T(8,128)(2,1)} %x.7, bf16[16,5120]{1,0:T(8,128)(2,1)} %copy-done.1, bf16[4,4096]{1,0:T(4,128)(2,1)} %w.9, ...), custom_call_target="tpu_custom_call" | custom-call | flops 536870912 | bytes 3145728 | tf_op jit(solution)/shard_map/state/pallas_call | solution.py:379
  28.6 1.6 %collective-permute-start.5 = (bf16[128,1024]{1,0:T(8,128)(2,1)}, bf16[128,1024]{1,0:T(8,128)(2,1)S(1)}, u32[]{:S(2)}, u32[]{:S(2)}) collective-permute-start(bf16[128,1024]{1,0:T(8,128)(2,1)} %get-tuple-element.48), channel_id=1, source_target_pairs={{0,4},{4,8},{8,12},{12,0},{1,5},{5,9},{9,13},{13,1},{2,6},{6,10},{... | collective-permute-start | bytes 786440 | tf_op jit(solution)/shard_map/ppermute | solution.py:375
  30.9 0.8 copy-done.4
  31.7 5.2 %state.2 = (bf16[512,1024]{1,0:T(8,128)(2,1)}, bf16[512,256]{1,0:T(8,128)(2,1)}, bf16[128,1024]{1,0:T(8,128)(2,1)}, f32[8,1024]{1,0:T(8,128)}) custom-call(s32[3]{0:T(128)} %pad_add_fusion.meta, s32[8]{0:T(128)} %docs.13, bf16[256,4096]{1,0:T(8,128)(2,1)} %x.7, bf16[16,5120]{1,0:T(8,128)(2,1)} %copy-done.1, bf16[4,4096]{1,0:T(4,128)(2,1)} %w.9, ...), custom_call_target="tpu_custom_call" | custom-call | flops 536870912 | bytes 3145728 | tf_op jit(solution)/shard_map/state/pallas_call | solution.py:379
  37.7 1.6 %collective-permute-start.3 = (bf16[128,1024]{1,0:T(8,128)(2,1)}, bf16[128,1024]{1,0:T(8,128)(2,1)S(1)}, u32[]{:S(2)}, u32[]{:S(2)}) collective-permute-start(bf16[128,1024]{1,0:T(8,128)(2,1)} %get-tuple-element.46), channel_id=1, source_target_pairs={{0,4},{4,8},{8,12},{12,0},{1,5},{5,9},{9,13},{13,1},{2,6},{6,10},{... | collective-permute-start | bytes 786440 | tf_op jit(solution)/shard_map/ppermute | solution.py:375
  39.8 1.0 copy-done.2
  40.8 7.6 %intra.2 = (f32[512,1024]{1,0:T(8,128)}, f32[512,1024]{1,0:T(8,128)}) custom-call(s32[3]{0:T(128)} %pad_add_fusion.meta, s32[8]{0:T(128)} %docs.13, bf16[512,1024]{1,0:T(8,128)(2,1)} %get-tuple-element.51.x, bf16[512,256]{1,0:T(8,128)(2,1)} %get-tuple-element.52.bc, f32[512,32]{1,0:T(8,128)} %get-tuple-element.53.cum, f32[32,512]{1,0:T(8,128)} %get-tuple-element.54.dlt, ...), custom_call_target="tpu_custom_call" | custom-call | flops 671088640 | bytes 7340032 | tf_op jit(solution)/shard_map/intra/pallas_call | solution.py:412
  48.9 1.3 %collective-permute-start.7 = (bf16[128,1024]{1,0:T(8,128)(2,1)S(1)}, bf16[128,1024]{1,0:T(8,128)(2,1)S(1)}, u32[]{:S(2)}, u32[]{:S(2)}) collective-permute-start(bf16[128,1024]{1,0:T(8,128)(2,1)S(1)} %add_convert_fusion.2), channel_id=1, source_target_pairs={{0,4},{4,8},{8,12},{12,0},{1,5},{5,9},{9,13},{13,1},{2,6},{6,10},{... | collective-permute-start | bytes 786440 | tf_op jit(solution)/shard_map/ppermute | solution.py:375
  50.2 7.5 %intra.3 = (f32[512,1024]{1,0:T(8,128)}, f32[512,1024]{1,0:T(8,128)}) custom-call(s32[3]{0:T(128)} %pad_add_fusion.meta, s32[8]{0:T(128)} %docs.13, bf16[512,1024]{1,0:T(8,128)(2,1)} %get-tuple-element.63.x, bf16[512,256]{1,0:T(8,128)(2,1)} %get-tuple-element.64.bc.refs_3_, f32[512,32]{1,0:T(8,128)} %get-tuple-element.53.cum, ...), custom_call_target="tpu_custom_call" | custom-call | flops 671088640 | bytes 7340032 | tf_op jit(solution)/shard_map/intra/pallas_call | solution.py:412
  58.4 5.5 %norm.1.refs_0_ = bf16[512,1024]{1,0:T(8,128)(2,1)} custom-call(s32[3]{0:T(128)} %pad_add_fusion.meta, f32[512,1024]{1,0:T(8,128)} %get-tuple-element.59.a, f32[512,1024]{1,0:T(8,128)} %get-tuple-element.60.f, bf16[512,256]{1,0:T(8,128)(2,1)} %get-tuple-element.52.bc, bf16[128,1024]{1,0:T(8,128)(2,1)} %copy-done.8, f32[1,4096]{1,0:T(1,128)} %bitcast.19), custom_call_target="tpu_custom_call" | custom-call | flops 134217728 | bytes 5242880 | tf_op jit(solution)/shard_map/norm/pallas_call | solution.py:441
  64.6 8.7 %project.1 = (bf16[512,2048]{1,0:T(8,128)(2,1)}, bf16[256,1024]{1,0:T(8,128)(2,1)}, f32[256,1024]{1,0:T(8,128)}) custom-call(s32[3]{0:T(128)} %pad_add_fusion.meta, bf16[512,1024]{1,0:T(8,128)(2,1)} %norm.1.refs_0_, f32[512,1024]{1,0:T(8,128)} %get-tuple-element.65.refs_1_, f32[512,1024]{1,0:T(8,128)} %get-tuple-element.66.refs_2_, ...), custom_call_target="tpu_custom_call" | custom-call | flops 2147483648 | bytes 4194304 | tf_op jit(solution)/shard_map/project/pallas_call | solution.py:465
  73.2 2.1 %collective-permute-done.9 = bf16[256,1024]{1,0:T(8,128)(2,1)S(1)} collective-permute-done((bf16[256,1024]{1,0:T(8,128)(2,1)}, bf16[256,1024]{1,0:T(8,128)(2,1)S(1)}, u32[]{:S(2)}, u32[]{:S(2)}) %collective-permute-start.9) | collective-permute-done | bytes 524320 | tf_op jit(solution)/shard_map/ppermute | solution.py:28
  75.4 1.4 %add_convert_fusion.1 = bf16[256,1024]{1,0:T(8,128)(2,1)S(1)} fusion(f32[256,1024]{1,0:T(8,128)} %get-tuple-element.69, bf16[256,1024]{1,0:T(8,128)(2,1)S(1)} %collective-permute-done.9), kind=kLoop, calls=%fused_computation.4 | loop fusion | flops 786432 | bytes 2097152 | tf_op jit(solution)/shard_map/convert_element_type | solution.py:488
  76.7 6.2 %product.2 = (bf16[256,1024]{1,0:T(8,128)(2,1)}, f32[256,1024]{1,0:T(8,128)}) custom-call(s32[3]{0:T(128)} %pad_add_fusion.meta, bf16[512,2048]{1,0:T(8,128)(2,1)} %get-tuple-element.74.hidden, bf16[2048,4096]{1,0:T(8,128)(2,1)} %w.11), custom_call_target="tpu_custom_call" | custom-call | flops 2147483648 | bytes 4194304 | tf_op jit(solution)/shard_map/product/pallas_call | solution.py:465
  83.1 1.5 %collective-permute-start.11 = (bf16[256,1024]{1,0:T(8,128)(2,1)S(1)}, bf16[256,1024]{1,0:T(8,128)(2,1)S(1)}, u32[]{:S(2)}, u32[]{:S(2)}) collective-permute-start(bf16[256,1024]{1,0:T(8,128)(2,1)S(1)} %add_convert_fusion.1), channel_id=1, source_target_pairs={{0,2},{2,0},{1,3},{3,1},{4,6},{6,4},{5,7},{7,5},{8,10},{10,8},{9,1... | collective-permute-start | bytes 1572872 | tf_op jit(solution)/shard_map/ppermute | solution.py:28
  85.1 2.2 %add_convert_fusion = bf16[256,1024]{1,0:T(8,128)(2,1)} fusion(f32[256,1024]{1,0:T(8,128)} %get-tuple-element.72, bf16[256,1024]{1,0:T(8,128)(2,1)S(1)} %collective-permute-done.10), kind=kLoop, calls=%fused_computation.3 | loop fusion | flops 786432 | bytes 2097152 | tf_op jit(solution)/shard_map/convert_element_type | solution.py:488
  87.2 1.5 %collective-permute-start.12 = (bf16[256,1024]{1,0:T(8,128)(2,1)}, bf16[256,1024]{1,0:T(8,128)(2,1)}, u32[]{:S(2)}, u32[]{:S(2)}) collective-permute-start(bf16[256,1024]{1,0:T(8,128)(2,1)} %add_convert_fusion), channel_id=1, source_target_pairs={{0,2},{2,0},{1,3},{3,1},{4,6},{6,4},{5,7},{7,5},{8,10},{10,8},{9,1... | collective-permute-start | bytes 1572872 | tf_op jit(solution)/shard_map/ppermute | solution.py:28
  88.7 9.4 %product.3 = (bf16[256,2048]{1,0:T(8,128)(2,1)}, f32[256,2048]{1,0:T(8,128)}) custom-call(s32[3]{0:T(128)} %pad_add_fusion.meta, bf16[512,2048]{1,0:T(8,128)(2,1)} %get-tuple-element.74.hidden, bf16[2048,4096]{1,0:T(8,128)(2,1)} %w.11), custom_call_target="tpu_custom_call" | custom-call | flops 4294967296 | bytes 8388608 | tf_op jit(solution)/shard_map/product/pallas_call | solution.py:465
  98.2 0.8 copy-done.11
  99.0 2.6 %add.41 = f32[256,1024]{1,0:T(8,128)} custom-call(f32[256,2048]{1,0:T(8,128)} %get-tuple-element.75.a, bf16[256,1024]{1,0:T(8,128)(2,1)} %copy-done.11), custom_call_target="tpu_custom_call" | custom-call | flops 274877906944 | bytes 2621440 | tf_op jit(solution)/shard_map/add/pallas_call | solution.py:496
  101.6 7.1 %collective-permute-done.12 = bf16[256,1024]{1,0:T(8,128)(2,1)} collective-permute-done((bf16[256,1024]{1,0:T(8,128)(2,1)}, bf16[256,1024]{1,0:T(8,128)(2,1)}, u32[]{:S(2)}, u32[]{:S(2)}) %collective-permute-start.12) | collective-permute-done | bytes 524320 | tf_op jit(solution)/shard_map/ppermute | solution.py:28
  108.6 1.2 %convert_add_fusion = f32[256,1024]{1,0:T(8,128)S(1)} fusion(bf16[256,1024]{1,0:T(8,128)(2,1)} %collective-permute-done.12, f32[256,2048]{1,0:T(8,128)S(1)} %copy-done.5), kind=kLoop, calls=%fused_computation.2 | loop fusion | flops 524288 | bytes 2621440 | tf_op jit(solution)/shard_map/add | solution.py:500
  109.8 2.5 %fusion = bf16[256,2048]{1,0:T(8,128)(2,1)} fusion(f32[256,1024]{1,0:T(8,128)S(1)} %convert_add_fusion, f32[256,1024]{1,0:T(8,128)S(1)} %copy-done.3, bf16[256,2048]{1,0:T(8,128)(2,1)} %collective-permute-done.13), kind=kLoop, calls=%fused_computation.1 | loop fusion | flops 2097152 | bytes 4194304 | tf_op jit(solution)/shard_map/convert_element_type | solution.py:501
  (51 shorter events, 7.3 us)
Async XLA Ops:
  1.8 9.4 %collective-permute-start = (bf16[16,5120]{1,0:T(8,128)(2,1)S(1)}, bf16[16,5120]{1,0:T(8,128)(2,1)S(1)}, u32[]{:S(2)}, u32[]{:S(2)}) collective-permute-start(bf16[16,5120]{1,0:T(8,128)(2,1)S(1)} %pad_maximum_fusion), channel_id=1, source_target_pairs={{0,1},{1,4},{4,5},{5,8},{8,9},{9,12},{12,13},{2,3},{3,6},{6,7},{7,... | collective-permute-start | bytes 491528 | tf_op jit(solution)/shard_map/ppermute | solution.py:24
  4.1 7.0 %collective-permute-start.1 = (f32[64,256]{1,0:T(8,128)}, f32[64,256]{1,0:T(8,128)S(1)}, u32[]{:S(2)}, u32[]{:S(2)}) collective-permute-start(f32[64,256]{1,0:T(8,128)} %bitcast.26), channel_id=1, source_target_pairs={{0,1},{1,0},{2,3},{3,2},{4,5},{5,4},{6,7},{7,6},{8,9},{9,8},{10,11... | collective-permute-start | bytes 196616 | tf_op jit(solution)/shard_map/ppermute | solution.py:28
  9.1 6.4 %copy-start = (bf16[256,4096]{1,0:T(8,128)(2,1)S(1)}, bf16[256,4096]{1,0:T(8,128)(2,1)}, u32[]{:S(2)}) copy-start(bf16[256,4096]{1,0:T(8,128)(2,1)} %gate_own.3) | copy-start | bytes 6291460
  11.1 9.4 %copy-start.12 = (f32[64,256]{1,0:T(8,128)}, f32[64,256]{1,0:T(8,128)S(1)}, u32[]{:S(2)}) copy-start(f32[64,256]{1,0:T(8,128)S(1)} %collective-permute-done.1.got_raw) | copy-start | bytes 196612
  11.1 0.7 copy-start.1
  15.4 8.0 %collective-permute-start.4 = (bf16[256,1280]{1,0:T(8,128)(2,1)}, bf16[256,1280]{1,0:T(8,128)(2,1)}, u32[]{:S(2)}, u32[]{:S(2)}) collective-permute-start(bf16[256,1280]{1,0:T(8,128)(2,1)} %conv.3), channel_id=1, source_target_pairs={{0,1},{1,0},{2,3},{3,2},{4,5},{5,4},{6,7},{7,6},{8,9},{9,8},{10,11... | collective-permute-start | bytes 1966088 | tf_op jit(solution)/shard_map/ppermute | solution.py:28
  15.6 4.2 %copy-start.10 = (f32[64]{0:T(128)S(1)}, f32[64]{0:T(128)}, u32[]{:S(2)}) copy-start(f32[64]{0:T(128)} %param.21) | copy-start | bytes 772
  15.6 24.2 %collective-permute-start.6 = (bf16[256,2048]{1,0:T(8,128)(2,1)S(1)}, bf16[256,2048]{1,0:T(8,128)(2,1)S(1)}, u32[]{:S(2)}, u32[]{:S(2)}) collective-permute-start(bf16[256,2048]{1,0:T(8,128)(2,1)S(1)} %constant_dynamic-slice_fusion), channel_id=1, source_target_pairs={{0,1},{1,0},{2,3},{3,2},{4,5},{5,4},{6,7},{7,6},{8,9},{9,8},{10,11... | collective-permute-start | bytes 3145736 | tf_op jit(solution)/shard_map/ppermute | solution.py:28
  19.8 11.1 %collective-permute-start.2 = (bf16[256,1280]{1,0:T(8,128)(2,1)}, bf16[256,1280]{1,0:T(8,128)(2,1)S(1)}, u32[]{:S(2)}, u32[]{:S(2)}) collective-permute-start(bf16[256,1280]{1,0:T(8,128)(2,1)} %conv.2), channel_id=1, source_target_pairs={{0,1},{1,0},{2,3},{3,2},{4,5},{5,4},{6,7},{7,6},{8,9},{9,8},{10,11... | collective-permute-start | bytes 1966088 | tf_op jit(solution)/shard_map/ppermute | solution.py:28
  28.6 10.7 %copy-start.9 = (bf16[128,1024]{1,0:T(8,128)(2,1)S(1)}, bf16[128,1024]{1,0:T(8,128)(2,1)}, u32[]{:S(2)}) copy-start(bf16[128,1024]{1,0:T(8,128)(2,1)} %get-tuple-element.48) | copy-start | bytes 786436
  28.6 10.7 %collective-permute-start.5 = (bf16[128,1024]{1,0:T(8,128)(2,1)}, bf16[128,1024]{1,0:T(8,128)(2,1)S(1)}, u32[]{:S(2)}, u32[]{:S(2)}) collective-permute-start(bf16[128,1024]{1,0:T(8,128)(2,1)} %get-tuple-element.48), channel_id=1, source_target_pairs={{0,4},{4,8},{8,12},{12,0},{1,5},{5,9},{9,13},{13,1},{2,6},{6,10},{... | collective-permute-start | bytes 786440 | tf_op jit(solution)/shard_map/ppermute | solution.py:375
  30.9 0.8 copy-start.4
  37.7 11.2 %collective-permute-start.3 = (bf16[128,1024]{1,0:T(8,128)(2,1)}, bf16[128,1024]{1,0:T(8,128)(2,1)S(1)}, u32[]{:S(2)}, u32[]{:S(2)}) collective-permute-start(bf16[128,1024]{1,0:T(8,128)(2,1)} %get-tuple-element.46), channel_id=1, source_target_pairs={{0,4},{4,8},{8,12},{12,0},{1,5},{5,9},{9,13},{13,1},{2,6},{6,10},{... | collective-permute-start | bytes 786440 | tf_op jit(solution)/shard_map/ppermute | solution.py:375
  39.4 18.3 %collective-permute-start.8 = (bf16[128,1024]{1,0:T(8,128)(2,1)S(1)}, bf16[128,1024]{1,0:T(8,128)(2,1)S(1)}, u32[]{:S(2)}, u32[]{:S(2)}) collective-permute-start(bf16[128,1024]{1,0:T(8,128)(2,1)S(1)} %add_convert_fusion.3), channel_id=1, source_target_pairs={{0,4},{4,8},{8,12},{12,0},{1,5},{5,9},{9,13},{13,1},{2,6},{6,10},{... | collective-permute-start | bytes 786440 | tf_op jit(solution)/shard_map/ppermute | solution.py:375
  39.8 1.0 copy-start.2
  40.8 8.0 %copy-start.7 = (bf16[128,1024]{1,0:T(8,128)(2,1)S(1)}, bf16[128,1024]{1,0:T(8,128)(2,1)}, u32[]{:S(2)}) copy-start(bf16[128,1024]{1,0:T(8,128)(2,1)} %get-tuple-element.46) | copy-start | bytes 786436
  48.9 14.9 %collective-permute-start.7 = (bf16[128,1024]{1,0:T(8,128)(2,1)S(1)}, bf16[128,1024]{1,0:T(8,128)(2,1)S(1)}, u32[]{:S(2)}, u32[]{:S(2)}) collective-permute-start(bf16[128,1024]{1,0:T(8,128)(2,1)S(1)} %add_convert_fusion.2), channel_id=1, source_target_pairs={{0,4},{4,8},{8,12},{12,0},{1,5},{5,9},{9,13},{13,1},{2,6},{6,10},{... | collective-permute-start | bytes 786440 | tf_op jit(solution)/shard_map/ppermute | solution.py:375
  57.6 0.7 copy-start.8
  63.8 0.7 copy-start.6
  73.2 2.1 %collective-permute-start.9 = (bf16[256,1024]{1,0:T(8,128)(2,1)}, bf16[256,1024]{1,0:T(8,128)(2,1)S(1)}, u32[]{:S(2)}, u32[]{:S(2)}) collective-permute-start(bf16[256,1024]{1,0:T(8,128)(2,1)} %get-tuple-element.70), channel_id=1, source_target_pairs={{0,1},{1,0},{2,3},{3,2},{4,5},{5,4},{6,7},{7,6},{8,9},{9,8},{10,11... | collective-permute-start | bytes 1572872 | tf_op jit(solution)/shard_map/ppermute | solution.py:28
  83.0 2.1 %collective-permute-start.10 = (bf16[256,1024]{1,0:T(8,128)(2,1)}, bf16[256,1024]{1,0:T(8,128)(2,1)S(1)}, u32[]{:S(2)}, u32[]{:S(2)}) collective-permute-start(bf16[256,1024]{1,0:T(8,128)(2,1)} %get-tuple-element.73), channel_id=1, source_target_pairs={{0,1},{1,0},{2,3},{3,2},{4,5},{5,4},{6,7},{7,6},{8,9},{9,8},{10,11... | collective-permute-start | bytes 1572872 | tf_op jit(solution)/shard_map/ppermute | solution.py:28
  83.1 15.1 %collective-permute-start.11 = (bf16[256,1024]{1,0:T(8,128)(2,1)S(1)}, bf16[256,1024]{1,0:T(8,128)(2,1)S(1)}, u32[]{:S(2)}, u32[]{:S(2)}) collective-permute-start(bf16[256,1024]{1,0:T(8,128)(2,1)S(1)} %add_convert_fusion.1), channel_id=1, source_target_pairs={{0,2},{2,0},{1,3},{3,1},{4,6},{6,4},{5,7},{7,5},{8,10},{10,8},{9,1... | collective-permute-start | bytes 1572872 | tf_op jit(solution)/shard_map/ppermute | solution.py:28
  87.2 21.4 %collective-permute-start.12 = (bf16[256,1024]{1,0:T(8,128)(2,1)}, bf16[256,1024]{1,0:T(8,128)(2,1)}, u32[]{:S(2)}, u32[]{:S(2)}) collective-permute-start(bf16[256,1024]{1,0:T(8,128)(2,1)} %add_convert_fusion), channel_id=1, source_target_pairs={{0,2},{2,0},{1,3},{3,1},{4,6},{6,4},{5,7},{7,5},{8,10},{10,8},{9,1... | collective-permute-start | bytes 1572872 | tf_op jit(solution)/shard_map/ppermute | solution.py:28
  98.2 11.7 %collective-permute-start.13 = (bf16[256,2048]{1,0:T(8,128)(2,1)}, bf16[256,2048]{1,0:T(8,128)(2,1)}, u32[]{:S(2)}, u32[]{:S(2)}) collective-permute-start(bf16[256,2048]{1,0:T(8,128)(2,1)} %get-tuple-element.78), channel_id=1, source_target_pairs={{0,1},{1,0},{2,3},{3,2},{4,5},{5,4},{6,7},{7,6},{8,9},{9,8},{10,11... | collective-permute-start | bytes 3145736 | tf_op jit(solution)/shard_map/ppermute | solution.py:28
  98.2 0.8 copy-start.11
  99.0 9.6 %copy-start.5 = (f32[256,2048]{1,0:T(8,128)S(1)}, f32[256,2048]{1,0:T(8,128)}, u32[]{:S(2)}) copy-start(f32[256,2048]{1,0:T(8,128)} %get-tuple-element.75.a) | copy-start | bytes 6291460
  101.6 8.3 %copy-start.3 = (f32[256,1024]{1,0:T(8,128)S(1)}, f32[256,1024]{1,0:T(8,128)}, u32[]{:S(2)}) copy-start(f32[256,1024]{1,0:T(8,128)} %add.41) | copy-start | bytes 3145732

commit v2 on v1

--- a/solution.py
+++ b/solution.py
@@ -13,7 +13,7 @@
 EPSILON = 1e-05
 LOG2E = 1.4426950408889634
 CEILING = 126.0
-VMEM = 60 << 20
+VMEM = 32 << 20
 F32 = jnp.float32
 BF16 = jnp.bfloat16
 
@@ -92,11 +92,14 @@
         rim_hit = (rim_col == rim_row - back) & (rim_col >= start[:rims])
         shifts.append((jnp.where(hit, 1.0, 0.0).astype(BF16), jnp.where(rim_hit, 1.0, 0.0).astype(BF16)))
     for index, (x, rim, w, bias) in enumerate(pieces):
+        weights = w[...].astype(F32)
+        if index:
+            weights = jnp.concatenate([weights[:, 0, 0, :], weights[:, 0, 1, :]], axis=1)
         span = min(256, x.shape[1])
         for low in range(0, x.shape[1], span):
             at = slice(low, low + span)
             value = x[:, at]
-            weight = w[:, at].astype(F32)
+            weight = weights[:, at]
             summed = bias[:, at] + value.astype(F32) * weight[taps - 1 : taps]
             top = jnp.zeros((rims, span), F32)
             for back in range(1, taps):
@@ -132,7 +135,11 @@
     raw[:, got_at] = jnp.where(mine, got_raw[:heads], got_raw[heads:])
     value = raw[...]
     size = jnp.maximum(value, 0.0) + jnp.log(1.0 + jnp.exp(-jnp.abs(value)))
-    decay = (-LOG2E * jnp.exp(jnp.where(mine, rate[:heads], rate[heads:]))) * size
+    wide = (heads, 2 * heads)
+    own_head = lax.broadcasted_iota(jnp.int32, wide, 0) + meta[0] * heads
+    chosen = own_head == lax.broadcasted_iota(jnp.int32, wide, 1)
+    rates = jnp.sum(jnp.where(chosen, rate[...], 0.0), axis=1, keepdims=True)
+    decay = (-LOG2E * jnp.exp(rates)) * size
     row = lax.broadcasted_iota(jnp.int32, (count, count), 0)
     col = lax.broadcasted_iota(jnp.int32, (count, count), 1)
     above = jnp.where(row <= col, 1.0, 0.0).astype(BF16)
@@ -180,7 +187,7 @@
         tails = mm(tail[...], head_lanes(2, heads, head_width, span, first_lane + low))
         weighted = (x_out[:, at].astype(F32) * tails).astype(BF16)
         s_out[:, at] = mm(b, weighted).astype(BF16)
-        d_out[:, at] = mm(kept[...], head_lanes(3, heads, head_width, span, first_lane + low))
+        d_out[:, at] = mm(kept[...], head_lanes(3, heads, head_width, span, first_lane + low))[:1]
 
 
 def intra_kernel(
@@ -317,7 +324,7 @@
     shape_of = jax.ShapeDtypeStruct
 
     def call(body, name, grid, in_specs, out_specs, out_shape, scratch=(), flops=0, moved=0, prefetch=2):
-        return pl.pallas_call(
+        kernel = pl.pallas_call(
             body,
             grid_spec=pltpu.PrefetchScalarGridSpec(
                 num_scalar_prefetch=prefetch, grid=grid, in_specs=in_specs, out_specs=out_specs,
@@ -328,18 +335,26 @@
             cost_estimate=pl.CostEstimate(flops=flops, bytes_accessed=moved, transcendentals=0),
             name=name,
         )
+        return lambda *operands: kernel(
+            *(pltpu.with_memory_space_constraint(v, pltpu.HBM) if any(v is p for p in pinned) else v for v in operands)
+        )
 
     s_input = state_proj.reshape(half, groups * block)
-    s_weight = state_weight.reshape(taps, groups * block)
     s_bias = state_bias.reshape(1, groups * block)
     bias = mix_bias.reshape(1, channels)
+    skip = skip_gain.reshape(1, all_heads)
+    gain = norm_gain.reshape(1, channels)
+    rate = decay_log.reshape(1, all_heads)
+    pinned = [
+        meta, docs, x_input, gate_input, mix_weight, bias, state_weight, s_bias, skip, gain, rate, out_weight
+    ]
     rims = 16
     s_rim = state_proj[half - rims :].reshape(rims, groups * block)
     rim = shifted(jnp.concatenate([x_input[half - rims :], s_rim], axis=1), ("ctx", "sub"), 1)
     raw = step_raw.T
     got_raw = swapped(raw, "sub")
     rim, got_raw = after(rim, got_raw)
-    mixed = (x_input, rim, mix_weight, bias, s_input, rim, s_weight, s_bias)
+    mixed = (x_input, rim, mix_weight, bias, s_input, rim, state_weight, s_bias)
 
     def mix_specs(part, other):
         at = lambda m: (1 - m[0] if other else m[0]) * parts + part
@@ -349,6 +364,7 @@
         for size, places in ((part_width, (at, at, at, at)), (block, (s_at, rim_at, s_at, s_at))):
             for rows, place in zip((half, rims, taps, 1), places):
                 specs.append(pl.BlockSpec((rows, size), lambda i, m, d, place=place: (0, place(m))))
+        specs[6] = pl.BlockSpec((taps, 1, 2, state_width), lambda i, m, d: (0, s_at(m), 0, 0))
         return specs
 
     got = []
@@ -362,14 +378,14 @@
 
     cum, dlt, tail, kept = call(
         decay_kernel, "decay", (1,),
-        [fixed(all_heads, half), fixed(all_heads, half), fixed(all_heads, 1)],
+        [fixed(all_heads, half), fixed(all_heads, half), fixed(1, all_heads)],
         [fixed(count, heads), fixed(heads, count), fixed(count, 2 * heads), fixed(8, 3 * heads)],
         [
             shape_of((count, heads), F32), shape_of((heads, count), F32),
             shape_of((count, 2 * heads), BF16), shape_of((8, 3 * heads), BF16),
         ],
         [pltpu.VMEM((heads, count), F32)], flops=2 * count * count * 128, moved=16 * count * heads,
-    )(meta, docs, raw, got_raw, decay_log.reshape(all_heads, 1))
+    )(meta, docs, raw, got_raw, rate)
 
     def onward(shard):
         return lax.ppermute(shard, "ctx", [(i, (i + 1) % ctx_size) for i in range(ctx_size)])
@@ -384,11 +400,11 @@
             mix_specs(part, False)
             + [fixed(half, part_width + block), fixed(count, 2 * heads), fixed(8, 3 * heads)],
             [
-                fixed(count, part_width), fixed(count, block), fixed(state_width, part_width), fixed(8, part_width),
+                fixed(count, part_width), fixed(count, block), fixed(state_width, part_width), fixed(1, part_width),
             ],
             [
                 shape_of((count, part_width), BF16), shape_of((count, block), BF16),
-                shape_of((state_width, part_width), BF16), shape_of((8, part_width), F32),
+                shape_of((state_width, part_width), BF16), shape_of((1, part_width), F32),
             ],
             flops=4 * half * count * part_width, moved=6 * count * part_width,
         )(meta, docs, *mixed, got[part], tail, kept)
@@ -396,7 +412,6 @@
 
     got_gate = swapped(lax.dynamic_slice_in_dim(gate_input, (1 - sub) * width, width, 1), "sub")
     by_row = lambda n: pl.BlockSpec((CHUNK, n), lambda i, *m: (i, 0))
-    skip = skip_gain.reshape(1, all_heads)
     ready = []
     for part in range(parts):
         x_cat, bc, state, decay, arriving = made[part]
@@ -404,7 +419,7 @@
             arriving, gate = after(arriving, ready[-1][0])
             ready[-1] = (gate, *ready[-1][1:])
         for _ in range(ctx_size // 2 - 1):
-            leaving = (state.astype(F32) + decay[:1] * arriving.astype(F32)).astype(BF16)
+            leaving = (state.astype(F32) + decay * arriving.astype(F32)).astype(BF16)
             leaving, x_cat = after(leaving, x_cat)
             arriving = onward(leaving)
         gate_at = lambda i, m, d, part=part: (lax.rem(i, splits), m[0] * parts + part)
@@ -433,7 +448,6 @@
         ready.append((gated, carry_gate, bc, arriving))
 
     divisor = HEADS // GROUPS * head_width
-    gain = norm_gain.reshape(1, channels)
     gain_at = lambda part: pl.BlockSpec((1, part_width), lambda i, m: (0, m[0] * parts + part))
     hiddens = []
     for part, (gated, carry_gate, bc, arriving) in enumerate(ready[:-1]):

time: 114 us -> 93 us (0.82)
  Pallas kernels: 68 us -> 49.5 us
  local copies, waits for them, and re-layouts: 12.5 us -> 3.2 us
  waiting for transfers between devices: 10.1 us -> 19 us
  other arithmetic: 7.98 us -> 5.61 us
    pallas_call x12, Pallas kernels: 68 us -> 49.5 us  [call(): kernel(*(pltpu.with_memory_space_constraint(v, pltpu.HBM) if any((v is p...]
    ppermute x9, waiting for transfers between devices: 9.67 us -> 15.5 us  [swapped(): lax.ppermute(shard, axis, [(i, i ^ 1) for i in range(lax.axis_size(axis))])]
    unnamed x26 -> x4, local copies, waits for them, and re-layouts: 4.77 us -> 0.01 us
    ppermute x4, waiting for transfers between devices: 0.44 us -> 3.48 us  [onward(): lax.ppermute(shard, 'ctx', [(i, (i + 1) % ctx_size) for i in range(ctx_si...]
    convert_element_type x2, other arithmetic: 3.52 us -> 1.09 us  [local(): summed = (keep + swapped(send, 'sub').astype(F32)).astype(BF16)]
    reshape x2 -> x0, local copies, waits for them, and re-layouts: 2.16 us -> none  [the longest x1 1.45 us: local(): s_weight = state_weight.reshape(taps, groups * block)]
    slice x2 -> x0, local copies, waits for them, and re-layouts: 1.52 us -> none  [local(): decay[:1] * arriving.astype(F32)]
  transfers between devices with their start and end apart: 14 -> 14, of which waited for: 5 -> 5; matrix products, arithmetic and copies ran while one was open for 9% -> 5% of each run, Pallas kernels for 44% -> 39%
where the time goes in v2:
time: 93 us; the launch traced here: 92.3 us
  Pallas kernels  49.5 us (53%)
  waiting for transfers between devices  19 us (20%)
  starting transfers between devices  14.7 us (16%)
  other arithmetic  5.61 us (6%)
  local copies, waits for them, and re-layouts  3.2 us (3%)
    pallas_call x12, Pallas kernels, call(): kernel(*(pltpu.with_memory_space_constraint(v, pltpu.HBM) if any((v is p...  49.5 us
    ppermute x9, waiting for transfers between devices, swapped(): lax.ppermute(shard, axis, [(i, i ^ 1) for i in range(lax.axis_size(axis))])  15.5 us
    ppermute x9, starting transfers between devices, swapped(): lax.ppermute(shard, axis, [(i, i ^ 1) for i in range(lax.axis_size(axis))])  6.78 us
    ppermute x4, starting transfers between devices, onward(): lax.ppermute(shard, 'ctx', [(i, (i + 1) % ctx_size) for i in range(ctx_si...  5.57 us
    ppermute x4, waiting for transfers between devices, onward(): lax.ppermute(shard, 'ctx', [(i, (i + 1) % ctx_size) for i in range(ctx_si...  3.48 us
    convert_element_type x1, other arithmetic, local(): (jnp.concatenate([early, *late], axis=1) + swapped(send, 'sub').astype(F3...  2.5 us
    ppermute x1, starting transfers between devices, shifted(): return lax.ppermute(shard, axis, pairs)  2.37 us
  transfers between devices with their start and end apart: 14, of which 5 were waited for; matrix products, arithmetic and copies ran while one was open for 5% of the time, Pallas kernels for 39%

profile of v2, /device:TPU:0, one launch (start us, length us, event | category | flops | bytes accessed | tf_op | source)
XLA Modules:
  0.0 92.3 jit_solution(2044640479590876616)
XLA Ops:
  0.0 0.8 slice.10
  0.8 0.9 slice.9
  1.8 2.4 %collective-permute-start = (bf16[16,5120]{1,0:T(8,128)(2,1)S(1)}, bf16[16,5120]{1,0:T(8,128)(2,1)S(1)}, u32[]{:S(2)}, u32[]{:S(2)}) collective-permute-start(bf16[16,5120]{1,0:T(8,128)(2,1)S(1)} %pad_maximum_fusion), channel_id=1, source_target_pairs={{0,1},{1,4},{4,5},{5,8},{8,9},{9,12},{12,13},{2,3},{3,6},{6,7},{7,... | collective-permute-start | bytes 491528 | tf_op jit(solution)/shard_map/ppermute | solution.py:24
  4.1 2.7 %collective-permute-start.1 = (f32[64,256]{1,0:T(8,128)}, f32[64,256]{1,0:T(8,128)S(1)}, u32[]{:S(2)}, u32[]{:S(2)}) collective-permute-start(f32[64,256]{1,0:T(8,128)} %bitcast.13), channel_id=1, source_target_pairs={{0,1},{1,0},{2,3},{3,2},{4,5},{5,4},{6,7},{7,6},{8,9},{9,8},{10,11... | collective-permute-start | bytes 196616 | tf_op jit(solution)/shard_map/ppermute | solution.py:28
  6.9 1.4 %reshape.23.s = bf16[256,1024]{1,0:T(8,128)(2,1)S(1)} reshape(bf16[256,4,2,128]{3,2,1,0:T(2,128)(2,1)} %param.15) | data formatting | bytes 1048576 | tf_op jit(solution)/shard_map/reshape | solution.py:342
  8.3 0.7 pad_add_fusion.meta
  9.0 2.8 %conv.3 = bf16[256,1280]{1,0:T(8,128)(2,1)S(1)} custom-call(s32[3]{0:T(128)} %pad_add_fusion.meta, s32[8]{0:T(128)} %docs.13, bf16[256,4096]{1,0:T(8,128)(2,1)} %x.7, bf16[16,5120]{1,0:T(8,128)(2,1)S(1)} %collective-permute-done.x_rim.s_rim, bf16[4,4096]{1,0:T(4,128)(2,1)} %w.9, f32[1,4096]{1,0:T(1,128)} %bitcast.15, bf16[256,1024]{1,0:T(8,128)(2,1)S(1)} %reshape.23.s, ...), custom_call_target="tpu_custom_call" | custom-call | flops 536870912 | bytes 1048576 | tf_op jit(solution)/shard_map/conv/pallas_call | solution.py:338
  12.0 0.5 collective-permute-start.6
  12.5 2.8 %conv.2 = bf16[256,1280]{1,0:T(8,128)(2,1)S(1)} custom-call(s32[3]{0:T(128)} %pad_add_fusion.meta, s32[8]{0:T(128)} %docs.13, bf16[256,4096]{1,0:T(8,128)(2,1)} %x.7, bf16[16,5120]{1,0:T(8,128)(2,1)S(1)} %collective-permute-done.x_rim.s_rim, bf16[4,4096]{1,0:T(4,128)(2,1)} %w.9, f32[1,4096]{1,0:T(1,128)} %bitcast.16, bf16[256,1024]{1,0:T(8,128)(2,1)S(1)} %reshape.23.s, ...), custom_call_target="tpu_custom_call" | custom-call | flops 536870912 | bytes 1048576 | tf_op jit(solution)/shard_map/conv/pallas_call | solution.py:338
  15.4 2.1 %decay.1 = (f32[512,32]{1,0:T(8,128)S(1)}, f32[32,512]{1,0:T(8,128)S(1)}, bf16[512,64]{1,0:T(8,128)(2,1)S(1)}, bf16[8,96]{1,0:T(8,128)(2,1)S(1)}) custom-call(s32[3]{0:T(128)} %pad_add_fusion.meta, s32[8]{0:T(128)} %docs.13, f32[64,256]{1,0:T(8,128)S(1)} %bitcast.14, f32[64,256]{1,0:T(8,128)S(1)} %collective-permute-done.1.got_raw, f32[1,64]{1,0:T(1,128)} %bitcast.27), custom_call_target="tpu_custom_call" | custom-call | flops 67108864 | bytes 262144 | tf_op jit(solution)/shard_map/decay/pallas_call | solution.py:338
  17.5 4.1 %state.3 = (bf16[512,1024]{1,0:T(8,128)(2,1)S(1)}, bf16[512,256]{1,0:T(8,128)(2,1)S(1)}, bf16[128,1024]{1,0:T(8,128)(2,1)S(1)}, f32[1,1024]{1,0:T(1,128)S(1)}) custom-call(s32[3]{0:T(128)} %pad_add_fusion.meta, s32[8]{0:T(128)} %docs.13, bf16[256,4096]{1,0:T(8,128)(2,1)} %x.7, bf16[16,5120]{1,0:T(8,128)(2,1)S(1)} %collective-permute-done.x_rim.s_rim, ...), custom_call_target="tpu_custom_call" | custom-call | flops 536870912 | bytes 3145728 | tf_op jit(solution)/shard_map/state/pallas_call | solution.py:338
  21.5 2.4 %collective-permute-start.5 = (bf16[128,1024]{1,0:T(8,128)(2,1)S(1)}, bf16[128,1024]{1,0:T(8,128)(2,1)S(1)}, u32[]{:S(2)}, u32[]{:S(2)}) collective-permute-start(bf16[128,1024]{1,0:T(8,128)(2,1)S(1)} %get-tuple-element.48), channel_id=1, source_target_pairs={{0,4},{4,8},{8,12},{12,0},{1,5},{5,9},{9,13},{13,1},{2,6},{6,10},{... | collective-permute-start | bytes 786440 | tf_op jit(solution)/shard_map/ppermute | solution.py:391
  24.0 4.1 %state.2 = (bf16[512,1024]{1,0:T(8,128)(2,1)S(1)}, bf16[512,256]{1,0:T(8,128)(2,1)S(1)}, bf16[128,1024]{1,0:T(8,128)(2,1)S(1)}, f32[1,1024]{1,0:T(1,128)S(1)}) custom-call(s32[3]{0:T(128)} %pad_add_fusion.meta, s32[8]{0:T(128)} %docs.13, bf16[256,4096]{1,0:T(8,128)(2,1)} %x.7, bf16[16,5120]{1,0:T(8,128)(2,1)S(1)} %collective-permute-done.x_rim.s_rim, ...), custom_call_target="tpu_custom_call" | custom-call | flops 536870912 | bytes 3145728 | tf_op jit(solution)/shard_map/state/pallas_call | solution.py:338
  28.0 1.6 %collective-permute-start.3 = (bf16[128,1024]{1,0:T(8,128)(2,1)S(1)}, bf16[128,1024]{1,0:T(8,128)(2,1)S(1)}, u32[]{:S(2)}, u32[]{:S(2)}) collective-permute-start(bf16[128,1024]{1,0:T(8,128)(2,1)S(1)} %get-tuple-element.46), channel_id=1, source_target_pairs={{0,4},{4,8},{8,12},{12,0},{1,5},{5,9},{9,13},{13,1},{2,6},{6,10},{... | collective-permute-start | bytes 786440 | tf_op jit(solution)/shard_map/ppermute | solution.py:391
  29.7 3.5 %collective-permute-done.5 = bf16[128,1024]{1,0:T(8,128)(2,1)S(1)} collective-permute-done((bf16[128,1024]{1,0:T(8,128)(2,1)S(1)}, bf16[128,1024]{1,0:T(8,128)(2,1)S(1)}, u32[]{:S(2)}, u32[]{:S(2)}) %collective-permute-start.5) | collective-permute-done | bytes 262176 | tf_op jit(solution)/shard_map/ppermute | solution.py:391
  33.3 6.2 %intra.2 = (f32[512,1024]{1,0:T(8,128)S(1)}, f32[512,1024]{1,0:T(8,128)S(1)}) custom-call(s32[3]{0:T(128)} %pad_add_fusion.meta, s32[8]{0:T(128)} %docs.13, bf16[512,1024]{1,0:T(8,128)(2,1)S(1)} %get-tuple-element.51.x, bf16[512,256]{1,0:T(8,128)(2,1)S(1)} %get-tuple-element.52.bc, f32[512,32]{1,0:T(8,128)S(1)} %get-tuple-element.53.cum, ...), custom_call_target="tpu_custom_call" | custom-call | flops 671088640 | bytes 7340032 | tf_op jit(solution)/shard_map/intra/pallas_call | solution.py:338
  39.6 1.4 %collective-permute-start.7 = (bf16[128,1024]{1,0:T(8,128)(2,1)S(1)}, bf16[128,1024]{1,0:T(8,128)(2,1)S(1)}, u32[]{:S(2)}, u32[]{:S(2)}) collective-permute-start(bf16[128,1024]{1,0:T(8,128)(2,1)S(1)} %add_convert_fusion.2), channel_id=1, source_target_pairs={{0,4},{4,8},{8,12},{12,0},{1,5},{5,9},{9,13},{13,1},{2,6},{6,10},{... | collective-permute-start | bytes 786440 | tf_op jit(solution)/shard_map/ppermute | solution.py:391
  41.0 6.4 %intra.3 = (f32[512,1024]{1,0:T(8,128)S(1)}, f32[512,1024]{1,0:T(8,128)S(1)}) custom-call(s32[3]{0:T(128)} %pad_add_fusion.meta, s32[8]{0:T(128)} %docs.13, bf16[512,1024]{1,0:T(8,128)(2,1)S(1)} %get-tuple-element.63.x, bf16[512,256]{1,0:T(8,128)(2,1)S(1)} %get-tuple-element.64.bc.refs_3_, f32[512,32]{1,0:T(8,128)S(1)} %get-tuple-element.53.cum, ...), custom_call_target="tpu_custom_call" | custom-call | flops 671088640 | bytes 7340032 | tf_op jit(solution)/shard_map/intra/pallas_call | solution.py:338
  47.4 2.7 %norm.1.refs_0_ = bf16[512,1024]{1,0:T(8,128)(2,1)S(1)} custom-call(s32[3]{0:T(128)} %pad_add_fusion.meta, f32[512,1024]{1,0:T(8,128)S(1)} %get-tuple-element.59.a, f32[512,1024]{1,0:T(8,128)S(1)} %get-tuple-element.60.f, bf16[512,256]{1,0:T(8,128)(2,1)S(1)} %get-tuple-element.52.bc, bf16[128,1024]{1,0:T(8,128)(2,1)S(1)} %collective-permute-done.8.incoming, ...), custom_call_target="tpu_custom_call" | custom-call | flops 134217728 | bytes 5242880 | tf_op jit(solution)/shard_map/norm/pallas_call | solution.py:338
  50.2 5.6 %project.1 = (bf16[512,2048]{1,0:T(8,128)(2,1)S(1)}, bf16[256,1024]{1,0:T(8,128)(2,1)S(1)}, f32[256,1024]{1,0:T(8,128)S(1)}) custom-call(s32[3]{0:T(128)} %pad_add_fusion.meta, bf16[512,1024]{1,0:T(8,128)(2,1)S(1)} %norm.1.refs_0_, f32[512,1024]{1,0:T(8,128)S(1)} %get-tuple-element.65.refs_1_, f32[512,1024]{1,0:T(8,128)S(1)} %get-tuple-element.66.refs_2_, ...), custom_call_target="tpu_custom_call" | custom-call | flops 2147483648 | bytes 4194304 | tf_op jit(solution)/shard_map/project/pallas_call | solution.py:338
  55.9 1.9 %collective-permute-done.9 = bf16[256,1024]{1,0:T(8,128)(2,1)S(1)} collective-permute-done((bf16[256,1024]{1,0:T(8,128)(2,1)S(1)}, bf16[256,1024]{1,0:T(8,128)(2,1)S(1)}, u32[]{:S(2)}, u32[]{:S(2)}) %collective-permute-start.9) | collective-permute-done | bytes 524320 | tf_op jit(solution)/shard_map/ppermute | solution.py:28
  57.9 4.9 %product.2 = (bf16[256,1024]{1,0:T(8,128)(2,1)S(1)}, f32[256,1024]{1,0:T(8,128)S(1)}) custom-call(s32[3]{0:T(128)} %pad_add_fusion.meta, bf16[512,2048]{1,0:T(8,128)(2,1)S(1)} %get-tuple-element.74.hidden, bf16[2048,4096]{1,0:T(8,128)(2,1)} %w.11), custom_call_target="tpu_custom_call" | custom-call | flops 2147483648 | bytes 4194304 | tf_op jit(solution)/shard_map/product/pallas_call | solution.py:338
  62.8 0.2 collective-permute-start.10
  63.0 1.5 %collective-permute-start.11 = (bf16[256,1024]{1,0:T(8,128)(2,1)S(1)}, bf16[256,1024]{1,0:T(8,128)(2,1)S(1)}, u32[]{:S(2)}, u32[]{:S(2)}) collective-permute-start(bf16[256,1024]{1,0:T(8,128)(2,1)S(1)} %add_convert_fusion.1), channel_id=1, source_target_pairs={{0,2},{2,0},{1,3},{3,1},{4,6},{6,4},{5,7},{7,5},{8,10},{10,8},{9,1... | collective-permute-start | bytes 1572872 | tf_op jit(solution)/shard_map/ppermute | solution.py:28
  64.5 0.3 collective-permute-done.10
  64.8 0.9 %add_convert_fusion = bf16[256,1024]{1,0:T(8,128)(2,1)} fusion(f32[256,1024]{1,0:T(8,128)S(1)} %get-tuple-element.72, bf16[256,1024]{1,0:T(8,128)(2,1)S(1)} %collective-permute-done.10), kind=kLoop, calls=%fused_computation.3 | loop fusion | flops 786432 | bytes 2097152 | tf_op jit(solution)/shard_map/convert_element_type | solution.py:502
  65.7 1.5 %collective-permute-start.12 = (bf16[256,1024]{1,0:T(8,128)(2,1)}, bf16[256,1024]{1,0:T(8,128)(2,1)}, u32[]{:S(2)}, u32[]{:S(2)}) collective-permute-start(bf16[256,1024]{1,0:T(8,128)(2,1)} %add_convert_fusion), channel_id=1, source_target_pairs={{0,2},{2,0},{1,3},{3,1},{4,6},{6,4},{5,7},{7,5},{8,10},{10,8},{9,1... | collective-permute-start | bytes 1572872 | tf_op jit(solution)/shard_map/ppermute | solution.py:28
  67.2 7.9 %product.3 = (bf16[256,2048]{1,0:T(8,128)(2,1)}, f32[256,2048]{1,0:T(8,128)S(1)}) custom-call(s32[3]{0:T(128)} %pad_add_fusion.meta, bf16[512,2048]{1,0:T(8,128)(2,1)S(1)} %get-tuple-element.74.hidden, bf16[2048,4096]{1,0:T(8,128)(2,1)} %w.11), custom_call_target="tpu_custom_call" | custom-call | flops 4294967296 | bytes 8388608 | tf_op jit(solution)/shard_map/product/pallas_call | solution.py:338
  75.2 2.6 %collective-permute-done.11.b = bf16[256,1024]{1,0:T(8,128)(2,1)S(1)} collective-permute-done((bf16[256,1024]{1,0:T(8,128)(2,1)S(1)}, bf16[256,1024]{1,0:T(8,128)(2,1)S(1)}, u32[]{:S(2)}, u32[]{:S(2)}) %collective-permute-start.11) | collective-permute-done | bytes 524320 | tf_op jit(solution)/shard_map/ppermute | solution.py:28
  77.9 10.7 %collective-permute-done.12 = bf16[256,1024]{1,0:T(8,128)(2,1)} collective-permute-done((bf16[256,1024]{1,0:T(8,128)(2,1)}, bf16[256,1024]{1,0:T(8,128)(2,1)}, u32[]{:S(2)}, u32[]{:S(2)}) %collective-permute-start.12) | collective-permute-done | bytes 524320 | tf_op jit(solution)/shard_map/ppermute | solution.py:28
  88.6 1.2 %convert_add_fusion = f32[256,1024]{1,0:T(8,128)S(1)} fusion(bf16[256,1024]{1,0:T(8,128)(2,1)} %collective-permute-done.12, f32[256,2048]{1,0:T(8,128)S(1)} %get-tuple-element.75.a), kind=kLoop, calls=%fused_computation.2 | loop fusion | flops 524288 | bytes 2621440 | tf_op jit(solution)/shard_map/add | solution.py:514
  89.8 2.5 %fusion = bf16[256,2048]{1,0:T(8,128)(2,1)} fusion(f32[256,1024]{1,0:T(8,128)S(1)} %convert_add_fusion, f32[256,1024]{1,0:T(8,128)S(1)} %add.41, bf16[256,2048]{1,0:T(8,128)(2,1)} %collective-permute-done.13), kind=kLoop, calls=%fused_computation.1 | loop fusion | flops 2097152 | bytes 4194304 | tf_op jit(solution)/shard_map/convert_element_type | solution.py:515
  (25 shorter events, 1.0 us)
Async XLA Ops:
  1.8 7.2 %collective-permute-start = (bf16[16,5120]{1,0:T(8,128)(2,1)S(1)}, bf16[16,5120]{1,0:T(8,128)(2,1)S(1)}, u32[]{:S(2)}, u32[]{:S(2)}) collective-permute-start(bf16[16,5120]{1,0:T(8,128)(2,1)S(1)} %pad_maximum_fusion), channel_id=1, source_target_pairs={{0,1},{1,4},{4,5},{5,8},{8,9},{9,12},{12,13},{2,3},{3,6},{6,7},{7,... | collective-permute-start | bytes 491528 | tf_op jit(solution)/shard_map/ppermute | solution.py:24
  4.1 4.8 %collective-permute-start.1 = (f32[64,256]{1,0:T(8,128)}, f32[64,256]{1,0:T(8,128)S(1)}, u32[]{:S(2)}, u32[]{:S(2)}) collective-permute-start(f32[64,256]{1,0:T(8,128)} %bitcast.13), channel_id=1, source_target_pairs={{0,1},{1,0},{2,3},{3,2},{4,5},{5,4},{6,7},{7,6},{8,9},{9,8},{10,11... | collective-permute-start | bytes 196616 | tf_op jit(solution)/shard_map/ppermute | solution.py:28
  8.3 3.6 %copy-start.1 = (bf16[256,4096]{1,0:T(8,128)(2,1)S(1)}, bf16[256,4096]{1,0:T(8,128)(2,1)}, u32[]{:S(2)}) copy-start(bf16[256,4096]{1,0:T(8,128)(2,1)} %gate_own.3) | copy-start | bytes 6291460
  11.7 5.7 %collective-permute-start.4 = (bf16[256,1280]{1,0:T(8,128)(2,1)S(1)}, bf16[256,1280]{1,0:T(8,128)(2,1)S(1)}, u32[]{:S(2)}, u32[]{:S(2)}) collective-permute-start(bf16[256,1280]{1,0:T(8,128)(2,1)S(1)} %conv.3), channel_id=1, source_target_pairs={{0,1},{1,0},{2,3},{3,2},{4,5},{5,4},{6,7},{7,6},{8,9},{9,8},{10,11... | collective-permute-start | bytes 1966088 | tf_op jit(solution)/shard_map/ppermute | solution.py:28
  12.0 3.4 %copy-start = (f32[256,64]{0,1:T(8,128)S(1)}, f32[256,64]{0,1:T(8,128)}, u32[]{:S(2)}) copy-start(f32[256,64]{0,1:T(8,128)} %param.20) | copy-start | bytes 196612
  12.0 21.3 %collective-permute-start.6 = (bf16[256,2048]{1,0:T(8,128)(2,1)S(1)}, bf16[256,2048]{1,0:T(8,128)(2,1)S(1)}, u32[]{:S(2)}, u32[]{:S(2)}) collective-permute-start(bf16[256,2048]{1,0:T(8,128)(2,1)S(1)} %constant_dynamic-slice_fusion), channel_id=1, source_target_pairs={{0,1},{1,0},{2,3},{3,2},{4,5},{5,4},{6,7},{7,6},{8,9},{9,8},{10,11... | collective-permute-start | bytes 3145736 | tf_op jit(solution)/shard_map/ppermute | solution.py:28
  15.2 8.8 %collective-permute-start.2 = (bf16[256,1280]{1,0:T(8,128)(2,1)S(1)}, bf16[256,1280]{1,0:T(8,128)(2,1)S(1)}, u32[]{:S(2)}, u32[]{:S(2)}) collective-permute-start(bf16[256,1280]{1,0:T(8,128)(2,1)S(1)} %conv.2), channel_id=1, source_target_pairs={{0,1},{1,0},{2,3},{3,2},{4,5},{5,4},{6,7},{7,6},{8,9},{9,8},{10,11... | collective-permute-start | bytes 1966088 | tf_op jit(solution)/shard_map/ppermute | solution.py:28
  21.5 11.6 %collective-permute-start.5 = (bf16[128,1024]{1,0:T(8,128)(2,1)S(1)}, bf16[128,1024]{1,0:T(8,128)(2,1)S(1)}, u32[]{:S(2)}, u32[]{:S(2)}) collective-permute-start(bf16[128,1024]{1,0:T(8,128)(2,1)S(1)} %get-tuple-element.48), channel_id=1, source_target_pairs={{0,4},{4,8},{8,12},{12,0},{1,5},{5,9},{9,13},{13,1},{2,6},{6,10},{... | collective-permute-start | bytes 786440 | tf_op jit(solution)/shard_map/ppermute | solution.py:391
  28.0 11.5 %collective-permute-start.3 = (bf16[128,1024]{1,0:T(8,128)(2,1)S(1)}, bf16[128,1024]{1,0:T(8,128)(2,1)S(1)}, u32[]{:S(2)}, u32[]{:S(2)}) collective-permute-start(bf16[128,1024]{1,0:T(8,128)(2,1)S(1)} %get-tuple-element.46), channel_id=1, source_target_pairs={{0,4},{4,8},{8,12},{12,0},{1,5},{5,9},{9,13},{13,1},{2,6},{6,10},{... | collective-permute-start | bytes 786440 | tf_op jit(solution)/shard_map/ppermute | solution.py:391
  33.2 14.2 %collective-permute-start.8 = (bf16[128,1024]{1,0:T(8,128)(2,1)S(1)}, bf16[128,1024]{1,0:T(8,128)(2,1)S(1)}, u32[]{:S(2)}, u32[]{:S(2)}) collective-permute-start(bf16[128,1024]{1,0:T(8,128)(2,1)S(1)} %add_convert_fusion.3), channel_id=1, source_target_pairs={{0,4},{4,8},{8,12},{12,0},{1,5},{5,9},{9,13},{13,1},{2,6},{6,10},{... | collective-permute-start | bytes 786440 | tf_op jit(solution)/shard_map/ppermute | solution.py:391
  39.6 10.6 %collective-permute-start.7 = (bf16[128,1024]{1,0:T(8,128)(2,1)S(1)}, bf16[128,1024]{1,0:T(8,128)(2,1)S(1)}, u32[]{:S(2)}, u32[]{:S(2)}) collective-permute-start(bf16[128,1024]{1,0:T(8,128)(2,1)S(1)} %add_convert_fusion.2), channel_id=1, source_target_pairs={{0,4},{4,8},{8,12},{12,0},{1,5},{5,9},{9,13},{13,1},{2,6},{6,10},{... | collective-permute-start | bytes 786440 | tf_op jit(solution)/shard_map/ppermute | solution.py:391
  55.8 2.0 %collective-permute-start.9 = (bf16[256,1024]{1,0:T(8,128)(2,1)S(1)}, bf16[256,1024]{1,0:T(8,128)(2,1)S(1)}, u32[]{:S(2)}, u32[]{:S(2)}) collective-permute-start(bf16[256,1024]{1,0:T(8,128)(2,1)S(1)} %get-tuple-element.70), channel_id=1, source_target_pairs={{0,1},{1,0},{2,3},{3,2},{4,5},{5,4},{6,7},{7,6},{8,9},{9,8},{10,11... | collective-permute-start | bytes 1572872 | tf_op jit(solution)/shard_map/ppermute | solution.py:28
  62.8 2.0 %collective-permute-start.10 = (bf16[256,1024]{1,0:T(8,128)(2,1)S(1)}, bf16[256,1024]{1,0:T(8,128)(2,1)S(1)}, u32[]{:S(2)}, u32[]{:S(2)}) collective-permute-start(bf16[256,1024]{1,0:T(8,128)(2,1)S(1)} %get-tuple-element.73), channel_id=1, source_target_pairs={{0,1},{1,0},{2,3},{3,2},{4,5},{5,4},{6,7},{7,6},{8,9},{9,8},{10,11... | collective-permute-start | bytes 1572872 | tf_op jit(solution)/shard_map/ppermute | solution.py:28
  63.0 14.8 %collective-permute-start.11 = (bf16[256,1024]{1,0:T(8,128)(2,1)S(1)}, bf16[256,1024]{1,0:T(8,128)(2,1)S(1)}, u32[]{:S(2)}, u32[]{:S(2)}) collective-permute-start(bf16[256,1024]{1,0:T(8,128)(2,1)S(1)} %add_convert_fusion.1), channel_id=1, source_target_pairs={{0,2},{2,0},{1,3},{3,1},{4,6},{6,4},{5,7},{7,5},{8,10},{10,8},{9,1... | collective-permute-start | bytes 1572872 | tf_op jit(solution)/shard_map/ppermute | solution.py:28
  65.7 22.8 %collective-permute-start.12 = (bf16[256,1024]{1,0:T(8,128)(2,1)}, bf16[256,1024]{1,0:T(8,128)(2,1)}, u32[]{:S(2)}, u32[]{:S(2)}) collective-permute-start(bf16[256,1024]{1,0:T(8,128)(2,1)} %add_convert_fusion), channel_id=1, source_target_pairs={{0,2},{2,0},{1,3},{3,1},{4,6},{6,4},{5,7},{7,5},{8,10},{10,8},{9,1... | collective-permute-start | bytes 1572872 | tf_op jit(solution)/shard_map/ppermute | solution.py:28
  75.1 14.6 %collective-permute-start.13 = (bf16[256,2048]{1,0:T(8,128)(2,1)}, bf16[256,2048]{1,0:T(8,128)(2,1)}, u32[]{:S(2)}, u32[]{:S(2)}) collective-permute-start(bf16[256,2048]{1,0:T(8,128)(2,1)} %get-tuple-element.78), channel_id=1, source_target_pairs={{0,1},{1,0},{2,3},{3,2},{4,5},{5,4},{6,7},{7,6},{8,9},{9,8},{10,11... | collective-permute-start | bytes 3145736 | tf_op jit(solution)/shard_map/ppermute | solution.py:28

commit v3 on v2

--- a/solution.py
+++ b/solution.py
@@ -13,7 +13,7 @@
 EPSILON = 1e-05
 LOG2E = 1.4426950408889634
 CEILING = 126.0
-VMEM = 32 << 20
+VMEM = 20 << 20
 F32 = jnp.float32
 BF16 = jnp.bfloat16
 
@@ -109,16 +109,6 @@
                 top = top + mm(rim_shift, rim[:, at]) * line
             store(index, at, slice(0, rims), silu(summed[:rims] + top).astype(BF16))
             store(index, at, slice(rims, count), silu(summed[rims:]).astype(BF16))
-
-
-def conv_kernel(meta, docs, x, x_rim, w, bias, s, s_rim, sw, sbias, out, *, taps):
-    width = x.shape[1]
-
-    def store(index, at, rows, value):
-        out[rows, slice(at.start + index * width, at.stop + index * width)] = value
-
-    first = meta[1] + meta[0] * x.shape[0]
-    convolved(first, docs, [(x, x_rim, w, bias), (s, s_rim, sw, sbias)], store, taps)
 
 
 def decay_kernel(
@@ -162,24 +152,29 @@
 
 
 def state_kernel(
-    meta, docs, x, x_rim, w, bias, s, s_rim, sw, sbias, got, tail, kept,
-    x_out, bc_out, s_out, d_out, *, taps, heads, head_width, first_lane,
+    meta, docs, x, got_x, rim_x, late_rim_x, w, bias, s, got_s, rim_s, late_rim_s, sw, sbias, tail, kept,
+    x_out, bc_out, s_out, d_out, raw_x, raw_s, *, taps, heads, head_width, first_lane,
 ):
     half, width = x.shape
+    rims = rim_x.shape[0]
     state_width = bc_out.shape[1] // 2
-    own_row = pl.multiple_of(meta[0] * half, half)
-    got_at = pl.ds(pl.multiple_of((1 - meta[0]) * half, half), half)
-
-    def store(index, at, rows, value):
-        place = pl.ds(pl.multiple_of(own_row + rows.start, 16), rows.stop - rows.start)
-        if index:
-            bc_out[place, at] = value
-        else:
-            x_out[place, at] = value
-
-    convolved(meta[1] + meta[0] * half, docs, [(x, x_rim, w, bias), (s, s_rim, sw, sbias)], store, taps)
-    x_out[got_at, :] = got[:, :width]
-    bc_out[got_at, :] = got[:, width:]
+    own_at = pl.ds(pl.multiple_of(rims + meta[0] * half, 16), half)
+    got_at = pl.ds(pl.multiple_of(rims + (1 - meta[0]) * half, 16), half)
+    for raw, own, got, rim, late in ((raw_x, x, got_x, rim_x, late_rim_x), (raw_s, s, got_s, rim_s, late_rim_s)):
+        raw[:rims, :] = rim[...] + late[...]
+        raw[own_at, :] = own[...]
+        raw[got_at, :] = got[...]
+    for index in range(2):
+        low = index * half
+
+        def store(piece, at, rows, value, low=low):
+            out = bc_out if piece else x_out
+            out[low + rows.start : low + rows.stop, at] = value
+
+        pieces = []
+        for raw, weight, offset in ((raw_x, w, bias), (raw_s, sw, sbias)):
+            pieces.append((raw.at[low + rims : low + rims + half], raw.at[low : low + rims], weight, offset))
+        convolved(meta[1] + low, docs, pieces, store, taps)
     b = bc_out[:, :state_width].T
     span = min(256, width)
     for low in range(0, width, span):
@@ -191,67 +186,69 @@
 
 
 def intra_kernel(
-    meta, docs, x, bc, cum, dlt, gate_own, gate_got, gain,
-    a_out, f_out, state, base, spread, skip, reach, into, tail,
+    meta, docs, x_all, bc_all, cum_all, dlt_all, gate_own, gate_got, gain,
+    a_out, f_out, state, spread, gates, kept_part,
     *, head_width, first_head, group_heads,
 ):
-    step = pl.program_id(0)
-    count, width = x.shape
-    heads = cum.shape[1]
-    state_width = bc.shape[1] // 2
-    first = meta[1] + step * count
-
-    @pl.when(step == 0)
-    def _():
-        state[...] = jnp.zeros_like(state)
-        base[...] = jnp.zeros_like(base)
-        spread[...] = head_lanes(3, heads, head_width, width, first_head * head_width)
-        mine = jnp.where(meta[0] == 0, gain[:, :heads], gain[:, heads:])
-        skip[...] = mm(jnp.concatenate(split3(jnp.broadcast_to(mine, (8, heads))), axis=1), spread[...])
-
-    starts = doc_start(rows_of(count, first), docs)
-    last_start = doc_start(first + count - 1, docs)
-    here = cum[...]
-    before = base[:1, :]
-    end = here[count - 1 :]
+    total, width = x_all.shape
+    heads = cum_all.shape[1]
+    count = CHUNK
+    splits = total // 2 // count
+    state_width = bc_all.shape[1] // 2
+    state[...] = jnp.zeros_like(state)
+    spread[...] = head_lanes(3, heads, head_width, width, first_head * head_width)
+    mine = jnp.where(meta[0] == 0, gain[:, :heads], gain[:, heads:])
+    skip = mm(jnp.concatenate(split3(jnp.broadcast_to(mine, (8, heads))), axis=1), spread[...])[:1]
+    row = lax.broadcasted_iota(jnp.int32, (count, count), 0)
+    col = lax.broadcasted_iota(jnp.int32, (count, count), 1)
+    low_lanes = lax.broadcasted_iota(jnp.int32, (count, 2 * head_width), 1) < head_width
+    zero = jnp.zeros((count, 2 * head_width), BF16)
 
     def spread_over(value):
         return mm(jnp.concatenate(split2(value), axis=1), spread[: 2 * heads])
 
-    reach[...] = spread_over(jnp.where(starts < first, jnp.exp2(here - before), 0.0))
-    into[...] = spread_over(jnp.where(starts < meta[1], jnp.exp2(here), 0.0))
-    to_end = jnp.exp2(end - dlt[...].T)
-    tail[...] = spread_over(jnp.where(rows_of(count, first) >= last_start, to_end, 0.0))
-    kept = jnp.broadcast_to(jnp.where(last_start < first, jnp.exp2(end - before), 0.0), (8, heads))
-    kept = mm(jnp.concatenate(split3(kept), axis=1), spread[...])[:1]
-    row = lax.broadcasted_iota(jnp.int32, (count, count), 0)
-    col = lax.broadcasted_iota(jnp.int32, (count, count), 1)
-    is_own = (step * count) // (count * (pl.num_programs(0) // 2)) == meta[0]
-    low_lanes = lax.broadcasted_iota(jnp.int32, (count, 2 * head_width), 1) < head_width
-    zero = jnp.zeros((count, 2 * head_width), BF16)
-    b = bc[:, :state_width]
-    c = bc[:, state_width:]
-    b_turned = b.T
-    scores = jnp.where((col <= row) & (col >= starts - first), contract_lanes(c, b), 0.0)
-    for head in range(0, group_heads, 2):
-        at = slice(head * head_width, (head + 2) * head_width)
-        pair = []
-        for k in (first_head + head, first_head + head + 1):
-            exponent = jnp.minimum(here[:, k : k + 1] - dlt[k : k + 1, :], CEILING)
-            pair.append((jnp.exp2(exponent) * scores).astype(BF16))
-        value = x[:, at]
-        stacked = jnp.concatenate([jnp.where(low_lanes, value, zero), jnp.where(low_lanes, zero, value)], axis=0)
-        within = mm(jnp.concatenate(pair, axis=1), stacked)
-        old = state[:, at]
-        carried = mm(c, old.astype(BF16)) * reach[:, at]
-        x_part = value.astype(F32)
-        y = within + carried + x_part * skip[:1, at]
-        gate = silu(jnp.where(is_own, gate_own[:, at], gate_got[:, at]).astype(F32))
-        a_out[:, at] = y * gate
-        f_out[:, at] = gate * into[:, at]
-        fresh = mm(b_turned, (x_part * tail[:, at]).astype(BF16))
-        state[:, at] = old * kept[:, at] + fresh
-    base[...] = jnp.broadcast_to(end, base.shape)
+    def chunk(step, before):
+        first = meta[1] + step * count
+        rows = pl.ds(pl.multiple_of(step * count, count), count)
+        half_rows = pl.ds(pl.multiple_of(lax.rem(step, splits) * count, count), count)
+        starts = doc_start(rows_of(count, first), docs)
+        last_start = doc_start(first + count - 1, docs)
+        here = cum_all[rows, :]
+        dlt = dlt_all[:, rows]
+        x = x_all[rows, :]
+        end = here[count - 1 :]
+        b = bc_all[rows, :state_width]
+        c = bc_all[rows, state_width:]
+        scores = jnp.where((col <= row) & (col >= starts - first), contract_lanes(c, b), 0.0)
+        reach = spread_over(jnp.where(starts < first, jnp.exp2(here - before), 0.0))
+        into = spread_over(jnp.where(starts < meta[1], jnp.exp2(here), 0.0))
+        to_end = jnp.exp2(end - dlt.T)
+        tail = spread_over(jnp.where(rows_of(count, first) >= last_start, to_end, 0.0))
+        kept = jnp.broadcast_to(jnp.where(last_start < first, jnp.exp2(end - before), 0.0), (8, heads))
+        kept = mm(jnp.concatenate(split3(kept), axis=1), spread[...])[:1]
+        is_own = step // splits == meta[0]
+        gate = silu(jnp.where(is_own, gate_own[half_rows, :], gate_got[half_rows, :]).astype(F32))
+        gates[...] = gate
+        f_out[rows, :] = gate * into
+        x_part = x.astype(F32)
+        old = state[...]
+        kept_part[...] = mm(c, old.astype(BF16)) * reach + x_part * skip
+        state[...] = old * kept + mm(b.T, (x_part * tail).astype(BF16))
+        for head in range(0, group_heads, 2):
+            at = slice(head * head_width, (head + 2) * head_width)
+            pair = []
+            for k in (first_head + head, first_head + head + 1):
+                exponent = jnp.minimum(here[:, k : k + 1] - dlt[k : k + 1, :], CEILING)
+                pair.append((jnp.exp2(exponent) * scores).astype(BF16))
+            value = x[:, at]
+            stacked = jnp.concatenate(
+                [jnp.where(low_lanes, value, zero), jnp.where(low_lanes, zero, value)], axis=0
+            )
+            within = mm(jnp.concatenate(pair, axis=1), stacked)
+            a_out[rows, at] = (within + kept_part[:, at]) * gates[:, at]
+        return end
+
+    lax.fori_loop(0, total // count, chunk, jnp.zeros((1, heads), F32))
 
 
 def normed(a, f, bc, incoming, gain, squares, divisor):
@@ -282,14 +279,19 @@
 
 def multiply(meta, hidden, w, send, keep):
     half = send.shape[0]
-    there = pl.ds(pl.multiple_of((1 - meta[0]) * half, half), half)
-    here = pl.ds(pl.multiple_of(meta[0] * half, half), half)
-    send[...] = mm(hidden[there, :], w[...]).astype(BF16)
-    keep[...] = mm(hidden[here, :], w[...])
-
-
-def add_kernel(a, b, out):
-    out[...] = a[...] + b[...].astype(F32)
+    product = mm(hidden[...], w[...])
+    mine = meta[0] == 0
+    send[...] = jnp.where(mine, product[half:], product[:half]).astype(BF16)
+    keep[...] = jnp.where(mine, product[:half], product[half:])
+
+
+def sum_kernel(*refs):
+    out = refs[-1]
+    total = refs[0][...]
+    for ref in refs[1:-1]:
+        if ref.shape == out.shape:
+            total = total + ref[...].astype(F32)
+    out[...] = total.astype(out.dtype)
 
 
 def local(
@@ -310,8 +312,6 @@
     part_heads = heads // parts
     part_width = part_heads * head_width
     block = 2 * state_width
-    chunks = count // CHUNK
-    splits = half // CHUNK
     sub = lax.axis_index("sub").astype(jnp.int32)
     ctx = lax.axis_index("ctx").astype(jnp.int32)
     tp = lax.axis_index("tp").astype(jnp.int32)
@@ -332,7 +332,7 @@
             ),
             out_shape=out_shape,
             compiler_params=params,
-            cost_estimate=pl.CostEstimate(flops=flops, bytes_accessed=moved, transcendentals=0),
+            cost_estimate=pl.CostEstimate(flops=0 * flops, bytes_accessed=0 * moved, transcendentals=0),
             name=name,
         )
         return lambda *operands: kernel(
@@ -349,32 +349,37 @@
         meta, docs, x_input, gate_input, mix_weight, bias, state_weight, s_bias, skip, gain, rate, out_weight
     ]
     rims = 16
-    s_rim = state_proj[half - rims :].reshape(rims, groups * block)
-    rim = shifted(jnp.concatenate([x_input[half - rims :], s_rim], axis=1), ("ctx", "sub"), 1)
+    s_width = parts * block
+    s_half = (lambda v, core: lax.dynamic_slice_in_dim(v, core * s_width, s_width, 1)) if whole_groups else (
+        lambda v, core: v
+    )
+    last_x, last_s = x_input[half - rims :], s_input[half - rims :]
+    flat = 2 * ctx_size
+
+    def rim_for(core):
+        shard = jnp.concatenate([last_x[:, core * width : (core + 1) * width], s_half(last_s, core)], axis=1)
+        return lax.ppermute(shard, ("ctx", "sub"), [(i, i + 1 + core) for i in range(1, flat - 2, 2)])
+
+    rim, late_rim = rim_for(0), rim_for(1)
     raw = step_raw.T
     got_raw = swapped(raw, "sub")
-    rim, got_raw = after(rim, got_raw)
-    mixed = (x_input, rim, mix_weight, bias, s_input, rim, state_weight, s_bias)
-
-    def mix_specs(part, other):
-        at = lambda m: (1 - m[0] if other else m[0]) * parts + part
+    got_x = swapped(lax.dynamic_slice_in_dim(x_input, (1 - sub) * width, width, 1), "sub")
+    got_s = swapped(s_half(s_input, 1 - sub), "sub")
+    got_gate = swapped(lax.dynamic_slice_in_dim(gate_input, (1 - sub) * width, width, 1), "sub")
+    got_gate, got_raw = after(got_gate, got_raw)
+    mixed = (x_input, got_x, rim, late_rim, mix_weight, bias, s_input, got_s, rim, late_rim, state_weight, s_bias)
+
+    def mix_specs(part):
+        at = lambda m: m[0] * parts + part
         s_at = at if whole_groups else (lambda m: 0)
-        rim_at = lambda m: channels // block + s_at(m)
+        here = lambda m: part
+        rim_at = lambda m: width // block + part
         specs = []
-        for size, places in ((part_width, (at, at, at, at)), (block, (s_at, rim_at, s_at, s_at))):
-            for rows, place in zip((half, rims, taps, 1), places):
+        for size, places in ((part_width, (at, here, here, here, at, at)), (block, (s_at, here, rim_at, rim_at, s_at, s_at))):
+            for rows, place in zip((half, half, rims, rims, taps, 1), places):
                 specs.append(pl.BlockSpec((rows, size), lambda i, m, d, place=place: (0, place(m))))
-        specs[6] = pl.BlockSpec((taps, 1, 2, state_width), lambda i, m, d: (0, s_at(m), 0, 0))
+        specs[10] = pl.BlockSpec((taps, 1, 2, state_width), lambda i, m, d: (0, s_at(m), 0, 0))
         return specs
-
-    got = []
-    for part in range(parts):
-        other = call(
-            functools.partial(conv_kernel, taps=taps), "conv", (1,), mix_specs(part, True),
-            fixed(half, part_width + block), shape_of((half, part_width + block), BF16),
-            flops=2 * taps * half * half * part_width, moved=4 * half * part_width,
-        )(meta, docs, *mixed)
-        got.append(swapped(other, "sub"))
 
     cum, dlt, tail, kept = call(
         decay_kernel, "decay", (1,),
@@ -391,14 +396,14 @@
         return lax.ppermute(shard, "ctx", [(i, (i + 1) % ctx_size) for i in range(ctx_size)])
 
     made = []
+    next_meta = meta
     for part in range(parts):
         x_cat, bc, state, decay = call(
             functools.partial(
                 state_kernel, taps=taps, heads=heads, head_width=head_width, first_lane=part * part_width
             ),
             "state", (1,),
-            mix_specs(part, False)
-            + [fixed(half, part_width + block), fixed(count, 2 * heads), fixed(8, 3 * heads)],
+            mix_specs(part) + [fixed(count, 2 * heads), fixed(8, 3 * heads)],
             [
                 fixed(count, part_width), fixed(count, block), fixed(state_width, part_width), fixed(1, part_width),
             ],
@@ -406,12 +411,14 @@
                 shape_of((count, part_width), BF16), shape_of((count, block), BF16),
                 shape_of((state_width, part_width), BF16), shape_of((1, part_width), F32),
             ],
+            [pltpu.VMEM((rims + count, part_width), BF16), pltpu.VMEM((rims + count, block), BF16)],
             flops=4 * half * count * part_width, moved=6 * count * part_width,
-        )(meta, docs, *mixed, got[part], tail, kept)
-        made.append((x_cat, bc, state, decay, onward(state)))
-
-    got_gate = swapped(lax.dynamic_slice_in_dim(gate_input, (1 - sub) * width, width, 1), "sub")
-    by_row = lambda n: pl.BlockSpec((CHUNK, n), lambda i, *m: (i, 0))
+        )(next_meta, docs, *mixed, tail, kept)
+        state, next_meta = after(state, next_meta)
+        pinned.append(next_meta)
+        made.append([x_cat, bc, state, decay, onward(state)])
+        if part:
+            made[part - 1][4], made[part][0] = after(made[part - 1][4], x_cat)
     ready = []
     for part in range(parts):
         x_cat, bc, state, decay, arriving = made[part]
@@ -422,26 +429,22 @@
             leaving = (state.astype(F32) + decay * arriving.astype(F32)).astype(BF16)
             leaving, x_cat = after(leaving, x_cat)
             arriving = onward(leaving)
-        gate_at = lambda i, m, d, part=part: (lax.rem(i, splits), m[0] * parts + part)
-        got_at = lambda i, m, d, part=part: (lax.rem(i, splits), part)
         gated, carry_gate = call(
             functools.partial(
                 intra_kernel, head_width=head_width, first_head=part * part_heads, group_heads=part_heads
             ),
-            "intra", (chunks,),
+            "intra", (1,),
             [
-                by_row(part_width), by_row(block), by_row(heads),
-                pl.BlockSpec((heads, CHUNK), lambda i, *m: (0, i)),
-                pl.BlockSpec((CHUNK, part_width), gate_at), pl.BlockSpec((CHUNK, part_width), got_at),
+                fixed(count, part_width), fixed(count, block), fixed(count, heads), fixed(heads, count),
+                pl.BlockSpec((half, part_width), lambda i, m, d, part=part: (0, m[0] * parts + part)),
+                pl.BlockSpec((half, part_width), lambda i, m, d, part=part: (0, part)),
                 fixed(1, all_heads),
             ],
-            [by_row(part_width), by_row(part_width)],
+            [fixed(count, part_width), fixed(count, part_width)],
             [shape_of((count, part_width), F32), shape_of((count, part_width), F32)],
             [
-                pltpu.VMEM((state_width, part_width), F32), pltpu.VMEM((8, heads), F32),
-                pltpu.VMEM((3 * heads, part_width), BF16), pltpu.VMEM((8, part_width), F32),
+                pltpu.VMEM((state_width, part_width), F32), pltpu.VMEM((3 * heads, part_width), BF16),
                 pltpu.VMEM((CHUNK, part_width), F32), pltpu.VMEM((CHUNK, part_width), F32),
-                pltpu.VMEM((CHUNK, part_width), F32),
             ],
             flops=10 * count * part_width * CHUNK, moved=14 * count * part_width,
         )(meta, docs, x_cat, bc, cum, dlt, gate_input, got_gate, skip)
@@ -453,9 +456,12 @@
     for part, (gated, carry_gate, bc, arriving) in enumerate(ready[:-1]):
         hiddens.append(
             call(
-                functools.partial(norm_kernel, divisor=divisor), "norm", (chunks,),
-                [by_row(part_width), by_row(part_width), by_row(block), fixed(state_width, part_width), gain_at(part)],
-                by_row(part_width), shape_of((count, part_width), BF16),
+                functools.partial(norm_kernel, divisor=divisor), "norm", (1,),
+                [
+                    fixed(count, part_width), fixed(count, part_width), fixed(count, block),
+                    fixed(state_width, part_width), gain_at(part),
+                ],
+                fixed(count, part_width), shape_of((count, part_width), BF16),
                 flops=2 * count * part_width * state_width, moved=10 * count * part_width, prefetch=1,
             )(meta, gated, carry_gate, bc, arriving, gain)
         )
@@ -474,45 +480,66 @@
     near_blocks = out_cols // mm_cols
     row_specs = [pl.BlockSpec((half, mm_cols), lambda i, m: (0, i))] * 2
 
-    def product(first, blocks, body, name, operands, specs, outs, out_shapes):
+    def product(first, blocks, body, name, operands, specs, outs, out_shapes, declared=1):
         cols = blocks * mm_cols
         return call(
             body, name, (blocks,),
-            specs + [pl.BlockSpec((width, mm_cols), lambda i, m: (0, first(m) + i))],
+            specs + [pl.BlockSpec((width, mm_cols), lambda i, m: (0, first(m, i)))],
             outs + row_specs,
             out_shapes + [shape_of((half, cols), BF16), shape_of((half, cols), F32)],
-            flops=2 * count * width * cols, moved=2 * width * cols, prefetch=1,
+            flops=declared * 2 * count * width * cols, moved=declared * 2 * width * cols, prefetch=1,
         )(meta, *operands, out_weight)
 
-    far_first = (lambda m: (1 - m[2]) * near_blocks) if pair else (lambda m: 0)
-    far_blocks = near_blocks if pair else features // mm_cols
-    lead = max(far_blocks // 2, 1)
     operands = [*hiddens, gated, carry_gate, bc, arriving, gain, *squares]
     specs = [fixed(*v.shape) for v in operands]
     specs[len(hiddens) + 4] = gain_at(parts - 1)
+    project = functools.partial(project_kernel, ready=len(hiddens), squared=len(squares), divisor=divisor)
+    hidden_spec, hidden_shape = fixed(count, width), shape_of((count, width), BF16)
+    if not pair:
+        every = features // mm_cols
+        _, send, keep = product(lambda m, i: i, every, project, "project", operands, specs, [hidden_spec], [hidden_shape])
+        summed = (keep + swapped(send, "sub").astype(F32)).astype(BF16)
+        return lax.psum_scatter(summed, "tp", scatter_dimension=1, tiled=True)
+    lead = max(3 * near_blocks // 4, 1)
+    far_first = lambda m: (1 - m[2]) * near_blocks
     hidden, send, keep = product(
-        far_first, lead, functools.partial(project_kernel, ready=len(hiddens), squared=len(squares), divisor=divisor),
-        "project", operands, specs, [fixed(count, width)], [shape_of((count, width), BF16)],
+        lambda m, i: far_first(m) + i, lead, project, "project", operands, specs, [hidden_spec], [hidden_shape]
     )
-    far = []
-    rest = [(lambda m: far_first(m) + lead, far_blocks - lead)] if far_blocks > lead else []
-    if pair:
-        rest.append((lambda m: m[2] * near_blocks, near_blocks))
-    for first, blocks in rest:
-        summed = (keep + swapped(send, "sub").astype(F32)).astype(BF16)
-        hidden, summed = after(hidden, summed)
-        far.append(swapped(summed, "tp") if pair else summed)
-        send, keep = product(first, blocks, multiply, "product", [hidden], [fixed(count, width)], [], [])
-    if not pair:
-        far.append((keep + swapped(send, "sub").astype(F32)).astype(BF16))
-        return lax.psum_scatter(jnp.concatenate(far, axis=1), "tp", scatter_dimension=1, tiled=True)
-    lead_cols = far[0].shape[1]
-    early = call(
-        add_kernel, "add", (1,), [fixed(half, lead_cols)] * 2, fixed(half, lead_cols),
-        shape_of((half, lead_cols), F32), flops=1 << 38, moved=10 * half * lead_cols, prefetch=0,
-    )(keep, far[0])
-    late = [keep[:, lead_cols:] + v.astype(F32) for v in far[1:]]
-    return (jnp.concatenate([early, *late], axis=1) + swapped(send, "sub").astype(F32)).astype(BF16)
+    summed = (keep + swapped(send, "sub").astype(F32)).astype(BF16)
+    hidden, summed = after(hidden, summed)
+    far_lead = swapped(summed, "tp")
+    rest = near_blocks - lead
+    send, keep = product(
+        lambda m, i: far_first(m) + lead + i, rest, multiply, "product", [hidden], [hidden_spec], [], []
+    )
+    summed = (keep + swapped(send, "sub").astype(F32)).astype(BF16)
+    hidden, summed = after(hidden, summed)
+    far_rest = swapped(summed, "tp")
+    send, keep = product(
+        lambda m, i: m[2] * near_blocks + i, near_blocks, multiply, "product", [hidden], [hidden_spec], [], [],
+        declared=0,
+    )
+    got = swapped(send, "sub")
+
+    def finish(first, terms, name, dtype, old=(), weight=0):
+        blocks = min(v.shape[1] for v in terms) // mm_cols
+        at = lambda v: (lambda i: (0, i + (first if v.shape[1] == out_cols else 0)))
+        cols = out_cols if dtype == BF16 else blocks * mm_cols
+        return pl.pallas_call(
+            sum_kernel, grid=(blocks,),
+            in_specs=[pl.BlockSpec((half, mm_cols), at(v)) for v in terms]
+            + [pl.BlockSpec(memory_space=pl.ANY)] * len(old),
+            out_specs=pl.BlockSpec((half, mm_cols), lambda i: (0, i + (first if dtype == BF16 else 0))),
+            out_shape=shape_of((half, cols), dtype),
+            input_output_aliases={len(terms): 0} if old else {},
+            compiler_params=params,
+            cost_estimate=pl.CostEstimate(flops=weight, bytes_accessed=0, transcendentals=0),
+            name=name,
+        )(*terms, *old)
+
+    early = finish(0, [keep, far_lead], "early", F32, weight=1 << 38)
+    output = finish(0, [early, got], "lead", BF16)
+    return finish(lead, [keep, got, far_rest], "rest", BF16, old=(output,))
 
 
 def solution(mesh):

time: 93 us -> 86.5 us (0.930)
  waiting for transfers between devices: 19 us -> 13.5 us
  other arithmetic: 5.61 us -> 2.45 us
  local copies, waits for them, and re-layouts: 3.2 us -> 4.82 us
  Pallas kernels: 49.5 us -> 51 us
    ppermute x9, waiting for transfers between devices: 15.5 us -> 9 us  [swapped(): lax.ppermute(shard, axis, [(i, i ^ 1) for i in range(lax.axis_size(axis))])]
    pallas_call x0 -> x3, Pallas kernels: none -> 5.25 us  [finish(): pl.pallas_call(sum_kernel, grid=(blocks,), in_specs=[pl.BlockSpec((half,...]
    pallas_call x12 -> x9, Pallas kernels: 49.5 us -> 45.7 us  [call(): kernel(*(pltpu.with_memory_space_constraint(v, pltpu.HBM) if any((v is p...]
    convert_element_type x1 -> x0, other arithmetic: 2.5 us -> none  [local(): (jnp.concatenate([early, *late], axis=1) + swapped(send, 'sub').astype(F3...]
    dynamic_slice x0 -> x3, local copies, waits for them, and re-layouts: none -> 2.48 us  [the longest x1 2.45 us: local(): lax.dynamic_slice_in_dim(x_input, (1 - sub) * width, width, 1)]
    ppermute x9, starting transfers between devices: 6.78 us -> 8.32 us  [swapped(): lax.ppermute(shard, axis, [(i, i ^ 1) for i in range(lax.axis_size(axis))])]
    ppermute x4, starting transfers between devices: 5.57 us -> 4.29 us  [onward(): lax.ppermute(shard, 'ctx', [(i, (i + 1) % ctx_size) for i in range(ctx_si...]
    add x1 -> x0, other arithmetic: 1.17 us -> none  [local(): late = [keep[:, lead_cols:] + v.astype(F32) for v in far[1:]]]
  transfers between devices with their start and end apart: 14 -> 15, of which waited for: 5 -> 7; matrix products, arithmetic and copies ran while one was open for 5% -> 8% of each run, Pallas kernels for 39% -> 43%
where the time goes in v3:
time: 86.5 us; the launch traced here: 85.9 us
  Pallas kernels  51 us (59%)
  starting transfers between devices  13.9 us (16%)
  waiting for transfers between devices  13.5 us (16%)
  local copies, waits for them, and re-layouts  4.82 us (6%)
  other arithmetic  2.45 us (3%)
    pallas_call x9, Pallas kernels, call(): kernel(*(pltpu.with_memory_space_constraint(v, pltpu.HBM) if any((v is p...  45.7 us
    ppermute x9, waiting for transfers between devices, swapped(): lax.ppermute(shard, axis, [(i, i ^ 1) for i in range(lax.axis_size(axis))])  9 us
    ppermute x9, starting transfers between devices, swapped(): lax.ppermute(shard, axis, [(i, i ^ 1) for i in range(lax.axis_size(axis))])  8.32 us
    pallas_call x3, Pallas kernels, finish(): pl.pallas_call(sum_kernel, grid=(blocks,), in_specs=[pl.BlockSpec((half,...  5.25 us
    ppermute x4, waiting for transfers between devices, onward(): lax.ppermute(shard, 'ctx', [(i, (i + 1) % ctx_size) for i in range(ctx_si...  4.46 us
    ppermute x4, starting transfers between devices, onward(): lax.ppermute(shard, 'ctx', [(i, (i + 1) % ctx_size) for i in range(ctx_si...  4.29 us
    dynamic_slice x1, local copies, waits for them, and re-layouts, local(): lax.dynamic_slice_in_dim(x_input, (1 - sub) * width, width, 1)  2.45 us
  transfers between devices with their start and end apart: 15, of which 7 were waited for; matrix products, arithmetic and copies ran while one was open for 8% of the time, Pallas kernels for 43%

profile of v3, /device:TPU:0, one launch (start us, length us, event | category | flops | bytes accessed | tf_op | source)
XLA Modules:
  0.0 85.9 jit_solution(5382519757285961101)
XLA Ops:
  0.5 2.5 %constant_dynamic-slice_fusion.2 = bf16[256,2048]{1,0:T(8,128)(2,1)} fusion(bf16[256,4096]{1,0:T(8,128)(2,1)} %x.3, s32[]{:T(128)S(6)} %select_n.7), kind=kLoop, calls=%fused_computation.8 | loop fusion | bytes 2097156 | tf_op jit(solution)/shard_map/dynamic_slice | solution.py:366
  3.0 1.1 %constant_dynamic-slice_fusion = bf16[256,2048]{1,0:T(8,128)(2,1)} fusion(bf16[256,4096]{1,0:T(8,128)(2,1)S(1)} %copy-done.1, s32[]{:T(128)S(6)} %select_n.7), kind=kLoop, calls=%fused_computation.6 | loop fusion | bytes 2097156 | tf_op jit(solution)/shard_map/dynamic_slice | solution.py:368
  4.5 0.9 %fusion = (bf16[16,2048]{1,0:T(8,128)(2,1)S(1)}, bf16[16,2048]{1,0:T(8,128)(2,1)S(1)}) fusion(bf16[256,4096]{1,0:T(8,128)(2,1)} %x.3), kind=kLoop, calls=%fused_computation.10 | loop fusion | bytes 262144 | tf_op jit(solution)/shard_map/slice | solution.py:360
  5.4 0.7 collective-permute-start.1
  6.5 4.0 %collective-permute-start.3 = (bf16[256,512]{1,0:T(8,128)(2,1)S(1)}, bf16[256,512]{1,0:T(8,128)(2,1)S(1)}, u32[]{:S(2)}, u32[]{:S(2)}) collective-permute-start(bf16[256,512]{1,0:T(8,128)(2,1)S(1)} %constant_dynamic-slice_fusion.1), channel_id=1, source_target_pairs={{0,1},{1,0},{2,3},{3,2},{4,5},{5,4},{6,7},{7,6},{8,9},{9,8},{10,11... | collective-permute-start | bytes 786440 | tf_op jit(solution)/shard_map/ppermute | solution.py:28
  10.5 0.6 pad_maximum_fusion.1
  11.2 0.7 collective-permute-start.2
  11.8 0.7 pad_add_fusion.meta
  12.5 2.1 %decay.1 = (f32[512,32]{1,0:T(8,128)S(1)}, f32[32,512]{1,0:T(8,128)S(1)}, bf16[512,64]{1,0:T(8,128)(2,1)S(1)}, bf16[8,96]{1,0:T(8,128)(2,1)S(1)}) custom-call(s32[3]{0:T(128)} %pad_add_fusion.meta, s32[8]{0:T(128)} %docs.9, f32[64,256]{1,0:T(8,128)S(1)} %bitcast.12, f32[64,256]{1,0:T(8,128)S(1)} %collective-permute-done.5.got_raw, f32[1,64]{1,0:T(1,128)} %bitcast.23), custom_call_target="tpu_custom_call" | custom-call | tf_op jit(solution)/shard_map/decay/pallas_call | solution.py:338
  14.6 5.3 %state.2 = (bf16[512,1024]{1,0:T(8,128)(2,1)S(1)}, bf16[512,256]{1,0:T(8,128)(2,1)S(1)}, bf16[128,1024]{1,0:T(8,128)(2,1)S(1)}, f32[1,1024]{1,0:T(1,128)S(1)}) custom-call(s32[3]{0:T(128)} %pad_add_fusion.meta, s32[8]{0:T(128)} %docs.9, bf16[256,4096]{1,0:T(8,128)(2,1)} %x.3, bf16[256,2048]{1,0:T(8,128)(2,1)S(1)} %collective-permute-done.got_x, ...), custom_call_target="tpu_custom_call" | custom-call | tf_op jit(solution)/shard_map/state/pallas_call | solution.py:338
  19.9 1.6 %collective-permute-start.7 = (bf16[128,1024]{1,0:T(8,128)(2,1)S(1)}, bf16[128,1024]{1,0:T(8,128)(2,1)S(1)}, u32[]{:S(2)}, u32[]{:S(2)}) collective-permute-start(bf16[128,1024]{1,0:T(8,128)(2,1)S(1)} %get-tuple-element.55), channel_id=1, source_target_pairs={{0,4},{4,8},{8,12},{12,0},{1,5},{5,9},{9,13},{13,1},{2,6},{6,10},{... | collective-permute-start | bytes 786440 | tf_op jit(solution)/shard_map/ppermute | solution.py:396
  21.6 5.3 %state.3 = (bf16[512,1024]{1,0:T(8,128)(2,1)S(1)}, bf16[512,256]{1,0:T(8,128)(2,1)S(1)}, bf16[128,1024]{1,0:T(8,128)(2,1)S(1)}, f32[1,1024]{1,0:T(1,128)S(1)}) custom-call(s32[3]{0:T(128)} %pad_add_fusion.meta, s32[8]{0:T(128)} %docs.9, bf16[256,4096]{1,0:T(8,128)(2,1)} %x.3, bf16[256,2048]{1,0:T(8,128)(2,1)S(1)} %collective-permute-done.got_x, ...), custom_call_target="tpu_custom_call" | custom-call | tf_op jit(solution)/shard_map/state/pallas_call | solution.py:338
  26.9 1.6 %collective-permute-start.6 = (bf16[128,1024]{1,0:T(8,128)(2,1)S(1)}, bf16[128,1024]{1,0:T(8,128)(2,1)S(1)}, u32[]{:S(2)}, u32[]{:S(2)}) collective-permute-start(bf16[128,1024]{1,0:T(8,128)(2,1)S(1)} %get-tuple-element.53), channel_id=1, source_target_pairs={{0,4},{4,8},{8,12},{12,0},{1,5},{5,9},{9,13},{13,1},{2,6},{6,10},{... | collective-permute-start | bytes 786440 | tf_op jit(solution)/shard_map/ppermute | solution.py:396
  28.5 0.8 collective-permute-done.7
  29.5 5.9 %intra.2 = (f32[512,1024]{1,0:T(8,128)S(1)}, f32[512,1024]{1,0:T(8,128)S(1)}) custom-call(s32[3]{0:T(128)} %pad_add_fusion.meta, s32[8]{0:T(128)} %docs.9, bf16[512,1024]{1,0:T(8,128)(2,1)S(1)} %get-tuple-element.60.x_all, bf16[512,256]{1,0:T(8,128)(2,1)S(1)} %get-tuple-element.61.bc_all.bc, f32[512,32]{1,0:T(8,128)S(1)} %get-tuple-element.62.cum_all, ...), custom_call_target="tpu_custom_call" | custom-call | tf_op jit(solution)/shard_map/intra/pallas_call | solution.py:338
  35.4 1.2 %collective-permute-done.6 = bf16[128,1024]{1,0:T(8,128)(2,1)S(1)} collective-permute-done((bf16[128,1024]{1,0:T(8,128)(2,1)S(1)}, bf16[128,1024]{1,0:T(8,128)(2,1)S(1)}, u32[]{:S(2)}, u32[]{:S(2)}) %collective-permute-start.6) | collective-permute-done | bytes 262176 | tf_op jit(solution)/shard_map/ppermute | solution.py:396
  36.7 1.0 %collective-permute-start.8 = (bf16[128,1024]{1,0:T(8,128)(2,1)S(1)}, bf16[128,1024]{1,0:T(8,128)(2,1)S(1)}, u32[]{:S(2)}, u32[]{:S(2)}) collective-permute-start(bf16[128,1024]{1,0:T(8,128)(2,1)S(1)} %add_convert_fusion.2), channel_id=1, source_target_pairs={{0,4},{4,8},{8,12},{12,0},{1,5},{5,9},{9,13},{13,1},{2,6},{6,10},{... | collective-permute-start | bytes 786440 | tf_op jit(solution)/shard_map/ppermute | solution.py:396
  37.7 5.9 %intra.3 = (f32[512,1024]{1,0:T(8,128)S(1)}, f32[512,1024]{1,0:T(8,128)S(1)}) custom-call(s32[3]{0:T(128)} %pad_add_fusion.meta, s32[8]{0:T(128)} %docs.9, bf16[512,1024]{1,0:T(8,128)(2,1)S(1)} %get-tuple-element.73.x_all, bf16[512,256]{1,0:T(8,128)(2,1)S(1)} %get-tuple-element.74.bc_all.refs_3_, f32[512,32]{1,0:T(8,128)S(1)} %get-tuple-element.62.cum_all, ...), custom_call_target="tpu_custom_call" | custom-call | tf_op jit(solution)/shard_map/intra/pallas_call | solution.py:338
  43.5 2.0 %norm.1.refs_0_ = bf16[512,1024]{1,0:T(8,128)(2,1)S(1)} custom-call(s32[3]{0:T(128)} %pad_add_fusion.meta, f32[512,1024]{1,0:T(8,128)S(1)} %get-tuple-element.69.a, f32[512,1024]{1,0:T(8,128)S(1)} %get-tuple-element.70.f, bf16[512,256]{1,0:T(8,128)(2,1)S(1)} %get-tuple-element.61.bc_all.bc, bf16[128,1024]{1,0:T(8,128)(2,1)S(1)} %collective-permute-done.9.incoming, ...), custom_call_target="tpu_custom_call" | custom-call | tf_op jit(solution)/shard_map/norm/pallas_call | solution.py:338
  45.5 2.4 %collective-permute-done.8.refs_4_ = bf16[128,1024]{1,0:T(8,128)(2,1)S(1)} collective-permute-done((bf16[128,1024]{1,0:T(8,128)(2,1)S(1)}, bf16[128,1024]{1,0:T(8,128)(2,1)S(1)}, u32[]{:S(2)}, u32[]{:S(2)}) %collective-permute-start.8) | collective-permute-done | bytes 262176 | tf_op jit(solution)/shard_map/ppermute | solution.py:396
  48.0 7.2 %project.1 = (bf16[512,2048]{1,0:T(8,128)(2,1)S(1)}, bf16[256,1536]{1,0:T(8,128)(2,1)S(1)}, f32[256,1536]{1,0:T(8,128)S(1)}) custom-call(s32[3]{0:T(128)} %pad_add_fusion.meta, bf16[512,1024]{1,0:T(8,128)(2,1)S(1)} %norm.1.refs_0_, f32[512,1024]{1,0:T(8,128)S(1)} %get-tuple-element.75.refs_1_, f32[512,1024]{1,0:T(8,128)S(1)} %get-tuple-element.76.refs_2_, ...), custom_call_target="tpu_custom_call" | custom-call | tf_op jit(solution)/shard_map/project/pallas_call | solution.py:338
  55.2 1.1 %collective-permute-start.10 = (bf16[256,1536]{1,0:T(8,128)(2,1)S(1)}, bf16[256,1536]{1,0:T(8,128)(2,1)S(1)}, u32[]{:S(2)}, u32[]{:S(2)}) collective-permute-start(bf16[256,1536]{1,0:T(8,128)(2,1)S(1)} %get-tuple-element.80), channel_id=1, source_target_pairs={{0,1},{1,0},{2,3},{3,2},{4,5},{5,4},{6,7},{7,6},{8,9},{9,8},{10,11... | collective-permute-start | bytes 2359304 | tf_op jit(solution)/shard_map/ppermute | solution.py:28
  56.3 1.9 %collective-permute-done.10 = bf16[256,1536]{1,0:T(8,128)(2,1)S(1)} collective-permute-done((bf16[256,1536]{1,0:T(8,128)(2,1)S(1)}, bf16[256,1536]{1,0:T(8,128)(2,1)S(1)}, u32[]{:S(2)}, u32[]{:S(2)}) %collective-permute-start.10) | collective-permute-done | bytes 786464 | tf_op jit(solution)/shard_map/ppermute | solution.py:28
  58.4 1.6 %collective-permute-start.14 = (bf16[256,1536]{1,0:T(8,128)(2,1)S(1)}, bf16[256,1536]{1,0:T(8,128)(2,1)S(1)}, u32[]{:S(2)}, u32[]{:S(2)}) collective-permute-start(bf16[256,1536]{1,0:T(8,128)(2,1)S(1)} %add_convert_fusion), channel_id=1, source_target_pairs={{0,2},{2,0},{1,3},{3,1},{4,6},{6,4},{5,7},{7,5},{8,10},{10,8},{9,1... | collective-permute-start | bytes 2359304 | tf_op jit(solution)/shard_map/ppermute | solution.py:28
  60.0 3.5 %product.2 = (bf16[256,512]{1,0:T(8,128)(2,1)S(1)}, f32[256,512]{1,0:T(8,128)S(1)}) custom-call(s32[3]{0:T(128)} %pad_add_fusion.meta, bf16[512,2048]{1,0:T(8,128)(2,1)S(1)} %get-tuple-element.84.hidden, bf16[2048,4096]{1,0:T(8,128)(2,1)} %w.7), custom_call_target="tpu_custom_call" | custom-call | tf_op jit(solution)/shard_map/product/pallas_call | solution.py:338
  63.6 1.5 %collective-permute-done.11 = bf16[256,512]{1,0:T(8,128)(2,1)S(1)} collective-permute-done((bf16[256,512]{1,0:T(8,128)(2,1)S(1)}, bf16[256,512]{1,0:T(8,128)(2,1)S(1)}, u32[]{:S(2)}, u32[]{:S(2)}) %collective-permute-start.11) | collective-permute-done | bytes 262176 | tf_op jit(solution)/shard_map/ppermute | solution.py:28
  65.1 0.8 add_convert_fusion.1
  66.4 8.6 %product.3 = (bf16[256,2048]{1,0:T(8,128)(2,1)}, f32[256,2048]{1,0:T(8,128)S(1)}) custom-call(s32[3]{0:T(128)} %pad_add_fusion.meta, bf16[512,2048]{1,0:T(8,128)(2,1)S(1)} %get-tuple-element.84.hidden, bf16[2048,4096]{1,0:T(8,128)(2,1)} %w.7), custom_call_target="tpu_custom_call" | custom-call | tf_op jit(solution)/shard_map/product/pallas_call | solution.py:338
  75.0 3.9 %collective-permute-done.14.refs_1_ = bf16[256,1536]{1,0:T(8,128)(2,1)S(1)} collective-permute-done((bf16[256,1536]{1,0:T(8,128)(2,1)S(1)}, bf16[256,1536]{1,0:T(8,128)(2,1)S(1)}, u32[]{:S(2)}, u32[]{:S(2)}) %collective-permute-start.14) | collective-permute-done | bytes 786464 | tf_op jit(solution)/shard_map/ppermute | solution.py:28
  79.3 2.9 %lead.1.refs_3_ = bf16[256,2048]{1,0:T(8,128)(2,1)} custom-call(f32[256,1536]{1,0:T(8,128)S(1)} %early.1.refs_0_, bf16[256,2048]{1,0:T(8,128)(2,1)} %collective-permute-done.12.refs_1_), custom_call_target="tpu_custom_call" | custom-call | tf_op jit(solution)/shard_map/lead/pallas_call | solution.py:528
  82.3 1.7 %collective-permute-done.13.refs_2_ = bf16[256,512]{1,0:T(8,128)(2,1)} collective-permute-done((bf16[256,512]{1,0:T(8,128)(2,1)}, bf16[256,512]{1,0:T(8,128)(2,1)}, u32[]{:S(2)}, u32[]{:S(2)}) %collective-permute-start.13) | collective-permute-done | bytes 262176 | tf_op jit(solution)/shard_map/ppermute | solution.py:28
  84.0 1.8 %rest.1 = bf16[256,2048]{1,0:T(8,128)(2,1)} custom-call(f32[256,2048]{1,0:T(8,128)S(1)} %get-tuple-element.85.refs_0_, bf16[256,2048]{1,0:T(8,128)(2,1)} %collective-permute-done.12.refs_1_, bf16[256,512]{1,0:T(8,128)(2,1)} %collective-permute-done.13.refs_2_, bf16[256,2048]{1,0:T(8,128)(2,1)} %lead.1.refs_3_), custom_call_target="tpu_custom_call", output_to_operand_aliasing={{}: (3, {})} | custom-call | tf_op jit(solution)/shard_map/rest/pallas_call | solution.py:528
  (32 shorter events, 3.0 us)
Async XLA Ops:
  0.0 11.2 %collective-permute-start.5 = (f32[64,256]{1,0:T(8,128)}, f32[64,256]{1,0:T(8,128)S(1)}, u32[]{:S(2)}, u32[]{:S(2)}) collective-permute-start(f32[64,256]{1,0:T(8,128)} %bitcast.11), channel_id=1, source_target_pairs={{0,1},{1,0},{2,3},{3,2},{4,5},{5,4},{6,7},{7,6},{8,9},{9,8},{10,11... | collective-permute-start | bytes 196616 | tf_op jit(solution)/shard_map/ppermute | solution.py:28
  0.5 2.5 %copy-start.1 = (bf16[256,4096]{1,0:T(8,128)(2,1)S(1)}, bf16[256,4096]{1,0:T(8,128)(2,1)}, u32[]{:S(2)}) copy-start(bf16[256,4096]{1,0:T(8,128)(2,1)} %gate_own.3) | copy-start | bytes 6291460
  0.5 4.9 %slice-start = ((bf16[256,4,2,128]{3,2,1,0:T(2,128)(2,1)}), bf16[16,4,2,128]{3,2,1,0:T(2,128)(2,1)S(1)}, s32[]{:S(2)}) async-start(bf16[256,4,2,128]{3,2,1,0:T(2,128)(2,1)} %param.15), calls=%async_computation | async-start | bytes 65536 | tf_op jit(solution)/shard_map/slice | solution.py:356
  0.5 5.7 %copy-start.2 = (bf16[256,4,2,128]{3,2,1,0:T(2,128)(2,1)S(1)}, bf16[256,4,2,128]{3,2,1,0:T(2,128)(2,1)}, u32[]{:S(2)}) copy-start(bf16[256,4,2,128]{3,2,1,0:T(2,128)(2,1)} %param.15) | copy-start | bytes 1572868
  2.9 9.6 %copy-start = (f32[256,64]{0,1:T(8,128)S(1)}, f32[256,64]{0,1:T(8,128)}, u32[]{:S(2)}) copy-start(f32[256,64]{0,1:T(8,128)} %param.20) | copy-start | bytes 196612
  2.9 11.7 %collective-permute-start = (bf16[256,2048]{1,0:T(8,128)(2,1)}, bf16[256,2048]{1,0:T(8,128)(2,1)S(1)}, u32[]{:S(2)}, u32[]{:S(2)}) collective-permute-start(bf16[256,2048]{1,0:T(8,128)(2,1)} %constant_dynamic-slice_fusion.2), channel_id=1, source_target_pairs={{0,1},{1,0},{2,3},{3,2},{4,5},{5,4},{6,7},{7,6},{8,9},{9,8},{10,11... | collective-permute-start | bytes 3145736 | tf_op jit(solution)/shard_map/ppermute | solution.py:28
  4.0 8.5 %collective-permute-start.4 = (bf16[256,2048]{1,0:T(8,128)(2,1)}, bf16[256,2048]{1,0:T(8,128)(2,1)S(1)}, u32[]{:S(2)}, u32[]{:S(2)}) collective-permute-start(bf16[256,2048]{1,0:T(8,128)(2,1)} %constant_dynamic-slice_fusion), channel_id=1, source_target_pairs={{0,1},{1,0},{2,3},{3,2},{4,5},{5,4},{6,7},{7,6},{8,9},{9,8},{10,11... | collective-permute-start | bytes 3145736 | tf_op jit(solution)/shard_map/ppermute | solution.py:28
  5.4 9.1 %collective-permute-start.1 = (bf16[16,2560]{1,0:T(8,128)(2,1)S(1)}, bf16[16,2560]{1,0:T(8,128)(2,1)S(1)}, u32[]{:S(2)}, u32[]{:S(2)}) collective-permute-start(bf16[16,2560]{1,0:T(8,128)(2,1)S(1)} %pad_maximum_fusion), channel_id=1, source_target_pairs={{1,4},{5,8},{9,12},{3,6},{7,10},{11,14},{17,20},{21,24},{25,28},{1... | collective-permute-start | bytes 245768 | tf_op jit(solution)/shard_map/ppermute | solution.py:361
  6.5 8.1 %collective-permute-start.3 = (bf16[256,512]{1,0:T(8,128)(2,1)S(1)}, bf16[256,512]{1,0:T(8,128)(2,1)S(1)}, u32[]{:S(2)}, u32[]{:S(2)}) collective-permute-start(bf16[256,512]{1,0:T(8,128)(2,1)S(1)} %constant_dynamic-slice_fusion.1), channel_id=1, source_target_pairs={{0,1},{1,0},{2,3},{3,2},{4,5},{5,4},{6,7},{7,6},{8,9},{9,8},{10,11... | collective-permute-start | bytes 786440 | tf_op jit(solution)/shard_map/ppermute | solution.py:28
  11.2 3.4 %collective-permute-start.2 = (bf16[16,2560]{1,0:T(8,128)(2,1)}, bf16[16,2560]{1,0:T(8,128)(2,1)S(1)}, u32[]{:S(2)}, u32[]{:S(2)}) collective-permute-start(bf16[16,2560]{1,0:T(8,128)(2,1)} %pad_maximum_fusion.1), channel_id=1, source_target_pairs={{1,5},{5,9},{9,13},{3,7},{7,11},{11,15},{17,21},{21,25},{25,29},{1... | collective-permute-start | bytes 245768 | tf_op jit(solution)/shard_map/ppermute | solution.py:361
  19.9 9.4 %collective-permute-start.7 = (bf16[128,1024]{1,0:T(8,128)(2,1)S(1)}, bf16[128,1024]{1,0:T(8,128)(2,1)S(1)}, u32[]{:S(2)}, u32[]{:S(2)}) collective-permute-start(bf16[128,1024]{1,0:T(8,128)(2,1)S(1)} %get-tuple-element.55), channel_id=1, source_target_pairs={{0,4},{4,8},{8,12},{12,0},{1,5},{5,9},{9,13},{13,1},{2,6},{6,10},{... | collective-permute-start | bytes 786440 | tf_op jit(solution)/shard_map/ppermute | solution.py:396
  26.9 9.7 %collective-permute-start.6 = (bf16[128,1024]{1,0:T(8,128)(2,1)S(1)}, bf16[128,1024]{1,0:T(8,128)(2,1)S(1)}, u32[]{:S(2)}, u32[]{:S(2)}) collective-permute-start(bf16[128,1024]{1,0:T(8,128)(2,1)S(1)} %get-tuple-element.53), channel_id=1, source_target_pairs={{0,4},{4,8},{8,12},{12,0},{1,5},{5,9},{9,13},{13,1},{2,6},{6,10},{... | collective-permute-start | bytes 786440 | tf_op jit(solution)/shard_map/ppermute | solution.py:396
  29.4 14.1 %collective-permute-start.9 = (bf16[128,1024]{1,0:T(8,128)(2,1)S(1)}, bf16[128,1024]{1,0:T(8,128)(2,1)S(1)}, u32[]{:S(2)}, u32[]{:S(2)}) collective-permute-start(bf16[128,1024]{1,0:T(8,128)(2,1)S(1)} %add_convert_fusion.3), channel_id=1, source_target_pairs={{0,4},{4,8},{8,12},{12,0},{1,5},{5,9},{9,13},{13,1},{2,6},{6,10},{... | collective-permute-start | bytes 786440 | tf_op jit(solution)/shard_map/ppermute | solution.py:396
  36.7 11.3 %collective-permute-start.8 = (bf16[128,1024]{1,0:T(8,128)(2,1)S(1)}, bf16[128,1024]{1,0:T(8,128)(2,1)S(1)}, u32[]{:S(2)}, u32[]{:S(2)}) collective-permute-start(bf16[128,1024]{1,0:T(8,128)(2,1)S(1)} %add_convert_fusion.2), channel_id=1, source_target_pairs={{0,4},{4,8},{8,12},{12,0},{1,5},{5,9},{9,13},{13,1},{2,6},{6,10},{... | collective-permute-start | bytes 786440 | tf_op jit(solution)/shard_map/ppermute | solution.py:396
  55.2 3.0 %collective-permute-start.10 = (bf16[256,1536]{1,0:T(8,128)(2,1)S(1)}, bf16[256,1536]{1,0:T(8,128)(2,1)S(1)}, u32[]{:S(2)}, u32[]{:S(2)}) collective-permute-start(bf16[256,1536]{1,0:T(8,128)(2,1)S(1)} %get-tuple-element.80), channel_id=1, source_target_pairs={{0,1},{1,0},{2,3},{3,2},{4,5},{5,4},{6,7},{7,6},{8,9},{9,8},{10,11... | collective-permute-start | bytes 2359304 | tf_op jit(solution)/shard_map/ppermute | solution.py:28
  58.4 20.4 %collective-permute-start.14 = (bf16[256,1536]{1,0:T(8,128)(2,1)S(1)}, bf16[256,1536]{1,0:T(8,128)(2,1)S(1)}, u32[]{:S(2)}, u32[]{:S(2)}) collective-permute-start(bf16[256,1536]{1,0:T(8,128)(2,1)S(1)} %add_convert_fusion), channel_id=1, source_target_pairs={{0,2},{2,0},{1,3},{3,1},{4,6},{6,4},{5,7},{7,5},{8,10},{10,8},{9,1... | collective-permute-start | bytes 2359304 | tf_op jit(solution)/shard_map/ppermute | solution.py:28
  63.5 1.6 %collective-permute-start.11 = (bf16[256,512]{1,0:T(8,128)(2,1)S(1)}, bf16[256,512]{1,0:T(8,128)(2,1)S(1)}, u32[]{:S(2)}, u32[]{:S(2)}) collective-permute-start(bf16[256,512]{1,0:T(8,128)(2,1)S(1)} %get-tuple-element.83), channel_id=1, source_target_pairs={{0,1},{1,0},{2,3},{3,2},{4,5},{5,4},{6,7},{7,6},{8,9},{9,8},{10,11... | collective-permute-start | bytes 786440 | tf_op jit(solution)/shard_map/ppermute | solution.py:28
  65.9 18.2 %collective-permute-start.13 = (bf16[256,512]{1,0:T(8,128)(2,1)}, bf16[256,512]{1,0:T(8,128)(2,1)}, u32[]{:S(2)}, u32[]{:S(2)}) collective-permute-start(bf16[256,512]{1,0:T(8,128)(2,1)} %add_convert_fusion.1), channel_id=1, source_target_pairs={{0,2},{2,0},{1,3},{3,1},{4,6},{6,4},{5,7},{7,5},{8,10},{10,8},{9,1... | collective-permute-start | bytes 786440 | tf_op jit(solution)/shard_map/ppermute | solution.py:28
  75.0 4.4 %collective-permute-start.12 = (bf16[256,2048]{1,0:T(8,128)(2,1)}, bf16[256,2048]{1,0:T(8,128)(2,1)}, u32[]{:S(2)}, u32[]{:S(2)}) collective-permute-start(bf16[256,2048]{1,0:T(8,128)(2,1)} %get-tuple-element.86), channel_id=1, source_target_pairs={{0,1},{1,0},{2,3},{3,2},{4,5},{5,4},{6,7},{7,6},{8,9},{9,8},{10,11... | collective-permute-start | bytes 3145736 | tf_op jit(solution)/shard_map/ppermute | solution.py:28

commit v4 on v3

--- a/solution.py
+++ b/solution.py
@@ -18,10 +18,9 @@
 BF16 = jnp.bfloat16
 
 
-def shifted(shard, axis, by):
+def shifted_ring(shard, axis):
     peers = lax.axis_size(axis)
-    pairs = [(i, i + by) for i in range(peers) if 0 <= i + by < peers]
-    return lax.ppermute(shard, axis, pairs)
+    return lax.ppermute(shard, axis, [(i, (i + 1) % peers) for i in range(peers)])
 
 
 def swapped(shard, axis):
@@ -78,37 +77,26 @@
     return jnp.where((lane >= low) & (lane < low + head_width), 1.0, 0.0).astype(BF16)
 
 
-def convolved(first, docs, pieces, store, taps):
-    count = pieces[0][0].shape[0]
-    rims = pieces[0][1].shape[0]
-    start = doc_start(rows_of(count, first), docs) - first
-    row = lax.broadcasted_iota(jnp.int32, (count, count), 0)
-    col = lax.broadcasted_iota(jnp.int32, (count, count), 1)
-    rim_row = lax.broadcasted_iota(jnp.int32, (rims, rims), 0)
-    rim_col = lax.broadcasted_iota(jnp.int32, (rims, rims), 1) - rims
-    shifts = []
-    for back in range(1, taps):
-        hit = (col == row - back) & (col >= start)
-        rim_hit = (rim_col == rim_row - back) & (rim_col >= start[:rims])
-        shifts.append((jnp.where(hit, 1.0, 0.0).astype(BF16), jnp.where(rim_hit, 1.0, 0.0).astype(BF16)))
-    for index, (x, rim, w, bias) in enumerate(pieces):
-        weights = w[...].astype(F32)
-        if index:
-            weights = jnp.concatenate([weights[:, 0, 0, :], weights[:, 0, 1, :]], axis=1)
-        span = min(256, x.shape[1])
-        for low in range(0, x.shape[1], span):
-            at = slice(low, low + span)
-            value = x[:, at]
-            weight = weights[:, at]
-            summed = bias[:, at] + value.astype(F32) * weight[taps - 1 : taps]
-            top = jnp.zeros((rims, span), F32)
-            for back in range(1, taps):
-                line = weight[taps - 1 - back : taps - back]
-                shift, rim_shift = shifts[back - 1]
-                summed = summed + mm(shift, value) * line
-                top = top + mm(rim_shift, rim[:, at]) * line
-            store(index, at, slice(0, rims), silu(summed[:rims] + top).astype(BF16))
-            store(index, at, slice(rims, count), silu(summed[rims:]).astype(BF16))
+def convolved(shifts, x, rim, w, bias, store, taps):
+    count = x.shape[0]
+    rims = rim.shape[0]
+    weights = w[...].astype(F32)
+    if len(weights.shape) == 4:
+        weights = jnp.concatenate([weights[:, 0, 0, :], weights[:, 0, 1, :]], axis=1)
+    span = min(256, x.shape[1])
+    for low in range(0, x.shape[1], span):
+        at = slice(low, low + span)
+        value = x[:, at]
+        weight = weights[:, at]
+        summed = bias[:, at] + value.astype(F32) * weight[taps - 1 : taps]
+        top = jnp.zeros((rims, span), F32)
+        for back in range(1, taps):
+            line = weight[taps - 1 - back : taps - back]
+            shift, rim_shift = shifts[back - 1]
+            summed = summed + mm(shift[...], value) * line
+            top = top + mm(rim_shift[...], rim[:, at]) * line
+        store(at, slice(0, rims), silu(summed[:rims] + top).astype(BF16))
+        store(at, slice(rims, count), silu(summed[rims:]).astype(BF16))
 
 
 def decay_kernel(
@@ -153,36 +141,52 @@
 
 def state_kernel(
     meta, docs, x, got_x, rim_x, late_rim_x, w, bias, s, got_s, rim_s, late_rim_s, sw, sbias, tail, kept,
-    x_out, bc_out, s_out, d_out, raw_x, raw_s, *, taps, heads, head_width, first_lane,
+    x_out, bc_out, s_out, d_out, raw_x, raw_s, shift, rim_shift, b_turned,
+    *, taps, heads, head_width, first_lane,
 ):
+    step = pl.program_id(0)
     half, width = x.shape
     rims = rim_x.shape[0]
     state_width = bc_out.shape[1] // 2
-    own_at = pl.ds(pl.multiple_of(rims + meta[0] * half, 16), half)
-    got_at = pl.ds(pl.multiple_of(rims + (1 - meta[0]) * half, 16), half)
-    for raw, own, got, rim, late in ((raw_x, x, got_x, rim_x, late_rim_x), (raw_s, s, got_s, rim_s, late_rim_s)):
-        raw[:rims, :] = rim[...] + late[...]
-        raw[own_at, :] = own[...]
-        raw[got_at, :] = got[...]
-    for index in range(2):
-        low = index * half
-
-        def store(piece, at, rows, value, low=low):
-            out = bc_out if piece else x_out
-            out[low + rows.start : low + rows.stop, at] = value
-
-        pieces = []
-        for raw, weight, offset in ((raw_x, w, bias), (raw_s, sw, sbias)):
-            pieces.append((raw.at[low + rims : low + rims + half], raw.at[low : low + rims], weight, offset))
-        convolved(meta[1] + low, docs, pieces, store, taps)
-    b = bc_out[:, :state_width].T
-    span = min(256, width)
-    for low in range(0, width, span):
-        at = slice(low, low + span)
-        tails = mm(tail[...], head_lanes(2, heads, head_width, span, first_lane + low))
-        weighted = (x_out[:, at].astype(F32) * tails).astype(BF16)
-        s_out[:, at] = mm(b, weighted).astype(BF16)
-        d_out[:, at] = mm(kept[...], head_lanes(3, heads, head_width, span, first_lane + low))[:1]
+
+    def mixed(raw, own, got, rim, late, weight, offset, out):
+        raw[:rims, :] = jnp.where(meta[0] == 0, rim[...], late[...])
+        raw[pl.ds(pl.multiple_of(rims + meta[0] * half, 16), half), :] = own[...]
+        raw[pl.ds(pl.multiple_of(rims + (1 - meta[0]) * half, 16), half), :] = got[...]
+        for index in range(2):
+            low = index * half
+
+            def store(at, rows, value, low=low):
+                out[low + rows.start : low + rows.stop, at] = value
+
+            shifts = [(shift.at[index, back], rim_shift.at[index, back]) for back in range(taps - 1)]
+            convolved(
+                shifts, raw.at[low + rims : low + rims + half], raw.at[low : low + rims], weight, offset, store, taps
+            )
+
+    @pl.when(step == 0)
+    def _():
+        row = lax.broadcasted_iota(jnp.int32, (half, half), 0)
+        col = lax.broadcasted_iota(jnp.int32, (half, half), 1)
+        rim_row = lax.broadcasted_iota(jnp.int32, (rims, rims), 0)
+        rim_col = lax.broadcasted_iota(jnp.int32, (rims, rims), 1) - rims
+        for index in range(2):
+            first = meta[1] + index * half
+            start = doc_start(rows_of(half, first), docs) - first
+            for back in range(1, taps):
+                hit = (col == row - back) & (col >= start)
+                rim_hit = (rim_col == rim_row - back) & (rim_col >= start[:rims])
+                shift[index, back - 1] = jnp.where(hit, 1.0, 0.0).astype(BF16)
+                rim_shift[index, back - 1] = jnp.where(rim_hit, 1.0, 0.0).astype(BF16)
+        mixed(raw_s, s, got_s, rim_s, late_rim_s, sw, sbias, bc_out)
+        b_turned[...] = bc_out[:, :state_width].T
+
+    mixed(raw_x, x, got_x, rim_x, late_rim_x, w, bias, x_out)
+    lanes = first_lane + step * width
+    tails = mm(tail[...], head_lanes(2, heads, head_width, width, lanes))
+    weighted = (x_out[...].astype(F32) * tails).astype(BF16)
+    s_out[...] = mm(b_turned[...], weighted).astype(BF16)
+    d_out[...] = mm(kept[...], head_lanes(3, heads, head_width, width, lanes))[:1]
 
 
 def intra_kernel(
@@ -323,7 +327,7 @@
     fixed = lambda *shape: pl.BlockSpec(shape, lambda i, *m: (0,) * len(shape))
     shape_of = jax.ShapeDtypeStruct
 
-    def call(body, name, grid, in_specs, out_specs, out_shape, scratch=(), flops=0, moved=0, prefetch=2):
+    def call(body, name, grid, in_specs, out_specs, out_shape, scratch=(), prefetch=2):
         kernel = pl.pallas_call(
             body,
             grid_spec=pltpu.PrefetchScalarGridSpec(
@@ -332,7 +336,7 @@
             ),
             out_shape=out_shape,
             compiler_params=params,
-            cost_estimate=pl.CostEstimate(flops=0 * flops, bytes_accessed=0 * moved, transcendentals=0),
+            cost_estimate=pl.CostEstimate(flops=0, bytes_accessed=0, transcendentals=0),
             name=name,
         )
         return lambda *operands: kernel(
@@ -349,24 +353,17 @@
         meta, docs, x_input, gate_input, mix_weight, bias, state_weight, s_bias, skip, gain, rate, out_weight
     ]
     rims = 16
-    s_width = parts * block
-    s_half = (lambda v, core: lax.dynamic_slice_in_dim(v, core * s_width, s_width, 1)) if whole_groups else (
-        lambda v, core: v
-    )
-    last_x, last_s = x_input[half - rims :], s_input[half - rims :]
-    flat = 2 * ctx_size
-
-    def rim_for(core):
-        shard = jnp.concatenate([last_x[:, core * width : (core + 1) * width], s_half(last_s, core)], axis=1)
-        return lax.ppermute(shard, ("ctx", "sub"), [(i, i + 1 + core) for i in range(1, flat - 2, 2)])
-
-    rim, late_rim = rim_for(0), rim_for(1)
+    cut_width = min(1024, part_width)
+    cuts = part_width // cut_width
+    s_width = parts * block if whole_groups else groups * block
     raw = step_raw.T
-    got_raw = swapped(raw, "sub")
-    got_x = swapped(lax.dynamic_slice_in_dim(x_input, (1 - sub) * width, width, 1), "sub")
-    got_s = swapped(s_half(s_input, 1 - sub), "sub")
-    got_gate = swapped(lax.dynamic_slice_in_dim(gate_input, (1 - sub) * width, width, 1), "sub")
-    got_gate, got_raw = after(got_gate, got_raw)
+    got_raw, x_later, gate_later = after(swapped(raw, "sub"), x_input, gate_input)
+    got_x = swapped(x_later, "sub")
+    got_s = swapped(s_input, "sub")
+    last_x, last_s = x_input[half - rims :], state_proj[half - rims :].reshape(rims, groups * block)
+    rim = shifted_ring(jnp.concatenate([last_x[:, :width], last_s[:, :s_width]], axis=1), ("ctx", "sub"))
+    late_rim = shifted_ring(jnp.concatenate([last_x[:, width:], last_s[:, -s_width:]], axis=1), "ctx")
+    got_gate = swapped(gate_later, "sub")
     mixed = (x_input, got_x, rim, late_rim, mix_weight, bias, s_input, got_s, rim, late_rim, state_weight, s_bias)
 
     def mix_specs(part):
@@ -375,9 +372,13 @@
         here = lambda m: part
         rim_at = lambda m: width // block + part
         specs = []
-        for size, places in ((part_width, (at, here, here, here, at, at)), (block, (s_at, here, rim_at, rim_at, s_at, s_at))):
-            for rows, place in zip((half, half, rims, rims, taps, 1), places):
-                specs.append(pl.BlockSpec((rows, size), lambda i, m, d, place=place: (0, place(m))))
+        x_at = lambda m, i: at(m) * cuts + i
+        x_here = lambda m, i: here(m) * cuts + i
+        specs = []
+        for rows, place in zip((half, half, rims, rims, taps, 1), (x_at, x_at, x_here, x_here, x_at, x_at)):
+            specs.append(pl.BlockSpec((rows, cut_width), lambda i, m, d, place=place: (0, place(m, i))))
+        for rows, place in zip((half, half, rims, rims, taps, 1), (s_at, s_at, rim_at, rim_at, s_at, s_at)):
+            specs.append(pl.BlockSpec((rows, block), lambda i, m, d, place=place: (0, place(m))))
         specs[10] = pl.BlockSpec((taps, 1, 2, state_width), lambda i, m, d: (0, s_at(m), 0, 0))
         return specs
 
@@ -389,11 +390,8 @@
             shape_of((count, heads), F32), shape_of((heads, count), F32),
             shape_of((count, 2 * heads), BF16), shape_of((8, 3 * heads), BF16),
         ],
-        [pltpu.VMEM((heads, count), F32)], flops=2 * count * count * 128, moved=16 * count * heads,
+        [pltpu.VMEM((heads, count), F32)],
     )(meta, docs, raw, got_raw, rate)
-
-    def onward(shard):
-        return lax.ppermute(shard, "ctx", [(i, (i + 1) % ctx_size) for i in range(ctx_size)])
 
     made = []
     next_meta = meta
@@ -402,21 +400,26 @@
             functools.partial(
                 state_kernel, taps=taps, heads=heads, head_width=head_width, first_lane=part * part_width
             ),
-            "state", (1,),
+            "state", (cuts,),
             mix_specs(part) + [fixed(count, 2 * heads), fixed(8, 3 * heads)],
             [
-                fixed(count, part_width), fixed(count, block), fixed(state_width, part_width), fixed(1, part_width),
+                pl.BlockSpec((count, cut_width), lambda i, m, d: (0, i)), fixed(count, block),
+                pl.BlockSpec((state_width, cut_width), lambda i, m, d: (0, i)),
+                pl.BlockSpec((1, cut_width), lambda i, m, d: (0, i)),
             ],
             [
                 shape_of((count, part_width), BF16), shape_of((count, block), BF16),
                 shape_of((state_width, part_width), BF16), shape_of((1, part_width), F32),
             ],
-            [pltpu.VMEM((rims + count, part_width), BF16), pltpu.VMEM((rims + count, block), BF16)],
-            flops=4 * half * count * part_width, moved=6 * count * part_width,
+            [
+                pltpu.VMEM((rims + count, cut_width), BF16), pltpu.VMEM((rims + count, block), BF16),
+                pltpu.VMEM((2, taps - 1, half, half), BF16), pltpu.VMEM((2, taps - 1, rims, rims), BF16),
+                pltpu.VMEM((state_width, count), BF16),
+            ],
         )(next_meta, docs, *mixed, tail, kept)
         state, next_meta = after(state, next_meta)
         pinned.append(next_meta)
-        made.append([x_cat, bc, state, decay, onward(state)])
+        made.append([x_cat, bc, state, decay, shifted_ring(state, "ctx")])
         if part:
             made[part - 1][4], made[part][0] = after(made[part - 1][4], x_cat)
     ready = []
@@ -428,7 +431,7 @@
         for _ in range(ctx_size // 2 - 1):
             leaving = (state.astype(F32) + decay * arriving.astype(F32)).astype(BF16)
             leaving, x_cat = after(leaving, x_cat)
-            arriving = onward(leaving)
+            arriving = shifted_ring(leaving, "ctx")
         gated, carry_gate = call(
             functools.partial(
                 intra_kernel, head_width=head_width, first_head=part * part_heads, group_heads=part_heads
@@ -437,16 +440,15 @@
             [
                 fixed(count, part_width), fixed(count, block), fixed(count, heads), fixed(heads, count),
                 pl.BlockSpec((half, part_width), lambda i, m, d, part=part: (0, m[0] * parts + part)),
-                pl.BlockSpec((half, part_width), lambda i, m, d, part=part: (0, part)),
+                pl.BlockSpec((half, part_width), lambda i, m, d, part=part: (0, m[0] * parts + part)),
                 fixed(1, all_heads),
             ],
             [fixed(count, part_width), fixed(count, part_width)],
-            [shape_of((count, part_width), F32), shape_of((count, part_width), F32)],
+            [shape_of((count, part_width), F32)] * 2,
             [
                 pltpu.VMEM((state_width, part_width), F32), pltpu.VMEM((3 * heads, part_width), BF16),
                 pltpu.VMEM((CHUNK, part_width), F32), pltpu.VMEM((CHUNK, part_width), F32),
             ],
-            flops=10 * count * part_width * CHUNK, moved=14 * count * part_width,
         )(meta, docs, x_cat, bc, cum, dlt, gate_input, got_gate, skip)
         ready.append((gated, carry_gate, bc, arriving))
 
@@ -462,7 +464,7 @@
                     fixed(state_width, part_width), gain_at(part),
                 ],
                 fixed(count, part_width), shape_of((count, part_width), BF16),
-                flops=2 * count * part_width * state_width, moved=10 * count * part_width, prefetch=1,
+                prefetch=1,
             )(meta, gated, carry_gate, bc, arriving, gain)
         )
 
@@ -480,14 +482,14 @@
     near_blocks = out_cols // mm_cols
     row_specs = [pl.BlockSpec((half, mm_cols), lambda i, m: (0, i))] * 2
 
-    def product(first, blocks, body, name, operands, specs, outs, out_shapes, declared=1):
+    def product(first, blocks, body, name, operands, specs, outs, out_shapes):
         cols = blocks * mm_cols
         return call(
             body, name, (blocks,),
             specs + [pl.BlockSpec((width, mm_cols), lambda i, m: (0, first(m, i)))],
             outs + row_specs,
             out_shapes + [shape_of((half, cols), BF16), shape_of((half, cols), F32)],
-            flops=declared * 2 * count * width * cols, moved=declared * 2 * width * cols, prefetch=1,
+            prefetch=1,
         )(meta, *operands, out_weight)
 
     operands = [*hiddens, gated, carry_gate, bc, arriving, gain, *squares]
@@ -517,7 +519,6 @@
     far_rest = swapped(summed, "tp")
     send, keep = product(
         lambda m, i: m[2] * near_blocks + i, near_blocks, multiply, "product", [hidden], [hidden_spec], [], [],
-        declared=0,
     )
     got = swapped(send, "sub")
 
@@ -539,7 +540,9 @@
 
     early = finish(0, [keep, far_lead], "early", F32, weight=1 << 38)
     output = finish(0, [early, got], "lead", BF16)
-    return finish(lead, [keep, got, far_rest], "rest", BF16, old=(output,))
+    cut = lead * mm_cols
+    last = (keep[:, cut:] + got[:, cut:].astype(F32) + far_rest.astype(F32)).astype(BF16)
+    return lax.dynamic_update_slice(output, last, (0, cut))
 
 
 def solution(mesh):

time: 86.5 us -> 83.2 us (0.962)
  starting transfers between devices: 13.9 us -> 8.69 us
  waiting for transfers between devices: 13.5 us -> 18.7 us
  Pallas kernels: 51 us -> 47.3 us
  other arithmetic: 2.45 us -> 3.62 us
  local copies, waits for them, and re-layouts: 4.82 us -> 3.93 us
    ppermute x9, starting transfers between devices: 8.32 us -> 3.62 us  [swapped(): lax.ppermute(shard, axis, [(i, i ^ 1) for i in range(lax.axis_size(axis))])]
    ppermute x6, waiting for transfers between devices: 4.47 us -> 8.4 us  [shifted_ring(): lax.ppermute(shard, axis, [(i, (i + 1) % peers) for i in range(peers)])]
    dynamic_slice x4 -> x0, local copies, waits for them, and re-layouts: 3.54 us -> none  [the longest x1 2.45 us: local(): lax.dynamic_slice_in_dim(x_input, (1 - sub) * width, width, 1)]
    pallas_call x3 -> x2, Pallas kernels: 5.25 us -> 3.41 us  [finish(): pl.pallas_call(sum_kernel, grid=(blocks,), in_specs=[pl.BlockSpec((half,...]
    dynamic_update_slice x0 -> x1, other arithmetic: none -> 1.84 us  [local(): return lax.dynamic_update_slice(output, last, (0, cut))]
    pallas_call x9, Pallas kernels: 45.7 us -> 43.9 us  [call(): kernel(*(pltpu.with_memory_space_constraint(v, pltpu.HBM) if any((v is p...]
    ppermute x9, waiting for transfers between devices: 9 us -> 10.3 us  [swapped(): lax.ppermute(shard, axis, [(i, i ^ 1) for i in range(lax.axis_size(axis))])]
    reshape x1, local copies, waits for them, and re-layouts: 0.37 us -> 1.4 us  [local(): s_input = state_proj.reshape(half, groups * block)]
  transfers between devices with their start and end apart: 15 -> 15, of which waited for: 7 -> 9; matrix products, arithmetic and copies ran while one was open for 8% -> 6% of each run, Pallas kernels for 43% -> 49%
where the time goes in v4:
time: 83.2 us; the launch traced here: 82.5 us
  Pallas kernels  47.3 us (57%)
  waiting for transfers between devices  18.7 us (22%)
  starting transfers between devices  8.69 us (10%)
  local copies, waits for them, and re-layouts  3.93 us (5%)
  other arithmetic  3.62 us (4%)
    pallas_call x9, Pallas kernels, call(): kernel(*(pltpu.with_memory_space_constraint(v, pltpu.HBM) if any((v is p...  43.9 us
    ppermute x9, waiting for transfers between devices, swapped(): lax.ppermute(shard, axis, [(i, i ^ 1) for i in range(lax.axis_size(axis))])  10.3 us
    ppermute x6, waiting for transfers between devices, shifted_ring(): lax.ppermute(shard, axis, [(i, (i + 1) % peers) for i in range(peers)])  8.4 us
    ppermute x6, starting transfers between devices, shifted_ring(): lax.ppermute(shard, axis, [(i, (i + 1) % peers) for i in range(peers)])  5.07 us
    ppermute x9, starting transfers between devices, swapped(): lax.ppermute(shard, axis, [(i, i ^ 1) for i in range(lax.axis_size(axis))])  3.62 us
    pallas_call x2, Pallas kernels, finish(): pl.pallas_call(sum_kernel, grid=(blocks,), in_specs=[pl.BlockSpec((half,...  3.41 us
    dynamic_update_slice x1, other arithmetic, local(): return lax.dynamic_update_slice(output, last, (0, cut))  1.84 us
  transfers between devices with their start and end apart: 15, of which 9 were waited for; matrix products, arithmetic and copies ran while one was open for 6% of the time, Pallas kernels for 49%

profile of v4, /device:TPU:0, one launch (start us, length us, event | category | flops | bytes accessed | tf_op | source)
XLA Modules:
  0.0 82.5 jit_solution(2999634036362013615)
XLA Ops:
  0.0 0.5 collective-permute-start
  0.5 1.1 %collective-permute-done.got_raw = f32[64,256]{1,0:T(8,128)S(1)} collective-permute-done((f32[64,256]{1,0:T(8,128)}, f32[64,256]{1,0:T(8,128)S(1)}, u32[]{:S(2)}, u32[]{:S(2)}) %collective-permute-start) | collective-permute-done | bytes 65568 | tf_op jit(solution)/shard_map/ppermute | solution.py:27
  2.1 1.4 %reshape.23.s = bf16[256,1024]{1,0:T(8,128)(2,1)S(1)} reshape(bf16[256,4,2,128]{3,2,1,0:T(2,128)(2,1)} %param.15) | data formatting | bytes 1048576 | tf_op jit(solution)/shard_map/reshape | solution.py:346
  3.9 0.8 slice.25
  4.7 0.9 %fusion.1 = (bf16[16,2048]{1,0:T(8,128)(2,1)S(1)}, bf16[16,2048]{1,0:T(8,128)(2,1)S(1)}) fusion(bf16[256,4096]{1,0:T(8,128)(2,1)} %x.3), kind=kLoop, calls=%fused_computation.9 | loop fusion | bytes 262144 | tf_op jit(solution)/shard_map/slice | solution.py:365
  5.8 2.9 %collective-permute-start.3 = (bf16[16,2560]{1,0:T(8,128)(2,1)S(1)}, bf16[16,2560]{1,0:T(8,128)(2,1)S(1)}, u32[]{:S(2)}, u32[]{:S(2)}) collective-permute-start(bf16[16,2560]{1,0:T(8,128)(2,1)S(1)} %pad_maximum_fusion.1), channel_id=1, source_target_pairs={{0,4},{4,8},{8,12},{12,0},{1,5},{5,9},{9,13},{13,1},{2,6},{6,10},{... | collective-permute-start | bytes 245768 | tf_op jit(solution)/shard_map/ppermute | solution.py:23
  8.8 0.6 pad_add_fusion.meta
  9.4 0.8 %copy-done = f32[256,64]{0,1:T(8,128)S(1)} copy-done((f32[256,64]{0,1:T(8,128)S(1)}, f32[256,64]{0,1:T(8,128)}, u32[]{:S(2)}) %copy-start) | copy-done | bytes 65560
  10.2 2.1 %decay.1 = (f32[512,32]{1,0:T(8,128)S(1)}, f32[32,512]{1,0:T(8,128)S(1)}, bf16[512,64]{1,0:T(8,128)(2,1)S(1)}, bf16[8,96]{1,0:T(8,128)(2,1)S(1)}) custom-call(s32[3]{0:T(128)} %pad_add_fusion.meta, s32[8]{0:T(128)} %docs.9, f32[64,256]{1,0:T(8,128)S(1)} %bitcast.12, f32[64,256]{1,0:T(8,128)S(1)} %collective-permute-done.got_raw, f32[1,64]{1,0:T(1,128)} %bitcast.23), custom_call_target="tpu_custom_call" | custom-call | tf_op jit(solution)/shard_map/decay/pallas_call | solution.py:342
  12.3 0.5 collective-permute-done.2.rim_x.rim_s
  12.7 1.2 %collective-permute-done.3.late_rim_x.late_rim_s = bf16[16,2560]{1,0:T(8,128)(2,1)S(1)} collective-permute-done((bf16[16,2560]{1,0:T(8,128)(2,1)S(1)}, bf16[16,2560]{1,0:T(8,128)(2,1)S(1)}, u32[]{:S(2)}, u32[]{:S(2)}) %collective-permute-start.3) | collective-permute-done | bytes 81952 | tf_op jit(solution)/shard_map/ppermute | solution.py:23
  13.9 4.4 %state.2 = (bf16[512,1024]{1,0:T(8,128)(2,1)S(1)}, bf16[512,256]{1,0:T(8,128)(2,1)S(1)}, bf16[128,1024]{1,0:T(8,128)(2,1)S(1)}, f32[1,1024]{1,0:T(1,128)S(1)}) custom-call(s32[3]{0:T(128)} %pad_add_fusion.meta, s32[8]{0:T(128)} %docs.9, bf16[256,4096]{1,0:T(8,128)(2,1)} %x.3, bf16[256,4096]{1,0:T(8,128)(2,1)} %collective-permute-done.1.got_x, ...), custom_call_target="tpu_custom_call" | custom-call | tf_op jit(solution)/shard_map/state/pallas_call | solution.py:342
  18.4 4.4 %state.3 = (bf16[512,1024]{1,0:T(8,128)(2,1)S(1)}, bf16[512,256]{1,0:T(8,128)(2,1)S(1)}, bf16[128,1024]{1,0:T(8,128)(2,1)S(1)}, f32[1,1024]{1,0:T(1,128)S(1)}) custom-call(s32[3]{0:T(128)} %pad_add_fusion.meta, s32[8]{0:T(128)} %docs.9, bf16[256,4096]{1,0:T(8,128)(2,1)} %x.3, bf16[256,4096]{1,0:T(8,128)(2,1)} %collective-permute-done.1.got_x, ...), custom_call_target="tpu_custom_call" | custom-call | tf_op jit(solution)/shard_map/state/pallas_call | solution.py:342
  22.8 1.6 %collective-permute-start.5 = (bf16[128,1024]{1,0:T(8,128)(2,1)S(1)}, bf16[128,1024]{1,0:T(8,128)(2,1)S(1)}, u32[]{:S(2)}, u32[]{:S(2)}) collective-permute-start(bf16[128,1024]{1,0:T(8,128)(2,1)S(1)} %get-tuple-element.55), channel_id=1, source_target_pairs={{0,4},{4,8},{8,12},{12,0},{1,5},{5,9},{9,13},{13,1},{2,6},{6,10},{... | collective-permute-start | bytes 786440 | tf_op jit(solution)/shard_map/ppermute | solution.py:23
  24.4 4.7 %collective-permute-done.6 = bf16[128,1024]{1,0:T(8,128)(2,1)S(1)} collective-permute-done((bf16[128,1024]{1,0:T(8,128)(2,1)S(1)}, bf16[128,1024]{1,0:T(8,128)(2,1)S(1)}, u32[]{:S(2)}, u32[]{:S(2)}) %collective-permute-start.6) | collective-permute-done | bytes 262176 | tf_op jit(solution)/shard_map/ppermute | solution.py:23
  29.3 5.9 %intra.2 = (f32[512,1024]{1,0:T(8,128)S(1)}, f32[512,1024]{1,0:T(8,128)S(1)}) custom-call(s32[3]{0:T(128)} %pad_add_fusion.meta, s32[8]{0:T(128)} %docs.9, bf16[512,1024]{1,0:T(8,128)(2,1)S(1)} %get-tuple-element.62.x_all, bf16[512,256]{1,0:T(8,128)(2,1)S(1)} %get-tuple-element.63.bc_all.bc, f32[512,32]{1,0:T(8,128)S(1)} %get-tuple-element.64.cum_all, ...), custom_call_target="tpu_custom_call" | custom-call | tf_op jit(solution)/shard_map/intra/pallas_call | solution.py:342
  35.5 5.9 %intra.3 = (f32[512,1024]{1,0:T(8,128)S(1)}, f32[512,1024]{1,0:T(8,128)S(1)}) custom-call(s32[3]{0:T(128)} %pad_add_fusion.meta, s32[8]{0:T(128)} %docs.9, bf16[512,1024]{1,0:T(8,128)(2,1)S(1)} %get-tuple-element.75.x_all, bf16[512,256]{1,0:T(8,128)(2,1)S(1)} %get-tuple-element.76.bc_all.refs_3_, f32[512,32]{1,0:T(8,128)S(1)} %get-tuple-element.64.cum_all, ...), custom_call_target="tpu_custom_call" | custom-call | tf_op jit(solution)/shard_map/intra/pallas_call | solution.py:342
  41.4 2.0 %norm.1.refs_0_ = bf16[512,1024]{1,0:T(8,128)(2,1)S(1)} custom-call(s32[3]{0:T(128)} %pad_add_fusion.meta, f32[512,1024]{1,0:T(8,128)S(1)} %get-tuple-element.71.a, f32[512,1024]{1,0:T(8,128)S(1)} %get-tuple-element.72.f, bf16[512,256]{1,0:T(8,128)(2,1)S(1)} %get-tuple-element.63.bc_all.bc, bf16[128,1024]{1,0:T(8,128)(2,1)S(1)} %collective-permute-done.9.incoming, ...), custom_call_target="tpu_custom_call" | custom-call | tf_op jit(solution)/shard_map/norm/pallas_call | solution.py:342
  43.4 2.0 %collective-permute-done.8.refs_4_ = bf16[128,1024]{1,0:T(8,128)(2,1)S(1)} collective-permute-done((bf16[128,1024]{1,0:T(8,128)(2,1)S(1)}, bf16[128,1024]{1,0:T(8,128)(2,1)S(1)}, u32[]{:S(2)}, u32[]{:S(2)}) %collective-permute-start.8) | collective-permute-done | bytes 262176 | tf_op jit(solution)/shard_map/ppermute | solution.py:23
  45.4 7.2 %project.1 = (bf16[512,2048]{1,0:T(8,128)(2,1)S(1)}, bf16[256,1536]{1,0:T(8,128)(2,1)S(1)}, f32[256,1536]{1,0:T(8,128)S(1)}) custom-call(s32[3]{0:T(128)} %pad_add_fusion.meta, bf16[512,1024]{1,0:T(8,128)(2,1)S(1)} %norm.1.refs_0_, f32[512,1024]{1,0:T(8,128)S(1)} %get-tuple-element.77.refs_1_, f32[512,1024]{1,0:T(8,128)S(1)} %get-tuple-element.78.refs_2_, ...), custom_call_target="tpu_custom_call" | custom-call | tf_op jit(solution)/shard_map/project/pallas_call | solution.py:342
  52.8 2.3 %collective-permute-done.10 = bf16[256,1536]{1,0:T(8,128)(2,1)S(1)} collective-permute-done((bf16[256,1536]{1,0:T(8,128)(2,1)S(1)}, bf16[256,1536]{1,0:T(8,128)(2,1)S(1)}, u32[]{:S(2)}, u32[]{:S(2)}) %collective-permute-start.10) | collective-permute-done | bytes 786464 | tf_op jit(solution)/shard_map/ppermute | solution.py:27
  55.3 1.6 %collective-permute-start.12 = (bf16[256,1536]{1,0:T(8,128)(2,1)S(1)}, bf16[256,1536]{1,0:T(8,128)(2,1)S(1)}, u32[]{:S(2)}, u32[]{:S(2)}) collective-permute-start(bf16[256,1536]{1,0:T(8,128)(2,1)S(1)} %add_convert_fusion), channel_id=1, source_target_pairs={{0,2},{2,0},{1,3},{3,1},{4,6},{6,4},{5,7},{7,5},{8,10},{10,8},{9,1... | collective-permute-start | bytes 2359304 | tf_op jit(solution)/shard_map/ppermute | solution.py:27
  56.9 3.5 %product.2 = (bf16[256,512]{1,0:T(8,128)(2,1)S(1)}, f32[256,512]{1,0:T(8,128)S(1)}) custom-call(s32[3]{0:T(128)} %pad_add_fusion.meta, bf16[512,2048]{1,0:T(8,128)(2,1)S(1)} %get-tuple-element.86.hidden, bf16[2048,4096]{1,0:T(8,128)(2,1)} %w.7), custom_call_target="tpu_custom_call" | custom-call | tf_op jit(solution)/shard_map/product/pallas_call | solution.py:342
  60.5 1.5 %collective-permute-done.11 = bf16[256,512]{1,0:T(8,128)(2,1)S(1)} collective-permute-done((bf16[256,512]{1,0:T(8,128)(2,1)S(1)}, bf16[256,512]{1,0:T(8,128)(2,1)S(1)}, u32[]{:S(2)}, u32[]{:S(2)}) %collective-permute-start.11) | collective-permute-done | bytes 262176 | tf_op jit(solution)/shard_map/ppermute | solution.py:27
  62.0 0.8 add_convert_fusion.2
  62.7 0.5 collective-permute-start.14
  63.2 8.6 %product.3 = (bf16[256,2048]{1,0:T(8,128)(2,1)}, f32[256,2048]{1,0:T(8,128)S(1)}) custom-call(s32[3]{0:T(128)} %pad_add_fusion.meta, bf16[512,2048]{1,0:T(8,128)(2,1)S(1)} %get-tuple-element.86.hidden, bf16[2048,4096]{1,0:T(8,128)(2,1)} %w.7), custom_call_target="tpu_custom_call" | custom-call | tf_op jit(solution)/shard_map/product/pallas_call | solution.py:342
  71.8 3.9 %collective-permute-done.12.refs_1_ = bf16[256,1536]{1,0:T(8,128)(2,1)S(1)} collective-permute-done((bf16[256,1536]{1,0:T(8,128)(2,1)S(1)}, bf16[256,1536]{1,0:T(8,128)(2,1)S(1)}, u32[]{:S(2)}, u32[]{:S(2)}) %collective-permute-start.12) | collective-permute-done | bytes 786464 | tf_op jit(solution)/shard_map/ppermute | solution.py:27
  75.7 0.5 early.1.refs_0_
  76.2 2.9 %lead.1 = bf16[256,2048]{1,0:T(8,128)(2,1)} custom-call(f32[256,1536]{1,0:T(8,128)S(1)} %early.1.refs_0_, bf16[256,2048]{1,0:T(8,128)(2,1)} %collective-permute-done.13.refs_1_), custom_call_target="tpu_custom_call" | custom-call | tf_op jit(solution)/shard_map/lead/pallas_call | solution.py:529
  79.1 1.5 %collective-permute-done.14 = bf16[256,512]{1,0:T(8,128)(2,1)} collective-permute-done((bf16[256,512]{1,0:T(8,128)(2,1)}, bf16[256,512]{1,0:T(8,128)(2,1)}, u32[]{:S(2)}, u32[]{:S(2)}) %collective-permute-start.14) | collective-permute-done | bytes 262176 | tf_op jit(solution)/shard_map/ppermute | solution.py:27
  80.6 1.8 %fusion = bf16[256,2048]{1,0:T(8,128)(2,1)} fusion(bf16[256,2048]{1,0:T(8,128)(2,1)} %lead.1, bf16[256,512]{1,0:T(8,128)(2,1)} %collective-permute-done.14, f32[256,2048]{1,0:T(8,128)S(1)} %get-tuple-element.87.refs_0_, bf16[256,2048]{1,0:T(8,128)(2,1)} %collective-permute-done.13.refs_1_), kind=kLoop, calls=%fused_computation.5 | loop fusion | flops 655360 | bytes 1310720 | tf_op jit(solution)/shard_map/dynamic_update_slice | solution.py:545
  (24 shorter events, 2.1 us)
Async XLA Ops:
  0.0 1.6 %collective-permute-start = (f32[64,256]{1,0:T(8,128)}, f32[64,256]{1,0:T(8,128)S(1)}, u32[]{:S(2)}, u32[]{:S(2)}) collective-permute-start(f32[64,256]{1,0:T(8,128)} %bitcast.11), channel_id=1, source_target_pairs={{0,1},{1,0},{2,3},{3,2},{4,5},{5,4},{6,7},{7,6},{8,9},{9,8},{10,11... | collective-permute-start | bytes 196616 | tf_op jit(solution)/shard_map/ppermute | solution.py:27
  1.6 12.4 %collective-permute-start.1 = (bf16[256,4096]{1,0:T(8,128)(2,1)}, bf16[256,4096]{1,0:T(8,128)(2,1)}, u32[]{:S(2)}, u32[]{:S(2)}) collective-permute-start(bf16[256,4096]{1,0:T(8,128)(2,1)} %x.3), channel_id=1, source_target_pairs={{0,1},{1,0},{2,3},{3,2},{4,5},{5,4},{6,7},{7,6},{8,9},{9,8},{10,11... | collective-permute-start | bytes 6291464 | tf_op jit(solution)/shard_map/ppermute | solution.py:27
  1.9 27.4 %collective-permute-start.7 = (bf16[256,4096]{1,0:T(8,128)(2,1)}, bf16[256,4096]{1,0:T(8,128)(2,1)S(1)}, u32[]{:S(2)}, u32[]{:S(2)}) collective-permute-start(bf16[256,4096]{1,0:T(8,128)(2,1)} %gate_own.3), channel_id=1, source_target_pairs={{0,1},{1,0},{2,3},{3,2},{4,5},{5,4},{6,7},{7,6},{8,9},{9,8},{10,11... | collective-permute-start | bytes 6291464 | tf_op jit(solution)/shard_map/ppermute | solution.py:27
  3.5 10.4 %collective-permute-start.4 = (bf16[256,1024]{1,0:T(8,128)(2,1)S(1)}, bf16[256,1024]{1,0:T(8,128)(2,1)S(1)}, u32[]{:S(2)}, u32[]{:S(2)}) collective-permute-start(bf16[256,1024]{1,0:T(8,128)(2,1)S(1)} %reshape.23.s), channel_id=1, source_target_pairs={{0,1},{1,0},{2,3},{3,2},{4,5},{5,4},{6,7},{7,6},{8,9},{9,8},{10,11... | collective-permute-start | bytes 1572872 | tf_op jit(solution)/shard_map/ppermute | solution.py:27
  5.6 7.1 %collective-permute-start.2 = (bf16[16,2560]{1,0:T(8,128)(2,1)S(1)}, bf16[16,2560]{1,0:T(8,128)(2,1)S(1)}, u32[]{:S(2)}, u32[]{:S(2)}) collective-permute-start(bf16[16,2560]{1,0:T(8,128)(2,1)S(1)} %pad_maximum_fusion), channel_id=1, source_target_pairs={{0,1},{1,4},{4,5},{5,8},{8,9},{9,12},{12,13},{13,0},{2,3},{3,6},{6... | collective-permute-start | bytes 245768 | tf_op jit(solution)/shard_map/ppermute | solution.py:23
  5.8 8.1 %collective-permute-start.3 = (bf16[16,2560]{1,0:T(8,128)(2,1)S(1)}, bf16[16,2560]{1,0:T(8,128)(2,1)S(1)}, u32[]{:S(2)}, u32[]{:S(2)}) collective-permute-start(bf16[16,2560]{1,0:T(8,128)(2,1)S(1)} %pad_maximum_fusion.1), channel_id=1, source_target_pairs={{0,4},{4,8},{8,12},{12,0},{1,5},{5,9},{9,13},{13,1},{2,6},{6,10},{... | collective-permute-start | bytes 245768 | tf_op jit(solution)/shard_map/ppermute | solution.py:23
  9.4 0.8 %copy-start = (f32[256,64]{0,1:T(8,128)S(1)}, f32[256,64]{0,1:T(8,128)}, u32[]{:S(2)}) copy-start(f32[256,64]{0,1:T(8,128)} %param.20) | copy-start | bytes 196612
  18.4 10.8 %collective-permute-start.6 = (bf16[128,1024]{1,0:T(8,128)(2,1)S(1)}, bf16[128,1024]{1,0:T(8,128)(2,1)S(1)}, u32[]{:S(2)}, u32[]{:S(2)}) collective-permute-start(bf16[128,1024]{1,0:T(8,128)(2,1)S(1)} %get-tuple-element.57), channel_id=1, source_target_pairs={{0,4},{4,8},{8,12},{12,0},{1,5},{5,9},{9,13},{13,1},{2,6},{6,10},{... | collective-permute-start | bytes 786440 | tf_op jit(solution)/shard_map/ppermute | solution.py:23
  22.8 12.4 %collective-permute-start.5 = (bf16[128,1024]{1,0:T(8,128)(2,1)S(1)}, bf16[128,1024]{1,0:T(8,128)(2,1)S(1)}, u32[]{:S(2)}, u32[]{:S(2)}) collective-permute-start(bf16[128,1024]{1,0:T(8,128)(2,1)S(1)} %get-tuple-element.55), channel_id=1, source_target_pairs={{0,4},{4,8},{8,12},{12,0},{1,5},{5,9},{9,13},{13,1},{2,6},{6,10},{... | collective-permute-start | bytes 786440 | tf_op jit(solution)/shard_map/ppermute | solution.py:23
  29.2 12.2 %collective-permute-start.9 = (bf16[128,1024]{1,0:T(8,128)(2,1)S(1)}, bf16[128,1024]{1,0:T(8,128)(2,1)S(1)}, u32[]{:S(2)}, u32[]{:S(2)}) collective-permute-start(bf16[128,1024]{1,0:T(8,128)(2,1)S(1)} %add_convert_fusion.4), channel_id=1, source_target_pairs={{0,4},{4,8},{8,12},{12,0},{1,5},{5,9},{9,13},{13,1},{2,6},{6,10},{... | collective-permute-start | bytes 786440 | tf_op jit(solution)/shard_map/ppermute | solution.py:23
  35.3 10.2 %collective-permute-start.8 = (bf16[128,1024]{1,0:T(8,128)(2,1)S(1)}, bf16[128,1024]{1,0:T(8,128)(2,1)S(1)}, u32[]{:S(2)}, u32[]{:S(2)}) collective-permute-start(bf16[128,1024]{1,0:T(8,128)(2,1)S(1)} %add_convert_fusion.3), channel_id=1, source_target_pairs={{0,4},{4,8},{8,12},{12,0},{1,5},{5,9},{9,13},{13,1},{2,6},{6,10},{... | collective-permute-start | bytes 786440 | tf_op jit(solution)/shard_map/ppermute | solution.py:23
  52.7 2.4 %collective-permute-start.10 = (bf16[256,1536]{1,0:T(8,128)(2,1)S(1)}, bf16[256,1536]{1,0:T(8,128)(2,1)S(1)}, u32[]{:S(2)}, u32[]{:S(2)}) collective-permute-start(bf16[256,1536]{1,0:T(8,128)(2,1)S(1)} %get-tuple-element.82), channel_id=1, source_target_pairs={{0,1},{1,0},{2,3},{3,2},{4,5},{5,4},{6,7},{7,6},{8,9},{9,8},{10,11... | collective-permute-start | bytes 2359304 | tf_op jit(solution)/shard_map/ppermute | solution.py:27
  55.3 20.4 %collective-permute-start.12 = (bf16[256,1536]{1,0:T(8,128)(2,1)S(1)}, bf16[256,1536]{1,0:T(8,128)(2,1)S(1)}, u32[]{:S(2)}, u32[]{:S(2)}) collective-permute-start(bf16[256,1536]{1,0:T(8,128)(2,1)S(1)} %add_convert_fusion), channel_id=1, source_target_pairs={{0,2},{2,0},{1,3},{3,1},{4,6},{6,4},{5,7},{7,5},{8,10},{10,8},{9,1... | collective-permute-start | bytes 2359304 | tf_op jit(solution)/shard_map/ppermute | solution.py:27
  60.4 1.6 %collective-permute-start.11 = (bf16[256,512]{1,0:T(8,128)(2,1)S(1)}, bf16[256,512]{1,0:T(8,128)(2,1)S(1)}, u32[]{:S(2)}, u32[]{:S(2)}) collective-permute-start(bf16[256,512]{1,0:T(8,128)(2,1)S(1)} %get-tuple-element.85), channel_id=1, source_target_pairs={{0,1},{1,0},{2,3},{3,2},{4,5},{5,4},{6,7},{7,6},{8,9},{9,8},{10,11... | collective-permute-start | bytes 786440 | tf_op jit(solution)/shard_map/ppermute | solution.py:27
  62.7 17.9 %collective-permute-start.14 = (bf16[256,512]{1,0:T(8,128)(2,1)}, bf16[256,512]{1,0:T(8,128)(2,1)}, u32[]{:S(2)}, u32[]{:S(2)}) collective-permute-start(bf16[256,512]{1,0:T(8,128)(2,1)} %add_convert_fusion.2), channel_id=1, source_target_pairs={{0,2},{2,0},{1,3},{3,1},{4,6},{6,4},{5,7},{7,5},{8,10},{10,8},{9,1... | collective-permute-start | bytes 786440 | tf_op jit(solution)/shard_map/ppermute | solution.py:27
  71.8 4.4 %collective-permute-start.13 = (bf16[256,2048]{1,0:T(8,128)(2,1)}, bf16[256,2048]{1,0:T(8,128)(2,1)}, u32[]{:S(2)}, u32[]{:S(2)}) collective-permute-start(bf16[256,2048]{1,0:T(8,128)(2,1)} %get-tuple-element.89), channel_id=1, source_target_pairs={{0,1},{1,0},{2,3},{3,2},{4,5},{5,4},{6,7},{7,6},{8,9},{9,8},{10,11... | collective-permute-start | bytes 3145736 | tf_op jit(solution)/shard_map/ppermute | solution.py:27

commit v5 on v4

--- a/solution.py
+++ b/solution.py
@@ -283,10 +283,10 @@
 
 def multiply(meta, hidden, w, send, keep):
     half = send.shape[0]
-    product = mm(hidden[...], w[...])
-    mine = meta[0] == 0
-    send[...] = jnp.where(mine, product[half:], product[:half]).astype(BF16)
-    keep[...] = jnp.where(mine, product[:half], product[half:])
+    there = pl.ds(pl.multiple_of((1 - meta[0]) * half, half), half)
+    here = pl.ds(pl.multiple_of(meta[0] * half, half), half)
+    send[...] = mm(hidden[there, :], w[...]).astype(BF16)
+    keep[...] = mm(hidden[here, :], w[...])
 
 
 def sum_kernel(*refs):
@@ -357,12 +357,17 @@
     cuts = part_width // cut_width
     s_width = parts * block if whole_groups else groups * block
     raw = step_raw.T
-    got_raw, x_later, gate_later = after(swapped(raw, "sub"), x_input, gate_input)
+    pinned.append(raw)
+    last_x, last_s = x_input[half - rims :], state_proj[half - rims :].reshape(rims, groups * block)
+    early_rows = jnp.concatenate([last_x[:, :width], last_s[:, :s_width]], axis=1)
+    late_rows = jnp.concatenate([last_x[:, width:], last_s[:, -s_width:]], axis=1)
+    got_raw, early_rows, late_rows, x_later, gate_later = after(
+        swapped(raw, "sub"), early_rows, late_rows, x_input, gate_input
+    )
+    rim = shifted_ring(early_rows, ("ctx", "sub"))
+    late_rim = shifted_ring(late_rows, "ctx")
     got_x = swapped(x_later, "sub")
     got_s = swapped(s_input, "sub")
-    last_x, last_s = x_input[half - rims :], state_proj[half - rims :].reshape(rims, groups * block)
-    rim = shifted_ring(jnp.concatenate([last_x[:, :width], last_s[:, :s_width]], axis=1), ("ctx", "sub"))
-    late_rim = shifted_ring(jnp.concatenate([last_x[:, width:], last_s[:, -s_width:]], axis=1), "ctx")
     got_gate = swapped(gate_later, "sub")
     mixed = (x_input, got_x, rim, late_rim, mix_weight, bias, s_input, got_s, rim, late_rim, state_weight, s_bias)
 

time: 83.2 us -> 81.8 us (0.983)
  local copies, waits for them, and re-layouts: 3.93 us -> 3.09 us
    unnamed x2 -> x0, local copies, waits for them, and re-layouts: 0.84 us -> none
  transfers between devices with their start and end apart: 15 -> 15, of which waited for: 9 -> 8; matrix products, arithmetic and copies ran while one was open for 6% -> 6% of each run, Pallas kernels for 49% -> 49%
where the time goes in v5:
time: 81.8 us; the launch traced here: 81 us
  Pallas kernels  46.8 us (57%)
  waiting for transfers between devices  18.1 us (22%)
  starting transfers between devices  9.23 us (11%)
  other arithmetic  3.58 us (4%)
  local copies, waits for them, and re-layouts  3.09 us (4%)
    pallas_call x9, Pallas kernels, call(): kernel(*(pltpu.with_memory_space_constraint(v, pltpu.HBM) if any((v is p...  43.4 us
    ppermute x9, waiting for transfers between devices, swapped(): lax.ppermute(shard, axis, [(i, i ^ 1) for i in range(lax.axis_size(axis))])  9.87 us
    ppermute x6, waiting for transfers between devices, shifted_ring(): lax.ppermute(shard, axis, [(i, (i + 1) % peers) for i in range(peers)])  8.27 us
    ppermute x6, starting transfers between devices, shifted_ring(): lax.ppermute(shard, axis, [(i, (i + 1) % peers) for i in range(peers)])  5.82 us
    ppermute x9, starting transfers between devices, swapped(): lax.ppermute(shard, axis, [(i, i ^ 1) for i in range(lax.axis_size(axis))])  3.41 us
    pallas_call x2, Pallas kernels, finish(): pl.pallas_call(sum_kernel, grid=(blocks,), in_specs=[pl.BlockSpec((half,...  3.41 us
    dynamic_update_slice x1, other arithmetic, local(): return lax.dynamic_update_slice(output, last, (0, cut))  1.84 us
  transfers between devices with their start and end apart: 15, of which 8 were waited for; matrix products, arithmetic and copies ran while one was open for 6% of the time, Pallas kernels for 49%

profile of v5, /device:TPU:0, one launch (start us, length us, event | category | flops | bytes accessed | tf_op | source)
XLA Modules:
  0.0 81.0 jit_solution(12830149504980853120)
XLA Ops:
  0.0 0.5 collective-permute-start
  0.5 0.8 slice.25
  1.3 0.9 %fusion.1 = (bf16[16,2048]{1,0:T(8,128)(2,1)S(1)}, bf16[16,2048]{1,0:T(8,128)(2,1)S(1)}) fusion(bf16[256,4096]{1,0:T(8,128)(2,1)} %x.3), kind=kLoop, calls=%fused_computation.9 | loop fusion | bytes 262144 | tf_op jit(solution)/shard_map/slice | solution.py:363
  2.3 0.5 collective-permute-start.7
  2.8 1.4 %reshape.23.s = bf16[256,1024]{1,0:T(8,128)(2,1)S(1)} reshape(bf16[256,4,2,128]{3,2,1,0:T(2,128)(2,1)} %param.15) | data formatting | bytes 1048576 | tf_op jit(solution)/shard_map/reshape | solution.py:346
  4.3 0.4 collective-permute-start.2
  4.8 2.7 %collective-permute-start.3 = (bf16[16,2560]{1,0:T(8,128)(2,1)S(1)}, bf16[16,2560]{1,0:T(8,128)(2,1)S(1)}, u32[]{:S(2)}, u32[]{:S(2)}) collective-permute-start(bf16[16,2560]{1,0:T(8,128)(2,1)S(1)} %get-tuple-element.52), channel_id=1, source_target_pairs={{0,4},{4,8},{8,12},{12,0},{1,5},{5,9},{9,13},{13,1},{2,6},{6,10},{... | collective-permute-start | bytes 245768 | tf_op jit(solution)/shard_map/ppermute | solution.py:23
  7.4 0.6 pad_add_fusion.meta
  8.0 2.2 %decay.1 = (f32[512,32]{1,0:T(8,128)S(1)}, f32[32,512]{1,0:T(8,128)S(1)}, bf16[512,64]{1,0:T(8,128)(2,1)S(1)}, bf16[8,96]{1,0:T(8,128)(2,1)S(1)}) custom-call(s32[3]{0:T(128)} %pad_add_fusion.meta, s32[8]{0:T(128)} %docs.9, f32[64,256]{1,0:T(8,128)} %bitcast.16, f32[64,256]{1,0:T(8,128)S(1)} %collective-permute-done.got_raw, f32[1,64]{1,0:T(1,128)} %bitcast.23), custom_call_target="tpu_custom_call" | custom-call | tf_op jit(solution)/shard_map/decay/pallas_call | solution.py:342
  10.3 1.1 %collective-permute-done.2.rim_x.rim_s = bf16[16,2560]{1,0:T(8,128)(2,1)S(1)} collective-permute-done((bf16[16,2560]{1,0:T(8,128)(2,1)S(1)}, bf16[16,2560]{1,0:T(8,128)(2,1)S(1)}, u32[]{:S(2)}, u32[]{:S(2)}) %collective-permute-start.2) | collective-permute-done | bytes 81952 | tf_op jit(solution)/shard_map/ppermute | solution.py:23
  11.4 0.9 %collective-permute-done.3.late_rim_x.late_rim_s = bf16[16,2560]{1,0:T(8,128)(2,1)S(1)} collective-permute-done((bf16[16,2560]{1,0:T(8,128)(2,1)S(1)}, bf16[16,2560]{1,0:T(8,128)(2,1)S(1)}, u32[]{:S(2)}, u32[]{:S(2)}) %collective-permute-start.3) | collective-permute-done | bytes 81952 | tf_op jit(solution)/shard_map/ppermute | solution.py:23
  12.3 4.4 %state.2 = (bf16[512,1024]{1,0:T(8,128)(2,1)S(1)}, bf16[512,256]{1,0:T(8,128)(2,1)S(1)}, bf16[128,1024]{1,0:T(8,128)(2,1)S(1)}, f32[1,1024]{1,0:T(1,128)S(1)}) custom-call(s32[3]{0:T(128)} %pad_add_fusion.meta, s32[8]{0:T(128)} %docs.9, bf16[256,4096]{1,0:T(8,128)(2,1)} %x.3, bf16[256,4096]{1,0:T(8,128)(2,1)} %collective-permute-done.1.got_x, ...), custom_call_target="tpu_custom_call" | custom-call | tf_op jit(solution)/shard_map/state/pallas_call | solution.py:342
  16.7 0.8 %collective-permute-start.6 = (bf16[128,1024]{1,0:T(8,128)(2,1)S(1)}, bf16[128,1024]{1,0:T(8,128)(2,1)S(1)}, u32[]{:S(2)}, u32[]{:S(2)}) collective-permute-start(bf16[128,1024]{1,0:T(8,128)(2,1)S(1)} %get-tuple-element.61), channel_id=1, source_target_pairs={{0,4},{4,8},{8,12},{12,0},{1,5},{5,9},{9,13},{13,1},{2,6},{6,10},{... | collective-permute-start | bytes 786440 | tf_op jit(solution)/shard_map/ppermute | solution.py:23
  17.5 4.4 %state.3 = (bf16[512,1024]{1,0:T(8,128)(2,1)S(1)}, bf16[512,256]{1,0:T(8,128)(2,1)S(1)}, bf16[128,1024]{1,0:T(8,128)(2,1)S(1)}, f32[1,1024]{1,0:T(1,128)S(1)}) custom-call(s32[3]{0:T(128)} %pad_add_fusion.meta, s32[8]{0:T(128)} %docs.9, bf16[256,4096]{1,0:T(8,128)(2,1)} %x.3, bf16[256,4096]{1,0:T(8,128)(2,1)} %collective-permute-done.1.got_x, ...), custom_call_target="tpu_custom_call" | custom-call | tf_op jit(solution)/shard_map/state/pallas_call | solution.py:342
  21.9 1.6 %collective-permute-start.5 = (bf16[128,1024]{1,0:T(8,128)(2,1)S(1)}, bf16[128,1024]{1,0:T(8,128)(2,1)S(1)}, u32[]{:S(2)}, u32[]{:S(2)}) collective-permute-start(bf16[128,1024]{1,0:T(8,128)(2,1)S(1)} %get-tuple-element.59), channel_id=1, source_target_pairs={{0,4},{4,8},{8,12},{12,0},{1,5},{5,9},{9,13},{13,1},{2,6},{6,10},{... | collective-permute-start | bytes 786440 | tf_op jit(solution)/shard_map/ppermute | solution.py:23
  23.5 4.1 %collective-permute-done.6 = bf16[128,1024]{1,0:T(8,128)(2,1)S(1)} collective-permute-done((bf16[128,1024]{1,0:T(8,128)(2,1)S(1)}, bf16[128,1024]{1,0:T(8,128)(2,1)S(1)}, u32[]{:S(2)}, u32[]{:S(2)}) %collective-permute-start.6) | collective-permute-done | bytes 262176 | tf_op jit(solution)/shard_map/ppermute | solution.py:23
  27.8 5.9 %intra.2 = (f32[512,1024]{1,0:T(8,128)S(1)}, f32[512,1024]{1,0:T(8,128)S(1)}) custom-call(s32[3]{0:T(128)} %pad_add_fusion.meta, s32[8]{0:T(128)} %docs.9, bf16[512,1024]{1,0:T(8,128)(2,1)S(1)} %get-tuple-element.66.x_all, bf16[512,256]{1,0:T(8,128)(2,1)S(1)} %get-tuple-element.67.bc_all.bc, f32[512,32]{1,0:T(8,128)S(1)} %get-tuple-element.68.cum_all, ...), custom_call_target="tpu_custom_call" | custom-call | tf_op jit(solution)/shard_map/intra/pallas_call | solution.py:342
  34.1 5.9 %intra.3 = (f32[512,1024]{1,0:T(8,128)S(1)}, f32[512,1024]{1,0:T(8,128)S(1)}) custom-call(s32[3]{0:T(128)} %pad_add_fusion.meta, s32[8]{0:T(128)} %docs.9, bf16[512,1024]{1,0:T(8,128)(2,1)S(1)} %get-tuple-element.79.x_all, bf16[512,256]{1,0:T(8,128)(2,1)S(1)} %get-tuple-element.80.bc_all.refs_3_, f32[512,32]{1,0:T(8,128)S(1)} %get-tuple-element.68.cum_all, ...), custom_call_target="tpu_custom_call" | custom-call | tf_op jit(solution)/shard_map/intra/pallas_call | solution.py:342
  40.0 2.0 %norm.1.refs_0_ = bf16[512,1024]{1,0:T(8,128)(2,1)S(1)} custom-call(s32[3]{0:T(128)} %pad_add_fusion.meta, f32[512,1024]{1,0:T(8,128)S(1)} %get-tuple-element.75.a, f32[512,1024]{1,0:T(8,128)S(1)} %get-tuple-element.76.f, bf16[512,256]{1,0:T(8,128)(2,1)S(1)} %get-tuple-element.67.bc_all.bc, bf16[128,1024]{1,0:T(8,128)(2,1)S(1)} %collective-permute-done.9.incoming, ...), custom_call_target="tpu_custom_call" | custom-call | tf_op jit(solution)/shard_map/norm/pallas_call | solution.py:342
  42.0 2.1 %collective-permute-done.8.refs_4_ = bf16[128,1024]{1,0:T(8,128)(2,1)S(1)} collective-permute-done((bf16[128,1024]{1,0:T(8,128)(2,1)S(1)}, bf16[128,1024]{1,0:T(8,128)(2,1)S(1)}, u32[]{:S(2)}, u32[]{:S(2)}) %collective-permute-start.8) | collective-permute-done | bytes 262176 | tf_op jit(solution)/shard_map/ppermute | solution.py:23
  44.1 7.2 %project.1 = (bf16[512,2048]{1,0:T(8,128)(2,1)S(1)}, bf16[256,1536]{1,0:T(8,128)(2,1)S(1)}, f32[256,1536]{1,0:T(8,128)S(1)}) custom-call(s32[3]{0:T(128)} %pad_add_fusion.meta, bf16[512,1024]{1,0:T(8,128)(2,1)S(1)} %norm.1.refs_0_, f32[512,1024]{1,0:T(8,128)S(1)} %get-tuple-element.81.refs_1_, f32[512,1024]{1,0:T(8,128)S(1)} %get-tuple-element.82.refs_2_, ...), custom_call_target="tpu_custom_call" | custom-call | tf_op jit(solution)/shard_map/project/pallas_call | solution.py:342
  51.4 2.3 %collective-permute-done.10 = bf16[256,1536]{1,0:T(8,128)(2,1)S(1)} collective-permute-done((bf16[256,1536]{1,0:T(8,128)(2,1)S(1)}, bf16[256,1536]{1,0:T(8,128)(2,1)S(1)}, u32[]{:S(2)}, u32[]{:S(2)}) %collective-permute-start.10) | collective-permute-done | bytes 786464 | tf_op jit(solution)/shard_map/ppermute | solution.py:27
  53.8 1.8 %collective-permute-start.12 = (bf16[256,1536]{1,0:T(8,128)(2,1)S(1)}, bf16[256,1536]{1,0:T(8,128)(2,1)S(1)}, u32[]{:S(2)}, u32[]{:S(2)}) collective-permute-start(bf16[256,1536]{1,0:T(8,128)(2,1)S(1)} %add_convert_fusion), channel_id=1, source_target_pairs={{0,2},{2,0},{1,3},{3,1},{4,6},{6,4},{5,7},{7,5},{8,10},{10,8},{9,1... | collective-permute-start | bytes 2359304 | tf_op jit(solution)/shard_map/ppermute | solution.py:27
  55.6 3.5 %product.2 = (bf16[256,512]{1,0:T(8,128)(2,1)S(1)}, f32[256,512]{1,0:T(8,128)S(1)}) custom-call(s32[3]{0:T(128)} %pad_add_fusion.meta, bf16[512,2048]{1,0:T(8,128)(2,1)S(1)} %get-tuple-element.90.hidden, bf16[2048,4096]{1,0:T(8,128)(2,1)} %w.7), custom_call_target="tpu_custom_call" | custom-call | tf_op jit(solution)/shard_map/product/pallas_call | solution.py:342
  59.2 1.5 %collective-permute-done.11 = bf16[256,512]{1,0:T(8,128)(2,1)S(1)} collective-permute-done((bf16[256,512]{1,0:T(8,128)(2,1)S(1)}, bf16[256,512]{1,0:T(8,128)(2,1)S(1)}, u32[]{:S(2)}, u32[]{:S(2)}) %collective-permute-start.11) | collective-permute-done | bytes 262176 | tf_op jit(solution)/shard_map/ppermute | solution.py:27
  60.7 0.8 add_convert_fusion.2
  61.8 7.9 %product.3 = (bf16[256,2048]{1,0:T(8,128)(2,1)}, f32[256,2048]{1,0:T(8,128)S(1)}) custom-call(s32[3]{0:T(128)} %pad_add_fusion.meta, bf16[512,2048]{1,0:T(8,128)(2,1)S(1)} %get-tuple-element.90.hidden, bf16[2048,4096]{1,0:T(8,128)(2,1)} %w.7), custom_call_target="tpu_custom_call" | custom-call | tf_op jit(solution)/shard_map/product/pallas_call | solution.py:342
  69.7 4.6 %collective-permute-done.12.refs_1_ = bf16[256,1536]{1,0:T(8,128)(2,1)S(1)} collective-permute-done((bf16[256,1536]{1,0:T(8,128)(2,1)S(1)}, bf16[256,1536]{1,0:T(8,128)(2,1)S(1)}, u32[]{:S(2)}, u32[]{:S(2)}) %collective-permute-start.12) | collective-permute-done | bytes 786464 | tf_op jit(solution)/shard_map/ppermute | solution.py:27
  74.3 0.5 early.1.refs_0_
  74.8 2.9 %lead.1 = bf16[256,2048]{1,0:T(8,128)(2,1)} custom-call(f32[256,1536]{1,0:T(8,128)S(1)} %early.1.refs_0_, bf16[256,2048]{1,0:T(8,128)(2,1)} %collective-permute-done.13.refs_1_), custom_call_target="tpu_custom_call" | custom-call | tf_op jit(solution)/shard_map/lead/pallas_call | solution.py:534
  77.7 1.5 %collective-permute-done.14 = bf16[256,512]{1,0:T(8,128)(2,1)} collective-permute-done((bf16[256,512]{1,0:T(8,128)(2,1)}, bf16[256,512]{1,0:T(8,128)(2,1)}, u32[]{:S(2)}, u32[]{:S(2)}) %collective-permute-start.14) | collective-permute-done | bytes 262176 | tf_op jit(solution)/shard_map/ppermute | solution.py:27
  79.2 1.8 %fusion = bf16[256,2048]{1,0:T(8,128)(2,1)} fusion(bf16[256,2048]{1,0:T(8,128)(2,1)} %lead.1, bf16[256,512]{1,0:T(8,128)(2,1)} %collective-permute-done.14, f32[256,2048]{1,0:T(8,128)S(1)} %get-tuple-element.91.refs_0_, bf16[256,2048]{1,0:T(8,128)(2,1)} %collective-permute-done.13.refs_1_), kind=kLoop, calls=%fused_computation.5 | loop fusion | flops 655360 | bytes 1310720 | tf_op jit(solution)/shard_map/dynamic_update_slice | solution.py:550
  (21 shorter events, 1.4 us)
Async XLA Ops:
  0.0 2.2 %collective-permute-start = (f32[64,256]{1,0:T(8,128)}, f32[64,256]{1,0:T(8,128)S(1)}, u32[]{:S(2)}, u32[]{:S(2)}) collective-permute-start(f32[64,256]{1,0:T(8,128)} %bitcast.15), channel_id=1, source_target_pairs={{0,1},{1,0},{2,3},{3,2},{4,5},{5,4},{6,7},{7,6},{8,9},{9,8},{10,11... | collective-permute-start | bytes 196616 | tf_op jit(solution)/shard_map/ppermute | solution.py:27
  2.2 10.1 %collective-permute-start.1 = (bf16[256,4096]{1,0:T(8,128)(2,1)}, bf16[256,4096]{1,0:T(8,128)(2,1)}, u32[]{:S(2)}, u32[]{:S(2)}) collective-permute-start(bf16[256,4096]{1,0:T(8,128)(2,1)} %x.3), channel_id=1, source_target_pairs={{0,1},{1,0},{2,3},{3,2},{4,5},{5,4},{6,7},{7,6},{8,9},{9,8},{10,11... | collective-permute-start | bytes 6291464 | tf_op jit(solution)/shard_map/ppermute | solution.py:27
  2.3 25.5 %collective-permute-start.7 = (bf16[256,4096]{1,0:T(8,128)(2,1)}, bf16[256,4096]{1,0:T(8,128)(2,1)S(1)}, u32[]{:S(2)}, u32[]{:S(2)}) collective-permute-start(bf16[256,4096]{1,0:T(8,128)(2,1)} %gate_own.3), channel_id=1, source_target_pairs={{0,1},{1,0},{2,3},{3,2},{4,5},{5,4},{6,7},{7,6},{8,9},{9,8},{10,11... | collective-permute-start | bytes 6291464 | tf_op jit(solution)/shard_map/ppermute | solution.py:27
  4.2 8.1 %collective-permute-start.4 = (bf16[256,1024]{1,0:T(8,128)(2,1)S(1)}, bf16[256,1024]{1,0:T(8,128)(2,1)S(1)}, u32[]{:S(2)}, u32[]{:S(2)}) collective-permute-start(bf16[256,1024]{1,0:T(8,128)(2,1)S(1)} %reshape.23.s), channel_id=1, source_target_pairs={{0,1},{1,0},{2,3},{3,2},{4,5},{5,4},{6,7},{7,6},{8,9},{9,8},{10,11... | collective-permute-start | bytes 1572872 | tf_op jit(solution)/shard_map/ppermute | solution.py:27
  4.3 7.1 %collective-permute-start.2 = (bf16[16,2560]{1,0:T(8,128)(2,1)S(1)}, bf16[16,2560]{1,0:T(8,128)(2,1)S(1)}, u32[]{:S(2)}, u32[]{:S(2)}) collective-permute-start(bf16[16,2560]{1,0:T(8,128)(2,1)S(1)} %get-tuple-element.51), channel_id=1, source_target_pairs={{0,1},{1,4},{4,5},{5,8},{8,9},{9,12},{12,13},{13,0},{2,3},{3,6},{6... | collective-permute-start | bytes 245768 | tf_op jit(solution)/shard_map/ppermute | solution.py:23
  4.8 7.5 %collective-permute-start.3 = (bf16[16,2560]{1,0:T(8,128)(2,1)S(1)}, bf16[16,2560]{1,0:T(8,128)(2,1)S(1)}, u32[]{:S(2)}, u32[]{:S(2)}) collective-permute-start(bf16[16,2560]{1,0:T(8,128)(2,1)S(1)} %get-tuple-element.52), channel_id=1, source_target_pairs={{0,4},{4,8},{8,12},{12,0},{1,5},{5,9},{9,13},{13,1},{2,6},{6,10},{... | collective-permute-start | bytes 245768 | tf_op jit(solution)/shard_map/ppermute | solution.py:23
  16.7 11.0 %collective-permute-start.6 = (bf16[128,1024]{1,0:T(8,128)(2,1)S(1)}, bf16[128,1024]{1,0:T(8,128)(2,1)S(1)}, u32[]{:S(2)}, u32[]{:S(2)}) collective-permute-start(bf16[128,1024]{1,0:T(8,128)(2,1)S(1)} %get-tuple-element.61), channel_id=1, source_target_pairs={{0,4},{4,8},{8,12},{12,0},{1,5},{5,9},{9,13},{13,1},{2,6},{6,10},{... | collective-permute-start | bytes 786440 | tf_op jit(solution)/shard_map/ppermute | solution.py:23
  21.9 11.8 %collective-permute-start.5 = (bf16[128,1024]{1,0:T(8,128)(2,1)S(1)}, bf16[128,1024]{1,0:T(8,128)(2,1)S(1)}, u32[]{:S(2)}, u32[]{:S(2)}) collective-permute-start(bf16[128,1024]{1,0:T(8,128)(2,1)S(1)} %get-tuple-element.59), channel_id=1, source_target_pairs={{0,4},{4,8},{8,12},{12,0},{1,5},{5,9},{9,13},{13,1},{2,6},{6,10},{... | collective-permute-start | bytes 786440 | tf_op jit(solution)/shard_map/ppermute | solution.py:23
  27.7 12.2 %collective-permute-start.9 = (bf16[128,1024]{1,0:T(8,128)(2,1)S(1)}, bf16[128,1024]{1,0:T(8,128)(2,1)S(1)}, u32[]{:S(2)}, u32[]{:S(2)}) collective-permute-start(bf16[128,1024]{1,0:T(8,128)(2,1)S(1)} %add_convert_fusion.4), channel_id=1, source_target_pairs={{0,4},{4,8},{8,12},{12,0},{1,5},{5,9},{9,13},{13,1},{2,6},{6,10},{... | collective-permute-start | bytes 786440 | tf_op jit(solution)/shard_map/ppermute | solution.py:23
  33.8 10.3 %collective-permute-start.8 = (bf16[128,1024]{1,0:T(8,128)(2,1)S(1)}, bf16[128,1024]{1,0:T(8,128)(2,1)S(1)}, u32[]{:S(2)}, u32[]{:S(2)}) collective-permute-start(bf16[128,1024]{1,0:T(8,128)(2,1)S(1)} %add_convert_fusion.3), channel_id=1, source_target_pairs={{0,4},{4,8},{8,12},{12,0},{1,5},{5,9},{9,13},{13,1},{2,6},{6,10},{... | collective-permute-start | bytes 786440 | tf_op jit(solution)/shard_map/ppermute | solution.py:23
  51.3 2.4 %collective-permute-start.10 = (bf16[256,1536]{1,0:T(8,128)(2,1)S(1)}, bf16[256,1536]{1,0:T(8,128)(2,1)S(1)}, u32[]{:S(2)}, u32[]{:S(2)}) collective-permute-start(bf16[256,1536]{1,0:T(8,128)(2,1)S(1)} %get-tuple-element.86), channel_id=1, source_target_pairs={{0,1},{1,0},{2,3},{3,2},{4,5},{5,4},{6,7},{7,6},{8,9},{9,8},{10,11... | collective-permute-start | bytes 2359304 | tf_op jit(solution)/shard_map/ppermute | solution.py:27
  53.8 20.5 %collective-permute-start.12 = (bf16[256,1536]{1,0:T(8,128)(2,1)S(1)}, bf16[256,1536]{1,0:T(8,128)(2,1)S(1)}, u32[]{:S(2)}, u32[]{:S(2)}) collective-permute-start(bf16[256,1536]{1,0:T(8,128)(2,1)S(1)} %add_convert_fusion), channel_id=1, source_target_pairs={{0,2},{2,0},{1,3},{3,1},{4,6},{6,4},{5,7},{7,5},{8,10},{10,8},{9,1... | collective-permute-start | bytes 2359304 | tf_op jit(solution)/shard_map/ppermute | solution.py:27
  59.1 1.6 %collective-permute-start.11 = (bf16[256,512]{1,0:T(8,128)(2,1)S(1)}, bf16[256,512]{1,0:T(8,128)(2,1)S(1)}, u32[]{:S(2)}, u32[]{:S(2)}) collective-permute-start(bf16[256,512]{1,0:T(8,128)(2,1)S(1)} %get-tuple-element.89), channel_id=1, source_target_pairs={{0,1},{1,0},{2,3},{3,2},{4,5},{5,4},{6,7},{7,6},{8,9},{9,8},{10,11... | collective-permute-start | bytes 786440 | tf_op jit(solution)/shard_map/ppermute | solution.py:27
  61.5 17.7 %collective-permute-start.14 = (bf16[256,512]{1,0:T(8,128)(2,1)}, bf16[256,512]{1,0:T(8,128)(2,1)}, u32[]{:S(2)}, u32[]{:S(2)}) collective-permute-start(bf16[256,512]{1,0:T(8,128)(2,1)} %add_convert_fusion.2), channel_id=1, source_target_pairs={{0,2},{2,0},{1,3},{3,1},{4,6},{6,4},{5,7},{7,5},{8,10},{10,8},{9,1... | collective-permute-start | bytes 786440 | tf_op jit(solution)/shard_map/ppermute | solution.py:27
  69.7 5.0 %collective-permute-start.13 = (bf16[256,2048]{1,0:T(8,128)(2,1)}, bf16[256,2048]{1,0:T(8,128)(2,1)}, u32[]{:S(2)}, u32[]{:S(2)}) collective-permute-start(bf16[256,2048]{1,0:T(8,128)(2,1)} %get-tuple-element.93), channel_id=1, source_target_pairs={{0,1},{1,0},{2,3},{3,2},{4,5},{5,4},{6,7},{7,6},{8,9},{9,8},{10,11... | collective-permute-start | bytes 3145736 | tf_op jit(solution)/shard_map/ppermute | solution.py:27

commit v6 on v5

--- a/solution.py
+++ b/solution.py
@@ -13,7 +13,7 @@
 EPSILON = 1e-05
 LOG2E = 1.4426950408889634
 CEILING = 126.0
-VMEM = 20 << 20
+VMEM = 28 << 20
 F32 = jnp.float32
 BF16 = jnp.bfloat16
 
@@ -546,7 +546,8 @@
     early = finish(0, [keep, far_lead], "early", F32, weight=1 << 38)
     output = finish(0, [early, got], "lead", BF16)
     cut = lead * mm_cols
-    last = (keep[:, cut:] + got[:, cut:].astype(F32) + far_rest.astype(F32)).astype(BF16)
+    (near,) = after(keep[:, cut:] + got[:, cut:].astype(F32))
+    last = (near + far_rest.astype(F32)).astype(BF16)
     return lax.dynamic_update_slice(output, last, (0, cut))
 
 

time: 81.8 us -> 81.8 us (level)
  waiting for transfers between devices: 18.1 us -> 16.8 us
  other arithmetic: 3.58 us -> 4.52 us
    ppermute x9, waiting for transfers between devices: 9.87 us -> 8.83 us  [swapped(): lax.ppermute(shard, axis, [(i, i ^ 1) for i in range(lax.axis_size(axis))])]
    add x0 -> x1, other arithmetic: none -> 1.03 us  [local(): near, = after(keep[:, cut:] + got[:, cut:].astype(F32))]
  transfers between devices with their start and end apart: 15 -> 15, of which waited for: 8 -> 8; matrix products, arithmetic and copies ran while one was open for 6% -> 7% of each run, Pallas kernels for 49% -> 49%
where the time goes in v6:
time: 81.8 us; the launch traced here: 81 us
  Pallas kernels  47.2 us (58%)
  waiting for transfers between devices  16.8 us (21%)
  starting transfers between devices  9.23 us (11%)
  other arithmetic  4.52 us (6%)
  local copies, waits for them, and re-layouts  3.09 us (4%)
    pallas_call x9, Pallas kernels, call(): kernel(*(pltpu.with_memory_space_constraint(v, pltpu.HBM) if any((v is p...  43.8 us
    ppermute x9, waiting for transfers between devices, swapped(): lax.ppermute(shard, axis, [(i, i ^ 1) for i in range(lax.axis_size(axis))])  8.83 us
    ppermute x6, waiting for transfers between devices, shifted_ring(): lax.ppermute(shard, axis, [(i, (i + 1) % peers) for i in range(peers)])  7.94 us
    ppermute x6, starting transfers between devices, shifted_ring(): lax.ppermute(shard, axis, [(i, (i + 1) % peers) for i in range(peers)])  5.82 us
    ppermute x9, starting transfers between devices, swapped(): lax.ppermute(shard, axis, [(i, i ^ 1) for i in range(lax.axis_size(axis))])  3.41 us
    pallas_call x2, Pallas kernels, finish(): pl.pallas_call(sum_kernel, grid=(blocks,), in_specs=[pl.BlockSpec((half,...  3.41 us
    dynamic_update_slice x1, other arithmetic, local(): return lax.dynamic_update_slice(output, last, (0, cut))  1.72 us
  transfers between devices with their start and end apart: 15, of which 8 were waited for; matrix products, arithmetic and copies ran while one was open for 7% of the time, Pallas kernels for 49%

profile of v6, /device:TPU:0, one launch (start us, length us, event | category | flops | bytes accessed | tf_op | source)
XLA Modules:
  0.0 81.0 jit_solution(7089604208797484785)
XLA Ops:
  0.0 0.5 collective-permute-start
  0.5 0.8 slice.25
  1.3 0.9 %fusion.1 = (bf16[16,2048]{1,0:T(8,128)(2,1)S(1)}, bf16[16,2048]{1,0:T(8,128)(2,1)S(1)}) fusion(bf16[256,4096]{1,0:T(8,128)(2,1)} %x.3), kind=kLoop, calls=%fused_computation.10 | loop fusion | bytes 262144 | tf_op jit(solution)/shard_map/slice | solution.py:363
  2.3 0.5 collective-permute-start.7
  2.8 1.4 %reshape.23.s = bf16[256,1024]{1,0:T(8,128)(2,1)S(1)} reshape(bf16[256,4,2,128]{3,2,1,0:T(2,128)(2,1)} %param.15) | data formatting | bytes 1048576 | tf_op jit(solution)/shard_map/reshape | solution.py:346
  4.8 2.7 %collective-permute-start.3 = (bf16[16,2560]{1,0:T(8,128)(2,1)S(1)}, bf16[16,2560]{1,0:T(8,128)(2,1)S(1)}, u32[]{:S(2)}, u32[]{:S(2)}) collective-permute-start(bf16[16,2560]{1,0:T(8,128)(2,1)S(1)} %get-tuple-element.52), channel_id=1, source_target_pairs={{0,4},{4,8},{8,12},{12,0},{1,5},{5,9},{9,13},{13,1},{2,6},{6,10},{... | collective-permute-start | bytes 245768 | tf_op jit(solution)/shard_map/ppermute | solution.py:23
  7.4 0.6 pad_add_fusion.meta
  8.0 2.2 %decay.1 = (f32[512,32]{1,0:T(8,128)S(1)}, f32[32,512]{1,0:T(8,128)S(1)}, bf16[512,64]{1,0:T(8,128)(2,1)S(1)}, bf16[8,96]{1,0:T(8,128)(2,1)S(1)}) custom-call(s32[3]{0:T(128)} %pad_add_fusion.meta, s32[8]{0:T(128)} %docs.9, f32[64,256]{1,0:T(8,128)} %bitcast.16, f32[64,256]{1,0:T(8,128)S(1)} %collective-permute-done.got_raw, f32[1,64]{1,0:T(1,128)} %bitcast.23), custom_call_target="tpu_custom_call" | custom-call | tf_op jit(solution)/shard_map/decay/pallas_call | solution.py:342
  10.3 1.1 %collective-permute-done.2.rim_x.rim_s = bf16[16,2560]{1,0:T(8,128)(2,1)S(1)} collective-permute-done((bf16[16,2560]{1,0:T(8,128)(2,1)S(1)}, bf16[16,2560]{1,0:T(8,128)(2,1)S(1)}, u32[]{:S(2)}, u32[]{:S(2)}) %collective-permute-start.2) | collective-permute-done | bytes 81952 | tf_op jit(solution)/shard_map/ppermute | solution.py:23
  11.4 0.9 %collective-permute-done.3.late_rim_x.late_rim_s = bf16[16,2560]{1,0:T(8,128)(2,1)S(1)} collective-permute-done((bf16[16,2560]{1,0:T(8,128)(2,1)S(1)}, bf16[16,2560]{1,0:T(8,128)(2,1)S(1)}, u32[]{:S(2)}, u32[]{:S(2)}) %collective-permute-start.3) | collective-permute-done | bytes 81952 | tf_op jit(solution)/shard_map/ppermute | solution.py:23
  12.3 4.4 %state.2 = (bf16[512,1024]{1,0:T(8,128)(2,1)S(1)}, bf16[512,256]{1,0:T(8,128)(2,1)S(1)}, bf16[128,1024]{1,0:T(8,128)(2,1)S(1)}, f32[1,1024]{1,0:T(1,128)S(1)}) custom-call(s32[3]{0:T(128)} %pad_add_fusion.meta, s32[8]{0:T(128)} %docs.9, bf16[256,4096]{1,0:T(8,128)(2,1)} %x.3, bf16[256,4096]{1,0:T(8,128)(2,1)} %collective-permute-done.1.got_x, ...), custom_call_target="tpu_custom_call" | custom-call | tf_op jit(solution)/shard_map/state/pallas_call | solution.py:342
  16.7 0.8 %collective-permute-start.6 = (bf16[128,1024]{1,0:T(8,128)(2,1)S(1)}, bf16[128,1024]{1,0:T(8,128)(2,1)S(1)}, u32[]{:S(2)}, u32[]{:S(2)}) collective-permute-start(bf16[128,1024]{1,0:T(8,128)(2,1)S(1)} %get-tuple-element.61), channel_id=1, source_target_pairs={{0,4},{4,8},{8,12},{12,0},{1,5},{5,9},{9,13},{13,1},{2,6},{6,10},{... | collective-permute-start | bytes 786440 | tf_op jit(solution)/shard_map/ppermute | solution.py:23
  17.5 4.4 %state.3 = (bf16[512,1024]{1,0:T(8,128)(2,1)S(1)}, bf16[512,256]{1,0:T(8,128)(2,1)S(1)}, bf16[128,1024]{1,0:T(8,128)(2,1)S(1)}, f32[1,1024]{1,0:T(1,128)S(1)}) custom-call(s32[3]{0:T(128)} %pad_add_fusion.meta, s32[8]{0:T(128)} %docs.9, bf16[256,4096]{1,0:T(8,128)(2,1)} %x.3, bf16[256,4096]{1,0:T(8,128)(2,1)} %collective-permute-done.1.got_x, ...), custom_call_target="tpu_custom_call" | custom-call | tf_op jit(solution)/shard_map/state/pallas_call | solution.py:342
  21.9 1.6 %collective-permute-start.5 = (bf16[128,1024]{1,0:T(8,128)(2,1)S(1)}, bf16[128,1024]{1,0:T(8,128)(2,1)S(1)}, u32[]{:S(2)}, u32[]{:S(2)}) collective-permute-start(bf16[128,1024]{1,0:T(8,128)(2,1)S(1)} %get-tuple-element.59), channel_id=1, source_target_pairs={{0,4},{4,8},{8,12},{12,0},{1,5},{5,9},{9,13},{13,1},{2,6},{6,10},{... | collective-permute-start | bytes 786440 | tf_op jit(solution)/shard_map/ppermute | solution.py:23
  23.5 4.1 %collective-permute-done.6 = bf16[128,1024]{1,0:T(8,128)(2,1)S(1)} collective-permute-done((bf16[128,1024]{1,0:T(8,128)(2,1)S(1)}, bf16[128,1024]{1,0:T(8,128)(2,1)S(1)}, u32[]{:S(2)}, u32[]{:S(2)}) %collective-permute-start.6) | collective-permute-done | bytes 262176 | tf_op jit(solution)/shard_map/ppermute | solution.py:23
  27.8 6.1 %intra.2 = (f32[512,1024]{1,0:T(8,128)S(1)}, f32[512,1024]{1,0:T(8,128)S(1)}) custom-call(s32[3]{0:T(128)} %pad_add_fusion.meta, s32[8]{0:T(128)} %docs.9, bf16[512,1024]{1,0:T(8,128)(2,1)S(1)} %get-tuple-element.66.x_all, bf16[512,256]{1,0:T(8,128)(2,1)S(1)} %get-tuple-element.67.bc_all.bc, f32[512,32]{1,0:T(8,128)S(1)} %get-tuple-element.68.cum_all, ...), custom_call_target="tpu_custom_call" | custom-call | tf_op jit(solution)/shard_map/intra/pallas_call | solution.py:342
  34.3 6.0 %intra.3 = (f32[512,1024]{1,0:T(8,128)S(1)}, f32[512,1024]{1,0:T(8,128)S(1)}) custom-call(s32[3]{0:T(128)} %pad_add_fusion.meta, s32[8]{0:T(128)} %docs.9, bf16[512,1024]{1,0:T(8,128)(2,1)S(1)} %get-tuple-element.79.x_all, bf16[512,256]{1,0:T(8,128)(2,1)S(1)} %get-tuple-element.80.bc_all.refs_3_, f32[512,32]{1,0:T(8,128)S(1)} %get-tuple-element.68.cum_all, ...), custom_call_target="tpu_custom_call" | custom-call | tf_op jit(solution)/shard_map/intra/pallas_call | solution.py:342
  40.3 2.0 %norm.1.refs_0_ = bf16[512,1024]{1,0:T(8,128)(2,1)S(1)} custom-call(s32[3]{0:T(128)} %pad_add_fusion.meta, f32[512,1024]{1,0:T(8,128)S(1)} %get-tuple-element.75.a, f32[512,1024]{1,0:T(8,128)S(1)} %get-tuple-element.76.f, bf16[512,256]{1,0:T(8,128)(2,1)S(1)} %get-tuple-element.67.bc_all.bc, bf16[128,1024]{1,0:T(8,128)(2,1)S(1)} %collective-permute-done.9.incoming, ...), custom_call_target="tpu_custom_call" | custom-call | tf_op jit(solution)/shard_map/norm/pallas_call | solution.py:342
  42.3 1.8 %collective-permute-done.8.refs_4_ = bf16[128,1024]{1,0:T(8,128)(2,1)S(1)} collective-permute-done((bf16[128,1024]{1,0:T(8,128)(2,1)S(1)}, bf16[128,1024]{1,0:T(8,128)(2,1)S(1)}, u32[]{:S(2)}, u32[]{:S(2)}) %collective-permute-start.8) | collective-permute-done | bytes 262176 | tf_op jit(solution)/shard_map/ppermute | solution.py:23
  44.1 7.2 %project.1 = (bf16[512,2048]{1,0:T(8,128)(2,1)S(1)}, bf16[256,1536]{1,0:T(8,128)(2,1)S(1)}, f32[256,1536]{1,0:T(8,128)S(1)}) custom-call(s32[3]{0:T(128)} %pad_add_fusion.meta, bf16[512,1024]{1,0:T(8,128)(2,1)S(1)} %norm.1.refs_0_, f32[512,1024]{1,0:T(8,128)S(1)} %get-tuple-element.81.refs_1_, f32[512,1024]{1,0:T(8,128)S(1)} %get-tuple-element.82.refs_2_, ...), custom_call_target="tpu_custom_call" | custom-call | tf_op jit(solution)/shard_map/project/pallas_call | solution.py:342
  51.4 2.3 %collective-permute-done.10 = bf16[256,1536]{1,0:T(8,128)(2,1)S(1)} collective-permute-done((bf16[256,1536]{1,0:T(8,128)(2,1)S(1)}, bf16[256,1536]{1,0:T(8,128)(2,1)S(1)}, u32[]{:S(2)}, u32[]{:S(2)}) %collective-permute-start.10) | collective-permute-done | bytes 786464 | tf_op jit(solution)/shard_map/ppermute | solution.py:27
  53.9 1.8 %collective-permute-start.12 = (bf16[256,1536]{1,0:T(8,128)(2,1)S(1)}, bf16[256,1536]{1,0:T(8,128)(2,1)S(1)}, u32[]{:S(2)}, u32[]{:S(2)}) collective-permute-start(bf16[256,1536]{1,0:T(8,128)(2,1)S(1)} %add_convert_fusion), channel_id=1, source_target_pairs={{0,2},{2,0},{1,3},{3,1},{4,6},{6,4},{5,7},{7,5},{8,10},{10,8},{9,1... | collective-permute-start | bytes 2359304 | tf_op jit(solution)/shard_map/ppermute | solution.py:27
  55.7 3.5 %product.2 = (bf16[256,512]{1,0:T(8,128)(2,1)S(1)}, f32[256,512]{1,0:T(8,128)S(1)}) custom-call(s32[3]{0:T(128)} %pad_add_fusion.meta, bf16[512,2048]{1,0:T(8,128)(2,1)S(1)} %get-tuple-element.90.hidden, bf16[2048,4096]{1,0:T(8,128)(2,1)} %w.7), custom_call_target="tpu_custom_call" | custom-call | tf_op jit(solution)/shard_map/product/pallas_call | solution.py:342
  59.3 1.5 %collective-permute-done.11 = bf16[256,512]{1,0:T(8,128)(2,1)S(1)} collective-permute-done((bf16[256,512]{1,0:T(8,128)(2,1)S(1)}, bf16[256,512]{1,0:T(8,128)(2,1)S(1)}, u32[]{:S(2)}, u32[]{:S(2)}) %collective-permute-start.11) | collective-permute-done | bytes 262176 | tf_op jit(solution)/shard_map/ppermute | solution.py:27
  60.8 0.8 add_convert_fusion.2
  61.8 7.9 %product.3 = (bf16[256,2048]{1,0:T(8,128)(2,1)}, f32[256,2048]{1,0:T(8,128)S(1)}) custom-call(s32[3]{0:T(128)} %pad_add_fusion.meta, bf16[512,2048]{1,0:T(8,128)(2,1)S(1)} %get-tuple-element.90.hidden, bf16[2048,4096]{1,0:T(8,128)(2,1)} %w.7), custom_call_target="tpu_custom_call" | custom-call | tf_op jit(solution)/shard_map/product/pallas_call | solution.py:342
  69.8 4.6 %collective-permute-done.12.refs_1_ = bf16[256,1536]{1,0:T(8,128)(2,1)S(1)} collective-permute-done((bf16[256,1536]{1,0:T(8,128)(2,1)S(1)}, bf16[256,1536]{1,0:T(8,128)(2,1)S(1)}, u32[]{:S(2)}, u32[]{:S(2)}) %collective-permute-start.12) | collective-permute-done | bytes 786464 | tf_op jit(solution)/shard_map/ppermute | solution.py:27
  74.3 0.5 early.1.refs_0_
  74.8 1.0 %convert_add_fusion = f32[256,512]{1,0:T(8,128)S(1)} fusion(f32[256,2048]{1,0:T(8,128)S(1)} %get-tuple-element.91.refs_0_, bf16[256,2048]{1,0:T(8,128)(2,1)} %collective-permute-done.13.refs_1_), kind=kLoop, calls=%fused_computation.2 | loop fusion | flops 262144 | bytes 1310720 | tf_op jit(solution)/shard_map/add | solution.py:549
  75.9 2.9 %lead.1 = bf16[256,2048]{1,0:T(8,128)(2,1)} custom-call(f32[256,1536]{1,0:T(8,128)S(1)} %early.1.refs_0_, bf16[256,2048]{1,0:T(8,128)(2,1)} %collective-permute-done.13.refs_1_), custom_call_target="tpu_custom_call" | custom-call | tf_op jit(solution)/shard_map/lead/pallas_call | solution.py:534
  78.8 0.5 collective-permute-done.14
  79.3 1.7 %fusion = bf16[256,2048]{1,0:T(8,128)(2,1)} fusion(bf16[256,2048]{1,0:T(8,128)(2,1)} %lead.1, f32[256,512]{1,0:T(8,128)S(1)} %convert_add_fusion, bf16[256,512]{1,0:T(8,128)(2,1)} %collective-permute-done.14), kind=kLoop, calls=%fused_computation.6 | loop fusion | flops 393216 | bytes 1048576 | tf_op jit(solution)/shard_map/dynamic_update_slice | solution.py:551
  (22 shorter events, 1.9 us)
Async XLA Ops:
  0.0 2.2 %collective-permute-start = (f32[64,256]{1,0:T(8,128)}, f32[64,256]{1,0:T(8,128)S(1)}, u32[]{:S(2)}, u32[]{:S(2)}) collective-permute-start(f32[64,256]{1,0:T(8,128)} %bitcast.15), channel_id=1, source_target_pairs={{0,1},{1,0},{2,3},{3,2},{4,5},{5,4},{6,7},{7,6},{8,9},{9,8},{10,11... | collective-permute-start | bytes 196616 | tf_op jit(solution)/shard_map/ppermute | solution.py:27
  2.2 10.1 %collective-permute-start.1 = (bf16[256,4096]{1,0:T(8,128)(2,1)}, bf16[256,4096]{1,0:T(8,128)(2,1)}, u32[]{:S(2)}, u32[]{:S(2)}) collective-permute-start(bf16[256,4096]{1,0:T(8,128)(2,1)} %x.3), channel_id=1, source_target_pairs={{0,1},{1,0},{2,3},{3,2},{4,5},{5,4},{6,7},{7,6},{8,9},{9,8},{10,11... | collective-permute-start | bytes 6291464 | tf_op jit(solution)/shard_map/ppermute | solution.py:27
  2.3 25.5 %collective-permute-start.7 = (bf16[256,4096]{1,0:T(8,128)(2,1)}, bf16[256,4096]{1,0:T(8,128)(2,1)S(1)}, u32[]{:S(2)}, u32[]{:S(2)}) collective-permute-start(bf16[256,4096]{1,0:T(8,128)(2,1)} %gate_own.3), channel_id=1, source_target_pairs={{0,1},{1,0},{2,3},{3,2},{4,5},{5,4},{6,7},{7,6},{8,9},{9,8},{10,11... | collective-permute-start | bytes 6291464 | tf_op jit(solution)/shard_map/ppermute | solution.py:27
  4.2 8.1 %collective-permute-start.4 = (bf16[256,1024]{1,0:T(8,128)(2,1)S(1)}, bf16[256,1024]{1,0:T(8,128)(2,1)S(1)}, u32[]{:S(2)}, u32[]{:S(2)}) collective-permute-start(bf16[256,1024]{1,0:T(8,128)(2,1)S(1)} %reshape.23.s), channel_id=1, source_target_pairs={{0,1},{1,0},{2,3},{3,2},{4,5},{5,4},{6,7},{7,6},{8,9},{9,8},{10,11... | collective-permute-start | bytes 1572872 | tf_op jit(solution)/shard_map/ppermute | solution.py:27
  4.3 7.1 %collective-permute-start.2 = (bf16[16,2560]{1,0:T(8,128)(2,1)S(1)}, bf16[16,2560]{1,0:T(8,128)(2,1)S(1)}, u32[]{:S(2)}, u32[]{:S(2)}) collective-permute-start(bf16[16,2560]{1,0:T(8,128)(2,1)S(1)} %get-tuple-element.51), channel_id=1, source_target_pairs={{0,1},{1,4},{4,5},{5,8},{8,9},{9,12},{12,13},{13,0},{2,3},{3,6},{6... | collective-permute-start | bytes 245768 | tf_op jit(solution)/shard_map/ppermute | solution.py:23
  4.8 7.5 %collective-permute-start.3 = (bf16[16,2560]{1,0:T(8,128)(2,1)S(1)}, bf16[16,2560]{1,0:T(8,128)(2,1)S(1)}, u32[]{:S(2)}, u32[]{:S(2)}) collective-permute-start(bf16[16,2560]{1,0:T(8,128)(2,1)S(1)} %get-tuple-element.52), channel_id=1, source_target_pairs={{0,4},{4,8},{8,12},{12,0},{1,5},{5,9},{9,13},{13,1},{2,6},{6,10},{... | collective-permute-start | bytes 245768 | tf_op jit(solution)/shard_map/ppermute | solution.py:23
  16.7 11.0 %collective-permute-start.6 = (bf16[128,1024]{1,0:T(8,128)(2,1)S(1)}, bf16[128,1024]{1,0:T(8,128)(2,1)S(1)}, u32[]{:S(2)}, u32[]{:S(2)}) collective-permute-start(bf16[128,1024]{1,0:T(8,128)(2,1)S(1)} %get-tuple-element.61), channel_id=1, source_target_pairs={{0,4},{4,8},{8,12},{12,0},{1,5},{5,9},{9,13},{13,1},{2,6},{6,10},{... | collective-permute-start | bytes 786440 | tf_op jit(solution)/shard_map/ppermute | solution.py:23
  21.9 12.0 %collective-permute-start.5 = (bf16[128,1024]{1,0:T(8,128)(2,1)S(1)}, bf16[128,1024]{1,0:T(8,128)(2,1)S(1)}, u32[]{:S(2)}, u32[]{:S(2)}) collective-permute-start(bf16[128,1024]{1,0:T(8,128)(2,1)S(1)} %get-tuple-element.59), channel_id=1, source_target_pairs={{0,4},{4,8},{8,12},{12,0},{1,5},{5,9},{9,13},{13,1},{2,6},{6,10},{... | collective-permute-start | bytes 786440 | tf_op jit(solution)/shard_map/ppermute | solution.py:23
  27.8 12.5 %collective-permute-start.9 = (bf16[128,1024]{1,0:T(8,128)(2,1)S(1)}, bf16[128,1024]{1,0:T(8,128)(2,1)S(1)}, u32[]{:S(2)}, u32[]{:S(2)}) collective-permute-start(bf16[128,1024]{1,0:T(8,128)(2,1)S(1)} %add_convert_fusion.4), channel_id=1, source_target_pairs={{0,4},{4,8},{8,12},{12,0},{1,5},{5,9},{9,13},{13,1},{2,6},{6,10},{... | collective-permute-start | bytes 786440 | tf_op jit(solution)/shard_map/ppermute | solution.py:23
  34.0 10.1 %collective-permute-start.8 = (bf16[128,1024]{1,0:T(8,128)(2,1)S(1)}, bf16[128,1024]{1,0:T(8,128)(2,1)S(1)}, u32[]{:S(2)}, u32[]{:S(2)}) collective-permute-start(bf16[128,1024]{1,0:T(8,128)(2,1)S(1)} %add_convert_fusion.3), channel_id=1, source_target_pairs={{0,4},{4,8},{8,12},{12,0},{1,5},{5,9},{9,13},{13,1},{2,6},{6,10},{... | collective-permute-start | bytes 786440 | tf_op jit(solution)/shard_map/ppermute | solution.py:23
  51.3 2.4 %collective-permute-start.10 = (bf16[256,1536]{1,0:T(8,128)(2,1)S(1)}, bf16[256,1536]{1,0:T(8,128)(2,1)S(1)}, u32[]{:S(2)}, u32[]{:S(2)}) collective-permute-start(bf16[256,1536]{1,0:T(8,128)(2,1)S(1)} %get-tuple-element.86), channel_id=1, source_target_pairs={{0,1},{1,0},{2,3},{3,2},{4,5},{5,4},{6,7},{7,6},{8,9},{9,8},{10,11... | collective-permute-start | bytes 2359304 | tf_op jit(solution)/shard_map/ppermute | solution.py:27
  53.9 20.4 %collective-permute-start.12 = (bf16[256,1536]{1,0:T(8,128)(2,1)S(1)}, bf16[256,1536]{1,0:T(8,128)(2,1)S(1)}, u32[]{:S(2)}, u32[]{:S(2)}) collective-permute-start(bf16[256,1536]{1,0:T(8,128)(2,1)S(1)} %add_convert_fusion), channel_id=1, source_target_pairs={{0,2},{2,0},{1,3},{3,1},{4,6},{6,4},{5,7},{7,5},{8,10},{10,8},{9,1... | collective-permute-start | bytes 2359304 | tf_op jit(solution)/shard_map/ppermute | solution.py:27
  59.2 1.6 %collective-permute-start.11 = (bf16[256,512]{1,0:T(8,128)(2,1)S(1)}, bf16[256,512]{1,0:T(8,128)(2,1)S(1)}, u32[]{:S(2)}, u32[]{:S(2)}) collective-permute-start(bf16[256,512]{1,0:T(8,128)(2,1)S(1)} %get-tuple-element.89), channel_id=1, source_target_pairs={{0,1},{1,0},{2,3},{3,2},{4,5},{5,4},{6,7},{7,6},{8,9},{9,8},{10,11... | collective-permute-start | bytes 786440 | tf_op jit(solution)/shard_map/ppermute | solution.py:27
  61.6 17.7 %collective-permute-start.14 = (bf16[256,512]{1,0:T(8,128)(2,1)}, bf16[256,512]{1,0:T(8,128)(2,1)}, u32[]{:S(2)}, u32[]{:S(2)}) collective-permute-start(bf16[256,512]{1,0:T(8,128)(2,1)} %add_convert_fusion.2), channel_id=1, source_target_pairs={{0,2},{2,0},{1,3},{3,1},{4,6},{6,4},{5,7},{7,5},{8,10},{10,8},{9,1... | collective-permute-start | bytes 786440 | tf_op jit(solution)/shard_map/ppermute | solution.py:27
  69.8 5.0 %collective-permute-start.13 = (bf16[256,2048]{1,0:T(8,128)(2,1)}, bf16[256,2048]{1,0:T(8,128)(2,1)}, u32[]{:S(2)}, u32[]{:S(2)}) collective-permute-start(bf16[256,2048]{1,0:T(8,128)(2,1)} %get-tuple-element.93), channel_id=1, source_target_pairs={{0,1},{1,0},{2,3},{3,2},{4,5},{5,4},{6,7},{7,6},{8,9},{9,8},{10,11... | collective-permute-start | bytes 3145736 | tf_op jit(solution)/shard_map/ppermute | solution.py:27

commit v7 on v5

--- a/solution.py
+++ b/solution.py
@@ -121,8 +121,8 @@
     row = lax.broadcasted_iota(jnp.int32, (count, count), 0)
     col = lax.broadcasted_iota(jnp.int32, (count, count), 1)
     above = jnp.where(row <= col, 1.0, 0.0).astype(BF16)
-    high, mid, low = split3(decay)
-    cum = mm(high, above) + (mm(mid, above) + mm(low, above))
+    sums = mm(jnp.concatenate(split3(decay), axis=0), above)
+    cum = sums[:heads] + (sums[heads : 2 * heads] + sums[2 * heads :])
     dlt_out[...] = cum - jnp.log2(size)
     end = cum[:, count - 1 :]
     places = first + lax.broadcasted_iota(jnp.int32, (1, count), 1)

time: 81.8 us -> 81.8 us (level)
  no operation moved by 1% of the time
where the time goes in v7:
time: 81.8 us; the launch traced here: 81 us
  Pallas kernels  46.7 us (57%)
  waiting for transfers between devices  18.2 us (22%)
  starting transfers between devices  9.23 us (11%)
  other arithmetic  3.58 us (4%)
  local copies, waits for them, and re-layouts  3.09 us (4%)
    pallas_call x9, Pallas kernels, call(): kernel(*(pltpu.with_memory_space_constraint(v, pltpu.HBM) if any((v is p...  43.3 us
    ppermute x9, waiting for transfers between devices, swapped(): lax.ppermute(shard, axis, [(i, i ^ 1) for i in range(lax.axis_size(axis))])  9.87 us
    ppermute x6, waiting for transfers between devices, shifted_ring(): lax.ppermute(shard, axis, [(i, (i + 1) % peers) for i in range(peers)])  8.37 us
    ppermute x6, starting transfers between devices, shifted_ring(): lax.ppermute(shard, axis, [(i, (i + 1) % peers) for i in range(peers)])  5.82 us
    ppermute x9, starting transfers between devices, swapped(): lax.ppermute(shard, axis, [(i, i ^ 1) for i in range(lax.axis_size(axis))])  3.41 us
    pallas_call x2, Pallas kernels, finish(): pl.pallas_call(sum_kernel, grid=(blocks,), in_specs=[pl.BlockSpec((half,...  3.41 us
    dynamic_update_slice x1, other arithmetic, local(): return lax.dynamic_update_slice(output, last, (0, cut))  1.84 us
  transfers between devices with their start and end apart: 15, of which 8 were waited for; matrix products, arithmetic and copies ran while one was open for 6% of the time, Pallas kernels for 49%

profile of v7, /device:TPU:0, one launch (start us, length us, event | category | flops | bytes accessed | tf_op | source)
XLA Modules:
  0.0 81.0 jit_solution(18142113965083591107)
XLA Ops:
  0.0 0.5 collective-permute-start
  0.5 0.8 slice.25
  1.3 0.9 %fusion.1 = (bf16[16,2048]{1,0:T(8,128)(2,1)S(1)}, bf16[16,2048]{1,0:T(8,128)(2,1)S(1)}) fusion(bf16[256,4096]{1,0:T(8,128)(2,1)} %x.3), kind=kLoop, calls=%fused_computation.9 | loop fusion | bytes 262144 | tf_op jit(solution)/shard_map/slice | solution.py:363
  2.3 0.5 collective-permute-start.7
  2.8 1.4 %reshape.23.s = bf16[256,1024]{1,0:T(8,128)(2,1)S(1)} reshape(bf16[256,4,2,128]{3,2,1,0:T(2,128)(2,1)} %param.15) | data formatting | bytes 1048576 | tf_op jit(solution)/shard_map/reshape | solution.py:346
  4.3 0.4 collective-permute-start.2
  4.8 2.7 %collective-permute-start.3 = (bf16[16,2560]{1,0:T(8,128)(2,1)S(1)}, bf16[16,2560]{1,0:T(8,128)(2,1)S(1)}, u32[]{:S(2)}, u32[]{:S(2)}) collective-permute-start(bf16[16,2560]{1,0:T(8,128)(2,1)S(1)} %get-tuple-element.52), channel_id=1, source_target_pairs={{0,4},{4,8},{8,12},{12,0},{1,5},{5,9},{9,13},{13,1},{2,6},{6,10},{... | collective-permute-start | bytes 245768 | tf_op jit(solution)/shard_map/ppermute | solution.py:23
  7.4 0.6 pad_add_fusion.meta
  8.0 2.1 %decay.1 = (f32[512,32]{1,0:T(8,128)S(1)}, f32[32,512]{1,0:T(8,128)S(1)}, bf16[512,64]{1,0:T(8,128)(2,1)S(1)}, bf16[8,96]{1,0:T(8,128)(2,1)S(1)}) custom-call(s32[3]{0:T(128)} %pad_add_fusion.meta, s32[8]{0:T(128)} %docs.9, f32[64,256]{1,0:T(8,128)} %bitcast.16, f32[64,256]{1,0:T(8,128)S(1)} %collective-permute-done.got_raw, f32[1,64]{1,0:T(1,128)} %bitcast.23), custom_call_target="tpu_custom_call" | custom-call | tf_op jit(solution)/shard_map/decay/pallas_call | solution.py:342
  10.2 1.2 %collective-permute-done.2.rim_x.rim_s = bf16[16,2560]{1,0:T(8,128)(2,1)S(1)} collective-permute-done((bf16[16,2560]{1,0:T(8,128)(2,1)S(1)}, bf16[16,2560]{1,0:T(8,128)(2,1)S(1)}, u32[]{:S(2)}, u32[]{:S(2)}) %collective-permute-start.2) | collective-permute-done | bytes 81952 | tf_op jit(solution)/shard_map/ppermute | solution.py:23
  11.4 0.9 %collective-permute-done.3.late_rim_x.late_rim_s = bf16[16,2560]{1,0:T(8,128)(2,1)S(1)} collective-permute-done((bf16[16,2560]{1,0:T(8,128)(2,1)S(1)}, bf16[16,2560]{1,0:T(8,128)(2,1)S(1)}, u32[]{:S(2)}, u32[]{:S(2)}) %collective-permute-start.3) | collective-permute-done | bytes 81952 | tf_op jit(solution)/shard_map/ppermute | solution.py:23
  12.3 4.4 %state.2 = (bf16[512,1024]{1,0:T(8,128)(2,1)S(1)}, bf16[512,256]{1,0:T(8,128)(2,1)S(1)}, bf16[128,1024]{1,0:T(8,128)(2,1)S(1)}, f32[1,1024]{1,0:T(1,128)S(1)}) custom-call(s32[3]{0:T(128)} %pad_add_fusion.meta, s32[8]{0:T(128)} %docs.9, bf16[256,4096]{1,0:T(8,128)(2,1)} %x.3, bf16[256,4096]{1,0:T(8,128)(2,1)} %collective-permute-done.1.got_x, ...), custom_call_target="tpu_custom_call" | custom-call | tf_op jit(solution)/shard_map/state/pallas_call | solution.py:342
  16.7 0.8 %collective-permute-start.6 = (bf16[128,1024]{1,0:T(8,128)(2,1)S(1)}, bf16[128,1024]{1,0:T(8,128)(2,1)S(1)}, u32[]{:S(2)}, u32[]{:S(2)}) collective-permute-start(bf16[128,1024]{1,0:T(8,128)(2,1)S(1)} %get-tuple-element.61), channel_id=1, source_target_pairs={{0,4},{4,8},{8,12},{12,0},{1,5},{5,9},{9,13},{13,1},{2,6},{6,10},{... | collective-permute-start | bytes 786440 | tf_op jit(solution)/shard_map/ppermute | solution.py:23
  17.5 4.4 %state.3 = (bf16[512,1024]{1,0:T(8,128)(2,1)S(1)}, bf16[512,256]{1,0:T(8,128)(2,1)S(1)}, bf16[128,1024]{1,0:T(8,128)(2,1)S(1)}, f32[1,1024]{1,0:T(1,128)S(1)}) custom-call(s32[3]{0:T(128)} %pad_add_fusion.meta, s32[8]{0:T(128)} %docs.9, bf16[256,4096]{1,0:T(8,128)(2,1)} %x.3, bf16[256,4096]{1,0:T(8,128)(2,1)} %collective-permute-done.1.got_x, ...), custom_call_target="tpu_custom_call" | custom-call | tf_op jit(solution)/shard_map/state/pallas_call | solution.py:342
  21.9 1.6 %collective-permute-start.5 = (bf16[128,1024]{1,0:T(8,128)(2,1)S(1)}, bf16[128,1024]{1,0:T(8,128)(2,1)S(1)}, u32[]{:S(2)}, u32[]{:S(2)}) collective-permute-start(bf16[128,1024]{1,0:T(8,128)(2,1)S(1)} %get-tuple-element.59), channel_id=1, source_target_pairs={{0,4},{4,8},{8,12},{12,0},{1,5},{5,9},{9,13},{13,1},{2,6},{6,10},{... | collective-permute-start | bytes 786440 | tf_op jit(solution)/shard_map/ppermute | solution.py:23
  23.5 4.1 %collective-permute-done.6 = bf16[128,1024]{1,0:T(8,128)(2,1)S(1)} collective-permute-done((bf16[128,1024]{1,0:T(8,128)(2,1)S(1)}, bf16[128,1024]{1,0:T(8,128)(2,1)S(1)}, u32[]{:S(2)}, u32[]{:S(2)}) %collective-permute-start.6) | collective-permute-done | bytes 262176 | tf_op jit(solution)/shard_map/ppermute | solution.py:23
  27.8 5.9 %intra.2 = (f32[512,1024]{1,0:T(8,128)S(1)}, f32[512,1024]{1,0:T(8,128)S(1)}) custom-call(s32[3]{0:T(128)} %pad_add_fusion.meta, s32[8]{0:T(128)} %docs.9, bf16[512,1024]{1,0:T(8,128)(2,1)S(1)} %get-tuple-element.66.x_all, bf16[512,256]{1,0:T(8,128)(2,1)S(1)} %get-tuple-element.67.bc_all.bc, f32[512,32]{1,0:T(8,128)S(1)} %get-tuple-element.68.cum_all, ...), custom_call_target="tpu_custom_call" | custom-call | tf_op jit(solution)/shard_map/intra/pallas_call | solution.py:342
  34.1 5.9 %intra.3 = (f32[512,1024]{1,0:T(8,128)S(1)}, f32[512,1024]{1,0:T(8,128)S(1)}) custom-call(s32[3]{0:T(128)} %pad_add_fusion.meta, s32[8]{0:T(128)} %docs.9, bf16[512,1024]{1,0:T(8,128)(2,1)S(1)} %get-tuple-element.79.x_all, bf16[512,256]{1,0:T(8,128)(2,1)S(1)} %get-tuple-element.80.bc_all.refs_3_, f32[512,32]{1,0:T(8,128)S(1)} %get-tuple-element.68.cum_all, ...), custom_call_target="tpu_custom_call" | custom-call | tf_op jit(solution)/shard_map/intra/pallas_call | solution.py:342
  40.0 2.0 %norm.1.refs_0_ = bf16[512,1024]{1,0:T(8,128)(2,1)S(1)} custom-call(s32[3]{0:T(128)} %pad_add_fusion.meta, f32[512,1024]{1,0:T(8,128)S(1)} %get-tuple-element.75.a, f32[512,1024]{1,0:T(8,128)S(1)} %get-tuple-element.76.f, bf16[512,256]{1,0:T(8,128)(2,1)S(1)} %get-tuple-element.67.bc_all.bc, bf16[128,1024]{1,0:T(8,128)(2,1)S(1)} %collective-permute-done.9.incoming, ...), custom_call_target="tpu_custom_call" | custom-call | tf_op jit(solution)/shard_map/norm/pallas_call | solution.py:342
  42.0 2.1 %collective-permute-done.8.refs_4_ = bf16[128,1024]{1,0:T(8,128)(2,1)S(1)} collective-permute-done((bf16[128,1024]{1,0:T(8,128)(2,1)S(1)}, bf16[128,1024]{1,0:T(8,128)(2,1)S(1)}, u32[]{:S(2)}, u32[]{:S(2)}) %collective-permute-start.8) | collective-permute-done | bytes 262176 | tf_op jit(solution)/shard_map/ppermute | solution.py:23
  44.1 7.2 %project.1 = (bf16[512,2048]{1,0:T(8,128)(2,1)S(1)}, bf16[256,1536]{1,0:T(8,128)(2,1)S(1)}, f32[256,1536]{1,0:T(8,128)S(1)}) custom-call(s32[3]{0:T(128)} %pad_add_fusion.meta, bf16[512,1024]{1,0:T(8,128)(2,1)S(1)} %norm.1.refs_0_, f32[512,1024]{1,0:T(8,128)S(1)} %get-tuple-element.81.refs_1_, f32[512,1024]{1,0:T(8,128)S(1)} %get-tuple-element.82.refs_2_, ...), custom_call_target="tpu_custom_call" | custom-call | tf_op jit(solution)/shard_map/project/pallas_call | solution.py:342
  51.4 2.3 %collective-permute-done.10 = bf16[256,1536]{1,0:T(8,128)(2,1)S(1)} collective-permute-done((bf16[256,1536]{1,0:T(8,128)(2,1)S(1)}, bf16[256,1536]{1,0:T(8,128)(2,1)S(1)}, u32[]{:S(2)}, u32[]{:S(2)}) %collective-permute-start.10) | collective-permute-done | bytes 786464 | tf_op jit(solution)/shard_map/ppermute | solution.py:27
  53.8 1.8 %collective-permute-start.12 = (bf16[256,1536]{1,0:T(8,128)(2,1)S(1)}, bf16[256,1536]{1,0:T(8,128)(2,1)S(1)}, u32[]{:S(2)}, u32[]{:S(2)}) collective-permute-start(bf16[256,1536]{1,0:T(8,128)(2,1)S(1)} %add_convert_fusion), channel_id=1, source_target_pairs={{0,2},{2,0},{1,3},{3,1},{4,6},{6,4},{5,7},{7,5},{8,10},{10,8},{9,1... | collective-permute-start | bytes 2359304 | tf_op jit(solution)/shard_map/ppermute | solution.py:27
  55.6 3.5 %product.2 = (bf16[256,512]{1,0:T(8,128)(2,1)S(1)}, f32[256,512]{1,0:T(8,128)S(1)}) custom-call(s32[3]{0:T(128)} %pad_add_fusion.meta, bf16[512,2048]{1,0:T(8,128)(2,1)S(1)} %get-tuple-element.90.hidden, bf16[2048,4096]{1,0:T(8,128)(2,1)} %w.7), custom_call_target="tpu_custom_call" | custom-call | tf_op jit(solution)/shard_map/product/pallas_call | solution.py:342
  59.2 1.5 %collective-permute-done.11 = bf16[256,512]{1,0:T(8,128)(2,1)S(1)} collective-permute-done((bf16[256,512]{1,0:T(8,128)(2,1)S(1)}, bf16[256,512]{1,0:T(8,128)(2,1)S(1)}, u32[]{:S(2)}, u32[]{:S(2)}) %collective-permute-start.11) | collective-permute-done | bytes 262176 | tf_op jit(solution)/shard_map/ppermute | solution.py:27
  60.7 0.8 add_convert_fusion.2
  61.8 7.9 %product.3 = (bf16[256,2048]{1,0:T(8,128)(2,1)}, f32[256,2048]{1,0:T(8,128)S(1)}) custom-call(s32[3]{0:T(128)} %pad_add_fusion.meta, bf16[512,2048]{1,0:T(8,128)(2,1)S(1)} %get-tuple-element.90.hidden, bf16[2048,4096]{1,0:T(8,128)(2,1)} %w.7), custom_call_target="tpu_custom_call" | custom-call | tf_op jit(solution)/shard_map/product/pallas_call | solution.py:342
  69.7 4.6 %collective-permute-done.12.refs_1_ = bf16[256,1536]{1,0:T(8,128)(2,1)S(1)} collective-permute-done((bf16[256,1536]{1,0:T(8,128)(2,1)S(1)}, bf16[256,1536]{1,0:T(8,128)(2,1)S(1)}, u32[]{:S(2)}, u32[]{:S(2)}) %collective-permute-start.12) | collective-permute-done | bytes 786464 | tf_op jit(solution)/shard_map/ppermute | solution.py:27
  74.3 0.5 early.1.refs_0_
  74.8 2.9 %lead.1 = bf16[256,2048]{1,0:T(8,128)(2,1)} custom-call(f32[256,1536]{1,0:T(8,128)S(1)} %early.1.refs_0_, bf16[256,2048]{1,0:T(8,128)(2,1)} %collective-permute-done.13.refs_1_), custom_call_target="tpu_custom_call" | custom-call | tf_op jit(solution)/shard_map/lead/pallas_call | solution.py:534
  77.7 1.5 %collective-permute-done.14 = bf16[256,512]{1,0:T(8,128)(2,1)} collective-permute-done((bf16[256,512]{1,0:T(8,128)(2,1)}, bf16[256,512]{1,0:T(8,128)(2,1)}, u32[]{:S(2)}, u32[]{:S(2)}) %collective-permute-start.14) | collective-permute-done | bytes 262176 | tf_op jit(solution)/shard_map/ppermute | solution.py:27
  79.2 1.8 %fusion = bf16[256,2048]{1,0:T(8,128)(2,1)} fusion(bf16[256,2048]{1,0:T(8,128)(2,1)} %lead.1, bf16[256,512]{1,0:T(8,128)(2,1)} %collective-permute-done.14, f32[256,2048]{1,0:T(8,128)S(1)} %get-tuple-element.91.refs_0_, bf16[256,2048]{1,0:T(8,128)(2,1)} %collective-permute-done.13.refs_1_), kind=kLoop, calls=%fused_computation.5 | loop fusion | flops 655360 | bytes 1310720 | tf_op jit(solution)/shard_map/dynamic_update_slice | solution.py:550
  (21 shorter events, 1.4 us)
Async XLA Ops:
  0.0 2.2 %collective-permute-start = (f32[64,256]{1,0:T(8,128)}, f32[64,256]{1,0:T(8,128)S(1)}, u32[]{:S(2)}, u32[]{:S(2)}) collective-permute-start(f32[64,256]{1,0:T(8,128)} %bitcast.15), channel_id=1, source_target_pairs={{0,1},{1,0},{2,3},{3,2},{4,5},{5,4},{6,7},{7,6},{8,9},{9,8},{10,11... | collective-permute-start | bytes 196616 | tf_op jit(solution)/shard_map/ppermute | solution.py:27
  2.2 10.1 %collective-permute-start.1 = (bf16[256,4096]{1,0:T(8,128)(2,1)}, bf16[256,4096]{1,0:T(8,128)(2,1)}, u32[]{:S(2)}, u32[]{:S(2)}) collective-permute-start(bf16[256,4096]{1,0:T(8,128)(2,1)} %x.3), channel_id=1, source_target_pairs={{0,1},{1,0},{2,3},{3,2},{4,5},{5,4},{6,7},{7,6},{8,9},{9,8},{10,11... | collective-permute-start | bytes 6291464 | tf_op jit(solution)/shard_map/ppermute | solution.py:27
  2.3 25.5 %collective-permute-start.7 = (bf16[256,4096]{1,0:T(8,128)(2,1)}, bf16[256,4096]{1,0:T(8,128)(2,1)S(1)}, u32[]{:S(2)}, u32[]{:S(2)}) collective-permute-start(bf16[256,4096]{1,0:T(8,128)(2,1)} %gate_own.3), channel_id=1, source_target_pairs={{0,1},{1,0},{2,3},{3,2},{4,5},{5,4},{6,7},{7,6},{8,9},{9,8},{10,11... | collective-permute-start | bytes 6291464 | tf_op jit(solution)/shard_map/ppermute | solution.py:27
  4.2 8.1 %collective-permute-start.4 = (bf16[256,1024]{1,0:T(8,128)(2,1)S(1)}, bf16[256,1024]{1,0:T(8,128)(2,1)S(1)}, u32[]{:S(2)}, u32[]{:S(2)}) collective-permute-start(bf16[256,1024]{1,0:T(8,128)(2,1)S(1)} %reshape.23.s), channel_id=1, source_target_pairs={{0,1},{1,0},{2,3},{3,2},{4,5},{5,4},{6,7},{7,6},{8,9},{9,8},{10,11... | collective-permute-start | bytes 1572872 | tf_op jit(solution)/shard_map/ppermute | solution.py:27
  4.3 7.1 %collective-permute-start.2 = (bf16[16,2560]{1,0:T(8,128)(2,1)S(1)}, bf16[16,2560]{1,0:T(8,128)(2,1)S(1)}, u32[]{:S(2)}, u32[]{:S(2)}) collective-permute-start(bf16[16,2560]{1,0:T(8,128)(2,1)S(1)} %get-tuple-element.51), channel_id=1, source_target_pairs={{0,1},{1,4},{4,5},{5,8},{8,9},{9,12},{12,13},{13,0},{2,3},{3,6},{6... | collective-permute-start | bytes 245768 | tf_op jit(solution)/shard_map/ppermute | solution.py:23
  4.8 7.5 %collective-permute-start.3 = (bf16[16,2560]{1,0:T(8,128)(2,1)S(1)}, bf16[16,2560]{1,0:T(8,128)(2,1)S(1)}, u32[]{:S(2)}, u32[]{:S(2)}) collective-permute-start(bf16[16,2560]{1,0:T(8,128)(2,1)S(1)} %get-tuple-element.52), channel_id=1, source_target_pairs={{0,4},{4,8},{8,12},{12,0},{1,5},{5,9},{9,13},{13,1},{2,6},{6,10},{... | collective-permute-start | bytes 245768 | tf_op jit(solution)/shard_map/ppermute | solution.py:23
  16.7 11.0 %collective-permute-start.6 = (bf16[128,1024]{1,0:T(8,128)(2,1)S(1)}, bf16[128,1024]{1,0:T(8,128)(2,1)S(1)}, u32[]{:S(2)}, u32[]{:S(2)}) collective-permute-start(bf16[128,1024]{1,0:T(8,128)(2,1)S(1)} %get-tuple-element.61), channel_id=1, source_target_pairs={{0,4},{4,8},{8,12},{12,0},{1,5},{5,9},{9,13},{13,1},{2,6},{6,10},{... | collective-permute-start | bytes 786440 | tf_op jit(solution)/shard_map/ppermute | solution.py:23
  21.9 11.8 %collective-permute-start.5 = (bf16[128,1024]{1,0:T(8,128)(2,1)S(1)}, bf16[128,1024]{1,0:T(8,128)(2,1)S(1)}, u32[]{:S(2)}, u32[]{:S(2)}) collective-permute-start(bf16[128,1024]{1,0:T(8,128)(2,1)S(1)} %get-tuple-element.59), channel_id=1, source_target_pairs={{0,4},{4,8},{8,12},{12,0},{1,5},{5,9},{9,13},{13,1},{2,6},{6,10},{... | collective-permute-start | bytes 786440 | tf_op jit(solution)/shard_map/ppermute | solution.py:23
  27.7 12.2 %collective-permute-start.9 = (bf16[128,1024]{1,0:T(8,128)(2,1)S(1)}, bf16[128,1024]{1,0:T(8,128)(2,1)S(1)}, u32[]{:S(2)}, u32[]{:S(2)}) collective-permute-start(bf16[128,1024]{1,0:T(8,128)(2,1)S(1)} %add_convert_fusion.4), channel_id=1, source_target_pairs={{0,4},{4,8},{8,12},{12,0},{1,5},{5,9},{9,13},{13,1},{2,6},{6,10},{... | collective-permute-start | bytes 786440 | tf_op jit(solution)/shard_map/ppermute | solution.py:23
  33.8 10.3 %collective-permute-start.8 = (bf16[128,1024]{1,0:T(8,128)(2,1)S(1)}, bf16[128,1024]{1,0:T(8,128)(2,1)S(1)}, u32[]{:S(2)}, u32[]{:S(2)}) collective-permute-start(bf16[128,1024]{1,0:T(8,128)(2,1)S(1)} %add_convert_fusion.3), channel_id=1, source_target_pairs={{0,4},{4,8},{8,12},{12,0},{1,5},{5,9},{9,13},{13,1},{2,6},{6,10},{... | collective-permute-start | bytes 786440 | tf_op jit(solution)/shard_map/ppermute | solution.py:23
  51.3 2.4 %collective-permute-start.10 = (bf16[256,1536]{1,0:T(8,128)(2,1)S(1)}, bf16[256,1536]{1,0:T(8,128)(2,1)S(1)}, u32[]{:S(2)}, u32[]{:S(2)}) collective-permute-start(bf16[256,1536]{1,0:T(8,128)(2,1)S(1)} %get-tuple-element.86), channel_id=1, source_target_pairs={{0,1},{1,0},{2,3},{3,2},{4,5},{5,4},{6,7},{7,6},{8,9},{9,8},{10,11... | collective-permute-start | bytes 2359304 | tf_op jit(solution)/shard_map/ppermute | solution.py:27
  53.8 20.5 %collective-permute-start.12 = (bf16[256,1536]{1,0:T(8,128)(2,1)S(1)}, bf16[256,1536]{1,0:T(8,128)(2,1)S(1)}, u32[]{:S(2)}, u32[]{:S(2)}) collective-permute-start(bf16[256,1536]{1,0:T(8,128)(2,1)S(1)} %add_convert_fusion), channel_id=1, source_target_pairs={{0,2},{2,0},{1,3},{3,1},{4,6},{6,4},{5,7},{7,5},{8,10},{10,8},{9,1... | collective-permute-start | bytes 2359304 | tf_op jit(solution)/shard_map/ppermute | solution.py:27
  59.1 1.6 %collective-permute-start.11 = (bf16[256,512]{1,0:T(8,128)(2,1)S(1)}, bf16[256,512]{1,0:T(8,128)(2,1)S(1)}, u32[]{:S(2)}, u32[]{:S(2)}) collective-permute-start(bf16[256,512]{1,0:T(8,128)(2,1)S(1)} %get-tuple-element.89), channel_id=1, source_target_pairs={{0,1},{1,0},{2,3},{3,2},{4,5},{5,4},{6,7},{7,6},{8,9},{9,8},{10,11... | collective-permute-start | bytes 786440 | tf_op jit(solution)/shard_map/ppermute | solution.py:27
  61.5 17.7 %collective-permute-start.14 = (bf16[256,512]{1,0:T(8,128)(2,1)}, bf16[256,512]{1,0:T(8,128)(2,1)}, u32[]{:S(2)}, u32[]{:S(2)}) collective-permute-start(bf16[256,512]{1,0:T(8,128)(2,1)} %add_convert_fusion.2), channel_id=1, source_target_pairs={{0,2},{2,0},{1,3},{3,1},{4,6},{6,4},{5,7},{7,5},{8,10},{10,8},{9,1... | collective-permute-start | bytes 786440 | tf_op jit(solution)/shard_map/ppermute | solution.py:27
  69.7 5.0 %collective-permute-start.13 = (bf16[256,2048]{1,0:T(8,128)(2,1)}, bf16[256,2048]{1,0:T(8,128)(2,1)}, u32[]{:S(2)}, u32[]{:S(2)}) collective-permute-start(bf16[256,2048]{1,0:T(8,128)(2,1)} %get-tuple-element.93), channel_id=1, source_target_pairs={{0,1},{1,0},{2,3},{3,2},{4,5},{5,4},{6,7},{7,6},{8,9},{9,8},{10,11... | collective-permute-start | bytes 3145736 | tf_op jit(solution)/shard_map/ppermute | solution.py:27

commit v8 on v5

--- a/solution.py
+++ b/solution.py
@@ -71,7 +71,9 @@
 
 def head_lanes(copies, heads, head_width, lanes, first_lane):
     shape = (copies * heads, lanes)
-    head = lax.rem(lax.broadcasted_iota(jnp.int32, shape, 0), heads)
+    head = lax.broadcasted_iota(jnp.int32, shape, 0)
+    for copy in range(1, copies):
+        head = jnp.where(head >= heads, head - heads, head)
     lane = first_lane + lax.broadcasted_iota(jnp.int32, shape, 1)
     low = head * head_width
     return jnp.where((lane >= low) & (lane < low + head_width), 1.0, 0.0).astype(BF16)

time: 81.8 us -> 81.8 us (level)
  no operation moved by 1% of the time
where the time goes in v8:
time: 81.8 us; the launch traced here: 81 us
  Pallas kernels  46.9 us (57%)
  waiting for transfers between devices  18.1 us (22%)
  starting transfers between devices  9.23 us (11%)
  other arithmetic  3.58 us (4%)
  local copies, waits for them, and re-layouts  3.09 us (4%)
    pallas_call x9, Pallas kernels, call(): kernel(*(pltpu.with_memory_space_constraint(v, pltpu.HBM) if any((v is p...  43.4 us
    ppermute x9, waiting for transfers between devices, swapped(): lax.ppermute(shard, axis, [(i, i ^ 1) for i in range(lax.axis_size(axis))])  9.86 us
    ppermute x6, waiting for transfers between devices, shifted_ring(): lax.ppermute(shard, axis, [(i, (i + 1) % peers) for i in range(peers)])  8.24 us
    ppermute x6, starting transfers between devices, shifted_ring(): lax.ppermute(shard, axis, [(i, (i + 1) % peers) for i in range(peers)])  5.82 us
    ppermute x9, starting transfers between devices, swapped(): lax.ppermute(shard, axis, [(i, i ^ 1) for i in range(lax.axis_size(axis))])  3.41 us
    pallas_call x2, Pallas kernels, finish(): pl.pallas_call(sum_kernel, grid=(blocks,), in_specs=[pl.BlockSpec((half,...  3.41 us
    dynamic_update_slice x1, other arithmetic, local(): return lax.dynamic_update_slice(output, last, (0, cut))  1.84 us
  transfers between devices with their start and end apart: 15, of which 8 were waited for; matrix products, arithmetic and copies ran while one was open for 6% of the time, Pallas kernels for 49%

profile of v8, /device:TPU:0, one launch (start us, length us, event | category | flops | bytes accessed | tf_op | source)
XLA Modules:
  0.0 81.0 jit_solution(12225448227087532830)
XLA Ops:
  0.0 0.5 collective-permute-start
  0.5 0.8 slice.25
  1.3 0.9 %fusion.1 = (bf16[16,2048]{1,0:T(8,128)(2,1)S(1)}, bf16[16,2048]{1,0:T(8,128)(2,1)S(1)}) fusion(bf16[256,4096]{1,0:T(8,128)(2,1)} %x.3), kind=kLoop, calls=%fused_computation.9 | loop fusion | bytes 262144 | tf_op jit(solution)/shard_map/slice | solution.py:365
  2.3 0.5 collective-permute-start.7
  2.8 1.4 %reshape.23.s = bf16[256,1024]{1,0:T(8,128)(2,1)S(1)} reshape(bf16[256,4,2,128]{3,2,1,0:T(2,128)(2,1)} %param.15) | data formatting | bytes 1048576 | tf_op jit(solution)/shard_map/reshape | solution.py:348
  4.3 0.4 collective-permute-start.2
  4.8 2.7 %collective-permute-start.3 = (bf16[16,2560]{1,0:T(8,128)(2,1)S(1)}, bf16[16,2560]{1,0:T(8,128)(2,1)S(1)}, u32[]{:S(2)}, u32[]{:S(2)}) collective-permute-start(bf16[16,2560]{1,0:T(8,128)(2,1)S(1)} %get-tuple-element.52), channel_id=1, source_target_pairs={{0,4},{4,8},{8,12},{12,0},{1,5},{5,9},{9,13},{13,1},{2,6},{6,10},{... | collective-permute-start | bytes 245768 | tf_op jit(solution)/shard_map/ppermute | solution.py:23
  7.4 0.6 pad_add_fusion.meta
  8.0 2.2 %decay.1 = (f32[512,32]{1,0:T(8,128)S(1)}, f32[32,512]{1,0:T(8,128)S(1)}, bf16[512,64]{1,0:T(8,128)(2,1)S(1)}, bf16[8,96]{1,0:T(8,128)(2,1)S(1)}) custom-call(s32[3]{0:T(128)} %pad_add_fusion.meta, s32[8]{0:T(128)} %docs.9, f32[64,256]{1,0:T(8,128)} %bitcast.16, f32[64,256]{1,0:T(8,128)S(1)} %collective-permute-done.got_raw, f32[1,64]{1,0:T(1,128)} %bitcast.23), custom_call_target="tpu_custom_call" | custom-call | tf_op jit(solution)/shard_map/decay/pallas_call | solution.py:344
  10.3 1.1 %collective-permute-done.2.rim_x.rim_s = bf16[16,2560]{1,0:T(8,128)(2,1)S(1)} collective-permute-done((bf16[16,2560]{1,0:T(8,128)(2,1)S(1)}, bf16[16,2560]{1,0:T(8,128)(2,1)S(1)}, u32[]{:S(2)}, u32[]{:S(2)}) %collective-permute-start.2) | collective-permute-done | bytes 81952 | tf_op jit(solution)/shard_map/ppermute | solution.py:23
  11.4 0.9 %collective-permute-done.3.late_rim_x.late_rim_s = bf16[16,2560]{1,0:T(8,128)(2,1)S(1)} collective-permute-done((bf16[16,2560]{1,0:T(8,128)(2,1)S(1)}, bf16[16,2560]{1,0:T(8,128)(2,1)S(1)}, u32[]{:S(2)}, u32[]{:S(2)}) %collective-permute-start.3) | collective-permute-done | bytes 81952 | tf_op jit(solution)/shard_map/ppermute | solution.py:23
  12.3 4.4 %state.2 = (bf16[512,1024]{1,0:T(8,128)(2,1)S(1)}, bf16[512,256]{1,0:T(8,128)(2,1)S(1)}, bf16[128,1024]{1,0:T(8,128)(2,1)S(1)}, f32[1,1024]{1,0:T(1,128)S(1)}) custom-call(s32[3]{0:T(128)} %pad_add_fusion.meta, s32[8]{0:T(128)} %docs.9, bf16[256,4096]{1,0:T(8,128)(2,1)} %x.3, bf16[256,4096]{1,0:T(8,128)(2,1)} %collective-permute-done.1.got_x, ...), custom_call_target="tpu_custom_call" | custom-call | tf_op jit(solution)/shard_map/state/pallas_call | solution.py:344
  16.7 0.8 %collective-permute-start.6 = (bf16[128,1024]{1,0:T(8,128)(2,1)S(1)}, bf16[128,1024]{1,0:T(8,128)(2,1)S(1)}, u32[]{:S(2)}, u32[]{:S(2)}) collective-permute-start(bf16[128,1024]{1,0:T(8,128)(2,1)S(1)} %get-tuple-element.61), channel_id=1, source_target_pairs={{0,4},{4,8},{8,12},{12,0},{1,5},{5,9},{9,13},{13,1},{2,6},{6,10},{... | collective-permute-start | bytes 786440 | tf_op jit(solution)/shard_map/ppermute | solution.py:23
  17.5 4.4 %state.3 = (bf16[512,1024]{1,0:T(8,128)(2,1)S(1)}, bf16[512,256]{1,0:T(8,128)(2,1)S(1)}, bf16[128,1024]{1,0:T(8,128)(2,1)S(1)}, f32[1,1024]{1,0:T(1,128)S(1)}) custom-call(s32[3]{0:T(128)} %pad_add_fusion.meta, s32[8]{0:T(128)} %docs.9, bf16[256,4096]{1,0:T(8,128)(2,1)} %x.3, bf16[256,4096]{1,0:T(8,128)(2,1)} %collective-permute-done.1.got_x, ...), custom_call_target="tpu_custom_call" | custom-call | tf_op jit(solution)/shard_map/state/pallas_call | solution.py:344
  21.9 1.6 %collective-permute-start.5 = (bf16[128,1024]{1,0:T(8,128)(2,1)S(1)}, bf16[128,1024]{1,0:T(8,128)(2,1)S(1)}, u32[]{:S(2)}, u32[]{:S(2)}) collective-permute-start(bf16[128,1024]{1,0:T(8,128)(2,1)S(1)} %get-tuple-element.59), channel_id=1, source_target_pairs={{0,4},{4,8},{8,12},{12,0},{1,5},{5,9},{9,13},{13,1},{2,6},{6,10},{... | collective-permute-start | bytes 786440 | tf_op jit(solution)/shard_map/ppermute | solution.py:23
  23.5 4.1 %collective-permute-done.6 = bf16[128,1024]{1,0:T(8,128)(2,1)S(1)} collective-permute-done((bf16[128,1024]{1,0:T(8,128)(2,1)S(1)}, bf16[128,1024]{1,0:T(8,128)(2,1)S(1)}, u32[]{:S(2)}, u32[]{:S(2)}) %collective-permute-start.6) | collective-permute-done | bytes 262176 | tf_op jit(solution)/shard_map/ppermute | solution.py:23
  27.8 5.9 %intra.2 = (f32[512,1024]{1,0:T(8,128)S(1)}, f32[512,1024]{1,0:T(8,128)S(1)}) custom-call(s32[3]{0:T(128)} %pad_add_fusion.meta, s32[8]{0:T(128)} %docs.9, bf16[512,1024]{1,0:T(8,128)(2,1)S(1)} %get-tuple-element.66.x_all, bf16[512,256]{1,0:T(8,128)(2,1)S(1)} %get-tuple-element.67.bc_all.bc, f32[512,32]{1,0:T(8,128)S(1)} %get-tuple-element.68.cum_all, ...), custom_call_target="tpu_custom_call" | custom-call | tf_op jit(solution)/shard_map/intra/pallas_call | solution.py:344
  34.1 5.9 %intra.3 = (f32[512,1024]{1,0:T(8,128)S(1)}, f32[512,1024]{1,0:T(8,128)S(1)}) custom-call(s32[3]{0:T(128)} %pad_add_fusion.meta, s32[8]{0:T(128)} %docs.9, bf16[512,1024]{1,0:T(8,128)(2,1)S(1)} %get-tuple-element.79.x_all, bf16[512,256]{1,0:T(8,128)(2,1)S(1)} %get-tuple-element.80.bc_all.refs_3_, f32[512,32]{1,0:T(8,128)S(1)} %get-tuple-element.68.cum_all, ...), custom_call_target="tpu_custom_call" | custom-call | tf_op jit(solution)/shard_map/intra/pallas_call | solution.py:344
  40.0 2.0 %norm.1.refs_0_ = bf16[512,1024]{1,0:T(8,128)(2,1)S(1)} custom-call(s32[3]{0:T(128)} %pad_add_fusion.meta, f32[512,1024]{1,0:T(8,128)S(1)} %get-tuple-element.75.a, f32[512,1024]{1,0:T(8,128)S(1)} %get-tuple-element.76.f, bf16[512,256]{1,0:T(8,128)(2,1)S(1)} %get-tuple-element.67.bc_all.bc, bf16[128,1024]{1,0:T(8,128)(2,1)S(1)} %collective-permute-done.9.incoming, ...), custom_call_target="tpu_custom_call" | custom-call | tf_op jit(solution)/shard_map/norm/pallas_call | solution.py:344
  42.0 2.1 %collective-permute-done.8.refs_4_ = bf16[128,1024]{1,0:T(8,128)(2,1)S(1)} collective-permute-done((bf16[128,1024]{1,0:T(8,128)(2,1)S(1)}, bf16[128,1024]{1,0:T(8,128)(2,1)S(1)}, u32[]{:S(2)}, u32[]{:S(2)}) %collective-permute-start.8) | collective-permute-done | bytes 262176 | tf_op jit(solution)/shard_map/ppermute | solution.py:23
  44.1 7.2 %project.1 = (bf16[512,2048]{1,0:T(8,128)(2,1)S(1)}, bf16[256,1536]{1,0:T(8,128)(2,1)S(1)}, f32[256,1536]{1,0:T(8,128)S(1)}) custom-call(s32[3]{0:T(128)} %pad_add_fusion.meta, bf16[512,1024]{1,0:T(8,128)(2,1)S(1)} %norm.1.refs_0_, f32[512,1024]{1,0:T(8,128)S(1)} %get-tuple-element.81.refs_1_, f32[512,1024]{1,0:T(8,128)S(1)} %get-tuple-element.82.refs_2_, ...), custom_call_target="tpu_custom_call" | custom-call | tf_op jit(solution)/shard_map/project/pallas_call | solution.py:344
  51.4 2.3 %collective-permute-done.10 = bf16[256,1536]{1,0:T(8,128)(2,1)S(1)} collective-permute-done((bf16[256,1536]{1,0:T(8,128)(2,1)S(1)}, bf16[256,1536]{1,0:T(8,128)(2,1)S(1)}, u32[]{:S(2)}, u32[]{:S(2)}) %collective-permute-start.10) | collective-permute-done | bytes 786464 | tf_op jit(solution)/shard_map/ppermute | solution.py:27
  53.8 1.8 %collective-permute-start.12 = (bf16[256,1536]{1,0:T(8,128)(2,1)S(1)}, bf16[256,1536]{1,0:T(8,128)(2,1)S(1)}, u32[]{:S(2)}, u32[]{:S(2)}) collective-permute-start(bf16[256,1536]{1,0:T(8,128)(2,1)S(1)} %add_convert_fusion), channel_id=1, source_target_pairs={{0,2},{2,0},{1,3},{3,1},{4,6},{6,4},{5,7},{7,5},{8,10},{10,8},{9,1... | collective-permute-start | bytes 2359304 | tf_op jit(solution)/shard_map/ppermute | solution.py:27
  55.6 3.5 %product.2 = (bf16[256,512]{1,0:T(8,128)(2,1)S(1)}, f32[256,512]{1,0:T(8,128)S(1)}) custom-call(s32[3]{0:T(128)} %pad_add_fusion.meta, bf16[512,2048]{1,0:T(8,128)(2,1)S(1)} %get-tuple-element.90.hidden, bf16[2048,4096]{1,0:T(8,128)(2,1)} %w.7), custom_call_target="tpu_custom_call" | custom-call | tf_op jit(solution)/shard_map/product/pallas_call | solution.py:344
  59.2 1.5 %collective-permute-done.11 = bf16[256,512]{1,0:T(8,128)(2,1)S(1)} collective-permute-done((bf16[256,512]{1,0:T(8,128)(2,1)S(1)}, bf16[256,512]{1,0:T(8,128)(2,1)S(1)}, u32[]{:S(2)}, u32[]{:S(2)}) %collective-permute-start.11) | collective-permute-done | bytes 262176 | tf_op jit(solution)/shard_map/ppermute | solution.py:27
  60.7 0.8 add_convert_fusion.2
  61.8 7.9 %product.3 = (bf16[256,2048]{1,0:T(8,128)(2,1)}, f32[256,2048]{1,0:T(8,128)S(1)}) custom-call(s32[3]{0:T(128)} %pad_add_fusion.meta, bf16[512,2048]{1,0:T(8,128)(2,1)S(1)} %get-tuple-element.90.hidden, bf16[2048,4096]{1,0:T(8,128)(2,1)} %w.7), custom_call_target="tpu_custom_call" | custom-call | tf_op jit(solution)/shard_map/product/pallas_call | solution.py:344
  69.7 4.6 %collective-permute-done.12.refs_1_ = bf16[256,1536]{1,0:T(8,128)(2,1)S(1)} collective-permute-done((bf16[256,1536]{1,0:T(8,128)(2,1)S(1)}, bf16[256,1536]{1,0:T(8,128)(2,1)S(1)}, u32[]{:S(2)}, u32[]{:S(2)}) %collective-permute-start.12) | collective-permute-done | bytes 786464 | tf_op jit(solution)/shard_map/ppermute | solution.py:27
  74.3 0.5 early.1.refs_0_
  74.8 2.9 %lead.1 = bf16[256,2048]{1,0:T(8,128)(2,1)} custom-call(f32[256,1536]{1,0:T(8,128)S(1)} %early.1.refs_0_, bf16[256,2048]{1,0:T(8,128)(2,1)} %collective-permute-done.13.refs_1_), custom_call_target="tpu_custom_call" | custom-call | tf_op jit(solution)/shard_map/lead/pallas_call | solution.py:536
  77.7 1.5 %collective-permute-done.14 = bf16[256,512]{1,0:T(8,128)(2,1)} collective-permute-done((bf16[256,512]{1,0:T(8,128)(2,1)}, bf16[256,512]{1,0:T(8,128)(2,1)}, u32[]{:S(2)}, u32[]{:S(2)}) %collective-permute-start.14) | collective-permute-done | bytes 262176 | tf_op jit(solution)/shard_map/ppermute | solution.py:27
  79.2 1.8 %fusion = bf16[256,2048]{1,0:T(8,128)(2,1)} fusion(bf16[256,2048]{1,0:T(8,128)(2,1)} %lead.1, bf16[256,512]{1,0:T(8,128)(2,1)} %collective-permute-done.14, f32[256,2048]{1,0:T(8,128)S(1)} %get-tuple-element.91.refs_0_, bf16[256,2048]{1,0:T(8,128)(2,1)} %collective-permute-done.13.refs_1_), kind=kLoop, calls=%fused_computation.5 | loop fusion | flops 655360 | bytes 1310720 | tf_op jit(solution)/shard_map/dynamic_update_slice | solution.py:552
  (21 shorter events, 1.4 us)
Async XLA Ops:
  0.0 2.2 %collective-permute-start = (f32[64,256]{1,0:T(8,128)}, f32[64,256]{1,0:T(8,128)S(1)}, u32[]{:S(2)}, u32[]{:S(2)}) collective-permute-start(f32[64,256]{1,0:T(8,128)} %bitcast.15), channel_id=1, source_target_pairs={{0,1},{1,0},{2,3},{3,2},{4,5},{5,4},{6,7},{7,6},{8,9},{9,8},{10,11... | collective-permute-start | bytes 196616 | tf_op jit(solution)/shard_map/ppermute | solution.py:27
  2.2 10.1 %collective-permute-start.1 = (bf16[256,4096]{1,0:T(8,128)(2,1)}, bf16[256,4096]{1,0:T(8,128)(2,1)}, u32[]{:S(2)}, u32[]{:S(2)}) collective-permute-start(bf16[256,4096]{1,0:T(8,128)(2,1)} %x.3), channel_id=1, source_target_pairs={{0,1},{1,0},{2,3},{3,2},{4,5},{5,4},{6,7},{7,6},{8,9},{9,8},{10,11... | collective-permute-start | bytes 6291464 | tf_op jit(solution)/shard_map/ppermute | solution.py:27
  2.3 25.5 %collective-permute-start.7 = (bf16[256,4096]{1,0:T(8,128)(2,1)}, bf16[256,4096]{1,0:T(8,128)(2,1)S(1)}, u32[]{:S(2)}, u32[]{:S(2)}) collective-permute-start(bf16[256,4096]{1,0:T(8,128)(2,1)} %gate_own.3), channel_id=1, source_target_pairs={{0,1},{1,0},{2,3},{3,2},{4,5},{5,4},{6,7},{7,6},{8,9},{9,8},{10,11... | collective-permute-start | bytes 6291464 | tf_op jit(solution)/shard_map/ppermute | solution.py:27
  4.2 8.1 %collective-permute-start.4 = (bf16[256,1024]{1,0:T(8,128)(2,1)S(1)}, bf16[256,1024]{1,0:T(8,128)(2,1)S(1)}, u32[]{:S(2)}, u32[]{:S(2)}) collective-permute-start(bf16[256,1024]{1,0:T(8,128)(2,1)S(1)} %reshape.23.s), channel_id=1, source_target_pairs={{0,1},{1,0},{2,3},{3,2},{4,5},{5,4},{6,7},{7,6},{8,9},{9,8},{10,11... | collective-permute-start | bytes 1572872 | tf_op jit(solution)/shard_map/ppermute | solution.py:27
  4.3 7.1 %collective-permute-start.2 = (bf16[16,2560]{1,0:T(8,128)(2,1)S(1)}, bf16[16,2560]{1,0:T(8,128)(2,1)S(1)}, u32[]{:S(2)}, u32[]{:S(2)}) collective-permute-start(bf16[16,2560]{1,0:T(8,128)(2,1)S(1)} %get-tuple-element.51), channel_id=1, source_target_pairs={{0,1},{1,4},{4,5},{5,8},{8,9},{9,12},{12,13},{13,0},{2,3},{3,6},{6... | collective-permute-start | bytes 245768 | tf_op jit(solution)/shard_map/ppermute | solution.py:23
  4.8 7.5 %collective-permute-start.3 = (bf16[16,2560]{1,0:T(8,128)(2,1)S(1)}, bf16[16,2560]{1,0:T(8,128)(2,1)S(1)}, u32[]{:S(2)}, u32[]{:S(2)}) collective-permute-start(bf16[16,2560]{1,0:T(8,128)(2,1)S(1)} %get-tuple-element.52), channel_id=1, source_target_pairs={{0,4},{4,8},{8,12},{12,0},{1,5},{5,9},{9,13},{13,1},{2,6},{6,10},{... | collective-permute-start | bytes 245768 | tf_op jit(solution)/shard_map/ppermute | solution.py:23
  16.7 11.0 %collective-permute-start.6 = (bf16[128,1024]{1,0:T(8,128)(2,1)S(1)}, bf16[128,1024]{1,0:T(8,128)(2,1)S(1)}, u32[]{:S(2)}, u32[]{:S(2)}) collective-permute-start(bf16[128,1024]{1,0:T(8,128)(2,1)S(1)} %get-tuple-element.61), channel_id=1, source_target_pairs={{0,4},{4,8},{8,12},{12,0},{1,5},{5,9},{9,13},{13,1},{2,6},{6,10},{... | collective-permute-start | bytes 786440 | tf_op jit(solution)/shard_map/ppermute | solution.py:23
  21.9 11.8 %collective-permute-start.5 = (bf16[128,1024]{1,0:T(8,128)(2,1)S(1)}, bf16[128,1024]{1,0:T(8,128)(2,1)S(1)}, u32[]{:S(2)}, u32[]{:S(2)}) collective-permute-start(bf16[128,1024]{1,0:T(8,128)(2,1)S(1)} %get-tuple-element.59), channel_id=1, source_target_pairs={{0,4},{4,8},{8,12},{12,0},{1,5},{5,9},{9,13},{13,1},{2,6},{6,10},{... | collective-permute-start | bytes 786440 | tf_op jit(solution)/shard_map/ppermute | solution.py:23
  27.7 12.2 %collective-permute-start.9 = (bf16[128,1024]{1,0:T(8,128)(2,1)S(1)}, bf16[128,1024]{1,0:T(8,128)(2,1)S(1)}, u32[]{:S(2)}, u32[]{:S(2)}) collective-permute-start(bf16[128,1024]{1,0:T(8,128)(2,1)S(1)} %add_convert_fusion.4), channel_id=1, source_target_pairs={{0,4},{4,8},{8,12},{12,0},{1,5},{5,9},{9,13},{13,1},{2,6},{6,10},{... | collective-permute-start | bytes 786440 | tf_op jit(solution)/shard_map/ppermute | solution.py:23
  33.8 10.3 %collective-permute-start.8 = (bf16[128,1024]{1,0:T(8,128)(2,1)S(1)}, bf16[128,1024]{1,0:T(8,128)(2,1)S(1)}, u32[]{:S(2)}, u32[]{:S(2)}) collective-permute-start(bf16[128,1024]{1,0:T(8,128)(2,1)S(1)} %add_convert_fusion.3), channel_id=1, source_target_pairs={{0,4},{4,8},{8,12},{12,0},{1,5},{5,9},{9,13},{13,1},{2,6},{6,10},{... | collective-permute-start | bytes 786440 | tf_op jit(solution)/shard_map/ppermute | solution.py:23
  51.3 2.4 %collective-permute-start.10 = (bf16[256,1536]{1,0:T(8,128)(2,1)S(1)}, bf16[256,1536]{1,0:T(8,128)(2,1)S(1)}, u32[]{:S(2)}, u32[]{:S(2)}) collective-permute-start(bf16[256,1536]{1,0:T(8,128)(2,1)S(1)} %get-tuple-element.86), channel_id=1, source_target_pairs={{0,1},{1,0},{2,3},{3,2},{4,5},{5,4},{6,7},{7,6},{8,9},{9,8},{10,11... | collective-permute-start | bytes 2359304 | tf_op jit(solution)/shard_map/ppermute | solution.py:27
  53.8 20.5 %collective-permute-start.12 = (bf16[256,1536]{1,0:T(8,128)(2,1)S(1)}, bf16[256,1536]{1,0:T(8,128)(2,1)S(1)}, u32[]{:S(2)}, u32[]{:S(2)}) collective-permute-start(bf16[256,1536]{1,0:T(8,128)(2,1)S(1)} %add_convert_fusion), channel_id=1, source_target_pairs={{0,2},{2,0},{1,3},{3,1},{4,6},{6,4},{5,7},{7,5},{8,10},{10,8},{9,1... | collective-permute-start | bytes 2359304 | tf_op jit(solution)/shard_map/ppermute | solution.py:27
  59.1 1.6 %collective-permute-start.11 = (bf16[256,512]{1,0:T(8,128)(2,1)S(1)}, bf16[256,512]{1,0:T(8,128)(2,1)S(1)}, u32[]{:S(2)}, u32[]{:S(2)}) collective-permute-start(bf16[256,512]{1,0:T(8,128)(2,1)S(1)} %get-tuple-element.89), channel_id=1, source_target_pairs={{0,1},{1,0},{2,3},{3,2},{4,5},{5,4},{6,7},{7,6},{8,9},{9,8},{10,11... | collective-permute-start | bytes 786440 | tf_op jit(solution)/shard_map/ppermute | solution.py:27
  61.5 17.7 %collective-permute-start.14 = (bf16[256,512]{1,0:T(8,128)(2,1)}, bf16[256,512]{1,0:T(8,128)(2,1)}, u32[]{:S(2)}, u32[]{:S(2)}) collective-permute-start(bf16[256,512]{1,0:T(8,128)(2,1)} %add_convert_fusion.2), channel_id=1, source_target_pairs={{0,2},{2,0},{1,3},{3,1},{4,6},{6,4},{5,7},{7,5},{8,10},{10,8},{9,1... | collective-permute-start | bytes 786440 | tf_op jit(solution)/shard_map/ppermute | solution.py:27
  69.7 5.0 %collective-permute-start.13 = (bf16[256,2048]{1,0:T(8,128)(2,1)}, bf16[256,2048]{1,0:T(8,128)(2,1)}, u32[]{:S(2)}, u32[]{:S(2)}) collective-permute-start(bf16[256,2048]{1,0:T(8,128)(2,1)} %get-tuple-element.93), channel_id=1, source_target_pairs={{0,1},{1,0},{2,3},{3,2},{4,5},{5,4},{6,7},{7,6},{8,9},{9,8},{10,11... | collective-permute-start | bytes 3145736 | tf_op jit(solution)/shard_map/ppermute | solution.py:27
